TPU v7x, 32 devices: a whole 2x2x4 slice. The times are simulated.
32 devices in a mesh: wide: 8 (over z, y), narrow: 4 (over x, core).
Axes of the slice: x: 2, y: 2, z: 4, core: 2. Of those that a mesh axis runs over, the one named last changes fastest.
Arguments:
- passages: bfloat16 [24, 512, 768], P('wide', 'narrow'), may hold values from -6 to 6
- queries: bfloat16 [8, 512, 768], P('wide', 'narrow'), may hold values from -6 to 6
- passage_cot: bfloat16 [24, 512, 768], P('wide', 'narrow'), may hold values from -3 to 3
- query_cot: bfloat16 [8, 512, 768], P('wide', 'narrow'), may hold values from -3 to 3
- passage_lengths: int32 [24, 5], P('wide'), may hold values from 1 to 400, as said below
- query_lengths: int32 [8, 17], P('wide'), may hold values from 1 to 40, 512 in all within a row
- labels: int32 [128], P('wide'), may hold values from 0 to 95
- w_qkv: bfloat16 [2, 768, 2304], P(None, ('wide', 'narrow')), may hold values from -0.3125 to 0.3125
- w_out: bfloat16 [2, 768, 768], P(None, ('wide', 'narrow')), may hold values from -0.875 to 0.875
- w_in: bfloat16 [2, 768, 3072], P(None, ('wide', 'narrow')), may hold values from -0.21875 to 0.21875
- w_back: bfloat16 [2, 3072, 768], P(None, ('wide', 'narrow')), may hold values from -0.15625 to 0.15625
- biases: bfloat16 [2, 6, 768], P(None, None, ('wide', 'narrow')), may hold values from -1 to 1
- norm_gains: bfloat16 [2, 2, 768], P(None, None, ('wide', 'narrow')), may hold values from 0.5 to 1.5
- in_bias: bfloat16 [2, 3072], P(None, ('wide', 'narrow')), may hold values from -1 to 1
Outputs:
- passage_out: bfloat16 [24, 512, 768], P('wide', 'narrow')
- query_out: bfloat16 [8, 512, 768], P('wide', 'narrow')
- passage_grad: bfloat16 [24, 512, 768], P('wide', 'narrow')
- query_grad: bfloat16 [8, 512, 768], P('wide', 'narrow')
- grad_w_qkv: float32 [2, 768, 2304], P(None, 'wide', 'narrow')
- grad_w_out: float32 [2, 768, 768], P(None, 'wide', 'narrow')
- grad_w_in: float32 [2, 768, 3072], P(None, 'wide', 'narrow')
- grad_w_back: float32 [2, 3072, 768], P(None, 'wide', 'narrow')
- grad_biases: float32 [2, 6, 768], P(None, None, ('wide', 'narrow'))
- grad_gains: float32 [2, 2, 768], P(None, None, ('wide', 'narrow'))
- grad_in_bias: float32 [2, 3072], P(None, ('wide', 'narrow'))
- rms_stats: float32 [2, 4], replicated
Inputs may be any that keep to these rules, and one draw needn't show every extreme that they name: `passage_lengths`: entries s < 4 of a row are its passages' lengths, the last entry its padding's; each row sums to 512. Among the 3 rows of each index of wide, one row, drawn from the seed, begins with a passage of exactly 400 tokens. `query_lengths`: entries s < 16 of a row are its queries' lengths, the last entry its padding's; each row sums to 512, and some row of every draw has an entry of exactly 40. `labels`: query r * 16 + s is segment s of query row r; passage r * 4 + s is segment s of passage row r.
All inputs are finite; a program needn't handle non-finite values.
Results may differ from a plain program's by a relative error of at most 0.015.
Values may be sent and summed in bfloat16 or wider, within the bound.
No kernel may reach another device: no remote copies, remote signals or barrier semaphores. Data moves between devices by JAX's collectives and lax.ppermute only.
A program may use at most 256 MiB of HBM per device.

v0:
```python
import jax
import jax.numpy as jnp
from jax import lax
from jax.sharding import PartitionSpec as P

HEAD_DIM = 64


EPSILON = 1e-05
SCORE_DIV = 12.0
MASKED = -1e30


def in_blocks(x, dim, size):
    before, after = (x.shape[:dim], x.shape[dim + 1 :])
    return jnp.moveaxis(x.reshape(*before, size, -1, *after), dim, 0)


def summed_on_arrival(x, axis, dim):
    size = lax.axis_size(axis)
    pieces = lax.all_to_all(in_blocks(x, dim, size), axis, 0, 0, tiled=True)
    return jnp.sum(pieces.astype(jnp.float32), axis=0)


def layer_norm(inputs, gain_row, shift_row):
    row_mean = jnp.mean(inputs, axis=-1, keepdims=True)
    centered = inputs - row_mean
    row_var = jnp.mean(centered * centered, axis=-1, keepdims=True)
    return centered * lax.rsqrt(row_var + EPSILON) * gain_row + shift_row


def segment_table(lengths, positions):
    row_ends = jnp.cumsum(lengths, axis=1, dtype=jnp.int32)
    starts = row_ends - lengths
    boundary = row_ends[:, :-1]
    segment = jnp.sum(
        (positions[None, :, None] >= boundary[:, None, :]).astype(jnp.int32),
        axis=2,
        dtype=jnp.int32,
    )
    return (segment, starts[:, :-1])


def matmul(left, right):
    return jnp.dot(left, right, preferred_element_type=jnp.float32)


def inner_rows(left, right):
    return lax.dot_general(
        left, right, (((0,), (0,)), ((), ())), preferred_element_type=jnp.float32
    )


def inner_cols(left, right):
    return lax.dot_general(
        left, right, (((1,), (1,)), ((), ())), preferred_element_type=jnp.float32
    )


def gelu_exact(inputs):
    return jax.nn.gelu(inputs, approximate=False)


def split_heads(matrix):
    return matrix.reshape(matrix.shape[0], matrix.shape[1] // HEAD_DIM, HEAD_DIM)


def masked_scores(query_heads, key_heads, seg_query, seg_keys):
    scores = jnp.einsum(
        "qhd,khd->hqk", query_heads, key_heads, preferred_element_type=jnp.float32
    ) * HEAD_DIM ** (-0.5)
    same_seg = seg_query[:, None] == seg_keys[None, :]
    return jnp.where(same_seg[None], scores, MASKED)


def attend_row(row_item):
    query_row, key_row, value_row, seg_query, seg_keys = row_item
    value_heads = split_heads(value_row)
    scores = masked_scores(split_heads(query_row), split_heads(key_row), seg_query, seg_keys)
    row_max = jnp.max(scores, axis=-1, keepdims=True)
    shifted = jnp.exp(scores - row_max)
    row_total = jnp.sum(shifted, axis=-1, keepdims=True)
    row_probs = (shifted / row_total).astype(jnp.bfloat16)
    context = jnp.einsum("hqk,khd->qhd", row_probs, value_heads, preferred_element_type=jnp.float32)
    log_sum = (row_max + jnp.log(row_total))[:, :, 0]
    return (context.reshape(query_row.shape).astype(jnp.bfloat16), log_sum)


def query_back(row_item):
    query_row, key_row, value_row, seg_query, seg_keys, log_sum, grad_row = row_item
    scores = masked_scores(split_heads(query_row), split_heads(key_row), seg_query, seg_keys)
    row_probs = jnp.exp(scores - log_sum[:, :, None])
    grad_probs = jnp.einsum(
        "qhd,khd->hqk",
        split_heads(grad_row),
        split_heads(value_row),
        preferred_element_type=jnp.float32,
    )
    row_delta = jnp.sum(row_probs * grad_probs, axis=-1, keepdims=True)
    grad_scores = (row_probs * (grad_probs - row_delta)).astype(jnp.bfloat16)
    grad_query = jnp.einsum(
        "hqk,khd->qhd", grad_scores, split_heads(key_row), preferred_element_type=jnp.float32
    ) * HEAD_DIM ** (-0.5)
    return (grad_query.reshape(query_row.shape).astype(jnp.bfloat16), row_delta[:, :, 0])


def key_back(row_item):
    query_full, key_row, value_row, seg_queries, seg_keys, log_full, delta_full, grad_full = (
        row_item
    )
    query_heads = split_heads(query_full)
    grad_heads = split_heads(grad_full)
    scores = masked_scores(query_heads, split_heads(key_row), seg_queries, seg_keys)
    row_probs = jnp.exp(scores - log_full[:, :, None])
    grad_probs = jnp.einsum(
        "qhd,khd->hqk", grad_heads, split_heads(value_row), preferred_element_type=jnp.float32
    )
    grad_scores = (row_probs * (grad_probs - delta_full[:, :, None])).astype(jnp.bfloat16)
    grad_keys = jnp.einsum(
        "hqk,qhd->khd", grad_scores, query_heads, preferred_element_type=jnp.float32
    ) * HEAD_DIM ** (-0.5)
    grad_values = jnp.einsum(
        "hqk,qhd->khd",
        row_probs.astype(jnp.bfloat16),
        grad_heads,
        preferred_element_type=jnp.float32,
    )
    return (
        grad_keys.reshape(key_row.shape).astype(jnp.bfloat16),
        grad_values.reshape(value_row.shape).astype(jnp.bfloat16),
    )


def body(
    passages,
    queries,
    passage_cot,
    query_cot,
    passage_lengths,
    query_lengths,
    labels,
    w_qkv,
    w_out,
    w_in,
    w_back,
    biases,
    norm_gains,
    in_bias,
):
    model_width = passages.shape[2]
    shard_len = passages.shape[1]
    length = shard_len * lax.axis_size("narrow")
    row_counts = (passages.shape[0], queries.shape[0])
    seg_counts = (passage_lengths.shape[1] - 1, query_lengths.shape[1] - 1)
    local_pos = lax.axis_index("narrow") * shard_len + jnp.arange(shard_len, dtype=jnp.int32)
    every_pos = jnp.arange(length, dtype=jnp.int32)
    pass_local, pass_starts = segment_table(passage_lengths, local_pos)
    query_local, query_starts = segment_table(query_lengths, local_pos)
    seg_local = jnp.concatenate([pass_local, query_local], axis=0)
    seg_every = jnp.concatenate(
        [segment_table(passage_lengths, every_pos)[0], segment_table(query_lengths, every_pos)[0]],
        axis=0,
    )
    valid_cols = (
        (pass_local < seg_counts[0]).astype(jnp.float32).reshape(-1, 1),
        (query_local < seg_counts[1]).astype(jnp.float32).reshape(-1, 1),
    )
    start_sets = (pass_starts, query_starts)
    inputs = (passages.reshape(-1, model_width), queries.reshape(-1, model_width))
    cot_rows = (passage_cot.reshape(-1, model_width), query_cot.reshape(-1, model_width))
    first_hots = [
        local_pos[None, None, :] == start_sets[tower_num][:, :, None] for tower_num in range(2)
    ]
    row_shape = (row_counts[0] + row_counts[1], shard_len, model_width)
    pass_tokens = row_counts[0] * shard_len
    gathered = (
        lax.all_gather(w_qkv, ("wide", "narrow"), axis=1, tiled=True),
        lax.all_gather(w_out, ("wide", "narrow"), axis=1, tiled=True),
        lax.all_gather(w_in, ("wide", "narrow"), axis=1, tiled=True),
        lax.all_gather(w_back, ("wide", "narrow"), axis=1, tiled=True),
        lax.all_gather(biases, ("wide", "narrow"), axis=2, tiled=True),
        lax.all_gather(norm_gains, ("wide", "narrow"), axis=2, tiled=True),
        lax.all_gather(in_bias, ("wide", "narrow"), axis=1, tiled=True),
    )
    query_parts = []
    key_parts = []
    value_parts = []
    for tower_num in range(2):
        projected = matmul(inputs[tower_num], gathered[0][tower_num])
        tower_bias = gathered[4][tower_num]
        query_parts.append((projected[:, :model_width] + tower_bias[0]).astype(jnp.bfloat16))
        key_parts.append(projected[:, model_width : 2 * model_width].astype(jnp.bfloat16))
        value_parts.append((projected[:, 2 * model_width :] + tower_bias[1]).astype(jnp.bfloat16))
    query_all = jnp.concatenate(query_parts, axis=0).reshape(row_shape)
    keys_local = jnp.concatenate(key_parts, axis=0).reshape(row_shape)
    values_local = jnp.concatenate(value_parts, axis=0).reshape(row_shape)
    keys_full, values_full = (
        lax.all_gather(keys_local, "narrow", axis=1, tiled=True),
        lax.all_gather(values_local, "narrow", axis=1, tiled=True),
    )
    context, log_sum = lax.map(
        attend_row, (query_all, keys_full, values_full, seg_local, seg_every)
    )
    context = context.reshape(-1, model_width)
    contexts = (context[:pass_tokens], context[pass_tokens:])
    kept = []
    stat_rows = []
    count_rows = []
    out_rows = []
    for tower_num in range(2):
        tower_bias = gathered[4][tower_num]
        tower_gain = gathered[5][tower_num]
        branch = matmul(contexts[tower_num], gathered[1][tower_num]) + tower_bias[2]
        residual = inputs[tower_num].astype(jnp.float32) + branch
        normed = layer_norm(residual, tower_gain[0], tower_bias[3])
        normed_low = normed.astype(jnp.bfloat16)
        hidden_pre = matmul(normed_low, gathered[2][tower_num]) + gathered[6][tower_num]
        active = gelu_exact(hidden_pre).astype(jnp.bfloat16)
        ffn_out = matmul(active, gathered[3][tower_num]) + tower_bias[4]
        residual_two = normed + ffn_out
        output_low = layer_norm(residual_two, tower_gain[1], tower_bias[5]).astype(jnp.bfloat16)
        valid_col = valid_cols[tower_num]
        stat_rows.append(
            jnp.stack(
                [
                    jnp.sum(valid_col * residual * residual),
                    jnp.sum(valid_col * branch * branch),
                    jnp.sum(valid_col * residual_two * residual_two),
                    jnp.sum(valid_col * ffn_out * ffn_out),
                ]
            )
        )
        count_rows.append(jnp.sum(valid_col))
        out_rows.append(output_low)
        kept.append((residual, normed_low, hidden_pre, active, residual_two))
    stat_stack = jnp.stack(stat_rows)
    count_stack = jnp.stack(count_rows)
    stat_sums, stat_counts = lax.psum((stat_stack, count_stack), ("wide", "narrow"))
    rms_stats = jnp.sqrt(stat_sums / (stat_counts[:, None] * model_width))
    pooled_parts = []
    for tower_num in range(2):
        pooled_parts.append(
            jnp.einsum(
                "rst,rtd->rsd",
                first_hots[tower_num].astype(jnp.bfloat16),
                out_rows[tower_num].reshape(row_counts[tower_num], shard_len, model_width),
                preferred_element_type=jnp.float32,
            ).reshape(-1, model_width)
        )
    pooled_pass, pooled_query = (
        lax.psum(pooled_parts[0].astype(jnp.bfloat16), "narrow").astype(jnp.float32),
        lax.psum(pooled_parts[1].astype(jnp.bfloat16), "narrow").astype(jnp.float32),
    )
    pooled_pass = pooled_pass.astype(jnp.bfloat16)
    pooled_query = pooled_query.astype(jnp.bfloat16)
    passages_every = lax.all_gather(pooled_pass, "wide", axis=0, tiled=True)
    match = inner_cols(pooled_query, passages_every) / SCORE_DIV
    match_max = jnp.max(match, axis=1, keepdims=True)
    match_exp = jnp.exp(match - match_max)
    match_probs = match_exp / jnp.sum(match_exp, axis=1, keepdims=True)
    label_hot = (labels[:, None] == jnp.arange(match.shape[1], dtype=jnp.int32)[None, :]).astype(
        jnp.float32
    )
    grad_match = ((match_probs - label_hot) / SCORE_DIV).astype(jnp.bfloat16)
    grad_pool_query = matmul(grad_match, passages_every)
    pass_term = inner_rows(grad_match, pooled_query)
    grad_pool_pass = summed_on_arrival(pass_term.astype(jnp.bfloat16), "wide", 0)
    grad_pools = (grad_pool_pass, grad_pool_query)
    back_weights = (
        lax.all_gather(w_qkv, ("wide", "narrow"), axis=1, tiled=True),
        lax.all_gather(w_out, ("wide", "narrow"), axis=1, tiled=True),
        lax.all_gather(w_in, ("wide", "narrow"), axis=1, tiled=True),
        lax.all_gather(w_back, ("wide", "narrow"), axis=1, tiled=True),
        lax.all_gather(biases, ("wide", "narrow"), axis=2, tiled=True),
        lax.all_gather(norm_gains, ("wide", "narrow"), axis=2, tiled=True),
        lax.all_gather(in_bias, ("wide", "narrow"), axis=1, tiled=True),
    )
    grad_ffn_list = []
    grad_hidden_list = []
    grad_branch_list = []
    grad_inb_list = []
    small_grads = []
    grad_residuals = []
    grad_contexts = []
    for tower_num in range(2):
        residual, normed_low, hidden_pre, active, residual_two = kept[tower_num]
        tower_bias = back_weights[4][tower_num]
        tower_gain = back_weights[5][tower_num]
        row_total = row_counts[tower_num]
        pool_rows = grad_pools[tower_num].reshape(row_total, seg_counts[tower_num], model_width)
        grad_output = cot_rows[tower_num].astype(jnp.float32) * valid_cols[tower_num]
        grad_output = grad_output + jnp.einsum(
            "rst,rsd->rtd",
            first_hots[tower_num].astype(jnp.float32),
            pool_rows,
            precision=lax.Precision.HIGHEST,
        ).reshape(-1, model_width)
        norm_two_back = jax.vjp(layer_norm, residual_two, tower_gain[1], tower_bias[5])[1]
        grad_resid_two, grad_gain_two, grad_shift_two = norm_two_back(grad_output)
        grad_ffn = grad_resid_two.astype(jnp.bfloat16)
        grad_ffn_list.append(grad_ffn)
        grad_ffn_bias = jnp.sum(grad_ffn.astype(jnp.float32), axis=0)
        grad_active = inner_cols(grad_ffn, back_weights[3][tower_num])
        gelu_back = jax.vjp(gelu_exact, hidden_pre)[1]
        grad_hidden = gelu_back(grad_active)[0].astype(jnp.bfloat16)
        grad_hidden_list.append(grad_hidden)
        grad_inb_list.append(jnp.sum(grad_hidden.astype(jnp.float32), axis=0))
        grad_normed = grad_resid_two + inner_cols(grad_hidden, back_weights[2][tower_num])
        norm_one_back = jax.vjp(layer_norm, residual, tower_gain[0], tower_bias[3])[1]
        grad_residual, grad_gain_one, grad_shift_one = norm_one_back(grad_normed)
        grad_branch = grad_residual.astype(jnp.bfloat16)
        grad_branch_list.append(grad_branch)
        grad_out_bias = jnp.sum(grad_branch.astype(jnp.float32), axis=0)
        grad_contexts.append(
            inner_cols(grad_branch, back_weights[1][tower_num]).astype(jnp.bfloat16)
        )
        grad_residuals.append(grad_residual)
        small_grads.append(
            (
                grad_out_bias,
                grad_shift_one,
                grad_ffn_bias,
                grad_shift_two,
                grad_gain_one,
                grad_gain_two,
            )
        )
    grad_context_all = jnp.concatenate(grad_contexts, axis=0).reshape(row_shape)
    grad_query, row_delta = lax.map(
        query_back,
        (query_all, keys_full, values_full, seg_local, seg_every, log_sum, grad_context_all),
    )
    query_every, grad_every = (
        lax.all_gather(query_all, "narrow", axis=1, tiled=True),
        lax.all_gather(grad_context_all, "narrow", axis=1, tiled=True),
    )
    log_every, delta_every = (
        lax.all_gather(log_sum, "narrow", axis=2, tiled=True),
        lax.all_gather(row_delta, "narrow", axis=2, tiled=True),
    )
    key_share, value_share = lax.map(
        key_back,
        (
            query_every,
            keys_local,
            values_local,
            seg_every,
            seg_local,
            log_every,
            delta_every,
            grad_every,
        ),
    )
    grad_qkv = jnp.concatenate([grad_query, key_share, value_share], axis=-1).reshape(
        -1, 3 * model_width
    )
    qkv_parts = (grad_qkv[:pass_tokens], grad_qkv[pass_tokens:])
    bias_list = []
    gain_list = []
    input_grads = []
    for tower_num in range(2):
        qkv_part = qkv_parts[tower_num]
        query_bias = jnp.sum(qkv_part[:, :model_width].astype(jnp.float32), axis=0)
        value_bias = jnp.sum(qkv_part[:, 2 * model_width :].astype(jnp.float32), axis=0)
        (
            grad_out_bias,
            grad_shift_one,
            grad_ffn_bias,
            grad_shift_two,
            grad_gain_one,
            grad_gain_two,
        ) = small_grads[tower_num]
        bias_list.append(
            jnp.stack(
                [
                    query_bias,
                    value_bias,
                    grad_out_bias,
                    grad_shift_one,
                    grad_ffn_bias,
                    grad_shift_two,
                ]
            )
        )
        gain_list.append(jnp.stack([grad_gain_one, grad_gain_two]))
        input_grad = grad_residuals[tower_num] + inner_cols(qkv_part, back_weights[0][tower_num])
        input_grads.append(input_grad.astype(jnp.bfloat16))
    left_all = (
        lax.all_gather(inputs[0], "narrow", axis=0, tiled=True),
        lax.all_gather(inputs[1], "narrow", axis=0, tiled=True),
        lax.all_gather(contexts[0], "narrow", axis=0, tiled=True),
        lax.all_gather(contexts[1], "narrow", axis=0, tiled=True),
        lax.all_gather(kept[0][1], "narrow", axis=0, tiled=True),
        lax.all_gather(kept[1][1], "narrow", axis=0, tiled=True),
        lax.all_gather(kept[0][3], "narrow", axis=0, tiled=True),
        lax.all_gather(kept[1][3], "narrow", axis=0, tiled=True),
    )
    right_cols = (
        lax.all_to_all(qkv_parts[0], "narrow", split_axis=1, concat_axis=0, tiled=True),
        lax.all_to_all(qkv_parts[1], "narrow", split_axis=1, concat_axis=0, tiled=True),
        lax.all_to_all(grad_branch_list[0], "narrow", split_axis=1, concat_axis=0, tiled=True),
        lax.all_to_all(grad_branch_list[1], "narrow", split_axis=1, concat_axis=0, tiled=True),
        lax.all_to_all(grad_hidden_list[0], "narrow", split_axis=1, concat_axis=0, tiled=True),
        lax.all_to_all(grad_hidden_list[1], "narrow", split_axis=1, concat_axis=0, tiled=True),
        lax.all_to_all(grad_ffn_list[0], "narrow", split_axis=1, concat_axis=0, tiled=True),
        lax.all_to_all(grad_ffn_list[1], "narrow", split_axis=1, concat_axis=0, tiled=True),
    )
    partials = tuple(
        (inner_rows(left_part, right_part) for left_part, right_part in zip(left_all, right_cols))
    )
    summed = (
        lax.psum_scatter(partials[0], "wide", scatter_dimension=0, tiled=True),
        lax.psum_scatter(partials[1], "wide", scatter_dimension=0, tiled=True),
        lax.psum_scatter(partials[2], "wide", scatter_dimension=0, tiled=True),
        lax.psum_scatter(partials[3], "wide", scatter_dimension=0, tiled=True),
        lax.psum_scatter(partials[4], "wide", scatter_dimension=0, tiled=True),
        lax.psum_scatter(partials[5], "wide", scatter_dimension=0, tiled=True),
        lax.psum_scatter(partials[6], "wide", scatter_dimension=0, tiled=True),
        lax.psum_scatter(partials[7], "wide", scatter_dimension=0, tiled=True),
    )
    small_sum = (
        lax.psum_scatter(bias_list[0], ("wide", "narrow"), scatter_dimension=1, tiled=True),
        lax.psum_scatter(bias_list[1], ("wide", "narrow"), scatter_dimension=1, tiled=True),
        lax.psum_scatter(
            gain_list[0].astype(jnp.float32), ("wide", "narrow"), scatter_dimension=1, tiled=True
        ),
        lax.psum_scatter(
            gain_list[1].astype(jnp.float32), ("wide", "narrow"), scatter_dimension=1, tiled=True
        ),
        lax.psum_scatter(grad_inb_list[0], ("wide", "narrow"), scatter_dimension=0, tiled=True),
        lax.psum_scatter(grad_inb_list[1], ("wide", "narrow"), scatter_dimension=0, tiled=True),
    )
    passage_out = out_rows[0].reshape(passages.shape)
    query_out = out_rows[1].reshape(queries.shape)
    passage_grad = input_grads[0].reshape(passages.shape)
    query_grad = input_grads[1].reshape(queries.shape)
    return (
        passage_out,
        query_out,
        passage_grad,
        query_grad,
        jnp.stack([summed[0], summed[1]]),
        jnp.stack([summed[2], summed[3]]),
        jnp.stack([summed[4], summed[5]]),
        jnp.stack([summed[6], summed[7]]),
        jnp.stack([small_sum[0], small_sum[1]]),
        jnp.stack([small_sum[2], small_sum[3]]),
        jnp.stack([small_sum[4], small_sum[5]]),
        rms_stats,
    )


def solution(mesh):
    return jax.shard_map(
        body,
        mesh=mesh,
        in_specs=(
            P("wide", "narrow", None),
            P("wide", "narrow", None),
            P("wide", "narrow", None),
            P("wide", "narrow", None),
            P("wide", None),
            P("wide", None),
            P("wide"),
            P(None, ("wide", "narrow"), None),
            P(None, ("wide", "narrow"), None),
            P(None, ("wide", "narrow"), None),
            P(None, ("wide", "narrow"), None),
            P(None, None, ("wide", "narrow")),
            P(None, None, ("wide", "narrow")),
            P(None, ("wide", "narrow")),
        ),
        out_specs=(
            P("wide", "narrow", None),
            P("wide", "narrow", None),
            P("wide", "narrow", None),
            P("wide", "narrow", None),
            P(None, "wide", "narrow"),
            P(None, "wide", "narrow"),
            P(None, "wide", "narrow"),
            P(None, "wide", "narrow"),
            P(None, None, ("wide", "narrow")),
            P(None, None, ("wide", "narrow")),
            P(None, ("wide", "narrow")),
            P(),
        ),
        check_vma=False,
    )
```

profile of v0, /device:TPU:0, one launch (start us, length us, event | category | flops | bytes accessed | tf_op | source)
XLA Modules:
  0.0 1402.1 jit_solution(9426912883568873879)
XLA Ops:
  8.7 44.8 %all_gather.72 = bf16[2,6,768]{1,0,2:T(2,128)(2,1)S(1)} all-gather(bf16[2,6,24]{1,0,2:T(2,128)(2,1)S(1)} %copy.157), channel_id=1, replica_groups=mesh['wide'=8,'narrow'=4] {'wide','narrow'}, dimensions={2}, use_global_device_ids=true | all-gather | bytes 19008 | tf_op jit(solution)/shard_map/all_gather | solution.py:181
  53.6 29.6 %fusion.82 = (f32[768]{0:T(1024)}, f32[768]{0:T(1024)}, f32[768]{0:T(1024)}, f32[768]{0:T(1024)S(1)}, f32[768]{0:T(1024)}, /*index=5*/f32[768]{0:T(1024)}, f32[7...) fusion(bf16[2,6,768]{1,0,2:T(2,128)(2,1)S(1)} %all_gather.72), kind=kLoop, calls=%fused_computation.203 | loop fusion | flops 9216 | bytes 55296 | tf_op jit(solution)/shard_map/convert_element_type | solution.py:29
  100.4 20.9 %all-gather.20.cloned.1.call-done = bf16[4,512,768]{1,2,0:T(8,128)(2,1)} async-done(((bf16[4,128,768]{1,2,0:T(8,128)(2,1)}), bf16[4,512,768]{1,2,0:T(8,128)(2,1)}) %all-gather.20.cloned.1.call-update) | async-done | bytes 3145744 | tf_op jit(solution)/shard_map/all_gather | solution.py:199
  121.3 30.6 %all-gather.22.cloned.1.call-done = bf16[4,512,768]{1,2,0:T(8,128)(2,1)} async-done(((bf16[4,128,768]{1,2,0:T(8,128)(2,1)}), bf16[4,512,768]{1,2,0:T(8,128)(2,1)}) %all-gather.22.cloned.1.call-update) | async-done | bytes 3145744 | tf_op jit(solution)/shard_map/all_gather | solution.py:198
  151.9 21.7 %while.36 = (s32[]{:T(128)}, bf16[4,128,768]{1,2,0:T(8,128)(2,1)S(1)}, f32[4,12,128]{2,1,0:T(8,128)S(1)}, bf16[4,512,768]{1,2,0:T(8,128)(2,1)}, s32[4,128]{1,0:T...) while((s32[]{:T(128)}, ...), condition=%wide.region_9.10_spmd, body=%wide.region_6.9_spmd.sunk | while | flops 210926080 | bytes 15660661 | solution.py:201
  175.7 40.4 %all-gather.2 = bf16[32,96,2]{1,2,0:T(2,128)(2,1)S(1)} all-gather(bf16[1,96,2]{1,2,0:T(2,128)(2,1)S(1)} %bitcast.481), channel_id=1, replica_groups=mesh['wide'=8,'narrow'=4] {'wide','narrow'}, dimensions={0}, use_global_device_ids=true | all-gather | bytes 12672 | tf_op jit(solution)/shard_map/all_gather | solution.py:183
  216.2 38.3 %all_gather.76 = bf16[2,2,768]{1,0,2:T(2,128)(2,1)S(1)} all-gather(bf16[2,2,24]{1,0,2:T(2,128)(2,1)S(1)} %copy.162), channel_id=1, replica_groups=mesh['wide'=8,'narrow'=4] {'wide','narrow'}, dimensions={2}, use_global_device_ids=true | all-gather | bytes 6336 | tf_op jit(solution)/shard_map/all_gather | solution.py:182
  256.1 9.7 fusion.83
  268.6 27.9 %all-gather.26.cloned.1.call-done = bf16[2,768,3072]{2,1,0:T(8,128)(2,1)} async-done(((bf16[2,24,3072]{2,1,0:T(8,128)(2,1)}), bf16[2,768,3072]{2,1,0:T(8,128)(2,1)}) %all-gather.26.cloned.1.call-update) | async-done | bytes 9437200 | tf_op jit(solution)/shard_map/all_gather | solution.py:179
  296.5 8.3 multiply_convert_fusion.8
  304.8 75.2 %all-gather.28.cloned.1.call-done = bf16[2,3072,768]{2,1,0:T(8,128)(2,1)} async-done(((bf16[2,96,768]{2,1,0:T(8,128)(2,1)}), bf16[2,3072,768]{2,1,0:T(8,128)(2,1)}) %all-gather.28.cloned.1.call-update) | async-done | bytes 9437200 | tf_op jit(solution)/shard_map/all_gather | solution.py:180
  380.0 4.1 fusion.79
  387.3 15.3 %multiply_convert_fusion.7 = (bf16[384,3072]{1,0:T(8,128)(2,1)}, f32[384,3072]{1,0:T(8,128)}, f32[384,3072]{1,0:T(8,128)}) fusion(f32[3072]{0:T(1024)S(1)} %bitcast.478, bf16[384,768]{1,0:T(8,128)(2,1)S(1)} %fusion.72, bf16[2,768,3072]{2,1,0:T(8,128)(2,1)} %all-gather.26.cloned.1.call-done), kind=kOutput, calls=%fused_computation.74 | convolution fusion | flops 1889796096 | bytes 17117184 | tf_op jit(solution)/shard_map/dot_general | solution.py:45
  402.7 6.2 fusion.144
  410.9 13.7 all-reduce.7
  424.6 31.0 %all-gather.3 = bf16[8,12,768]{2,1,0:T(8,128)(2,1)S(1)} all-gather(bf16[1,12,768]{2,1,0:T(8,128)(2,1)} %bitcast.475), channel_id=1, replica_groups=mesh['wide'=8,'narrow'=4] {'wide'}, dimensions={0}, use_global_device_ids=true | all-gather | bytes 165888 | tf_op jit(solution)/shard_map/all_gather | solution.py:256
  469.7 4.8 convert_reduce_fusion.1
  474.5 5.1 multiply_reduce_fusion.8
  490.9 8.9 convert_reduce_fusion
  523.3 14.8 %all_gather.90 = bf16[512,768]{1,0:T(8,128)(2,1)} all-gather(bf16[128,768]{1,0:T(8,128)(2,1)S(1)} %fusion.101), channel_id=1, replica_groups=mesh['wide'=8,'narrow'=4] {'narrow'}, dimensions={0}, use_global_device_ids=true | all-gather | bytes 983040 | tf_op jit(solution)/shard_map/all_gather | solution.py:394
  538.1 8.7 all-gather.1
  546.9 5.9 all_gather.82
  554.8 28.4 %while.37 = (s32[]{:T(128)}, bf16[4,128,768]{2,1,0:T(8,128)(2,1)S(1)}, f32[4,12,128]{2,1,0:T(8,128)S(1)}, bf16[4,512,768]{1,2,0:T(8,128)(2,1)}, s32[4,128]{1,0:T...) while((s32[]{:T(128)}, ...), condition=%wide.region_33.34_spmd, body=%wide.region_31.33_spmd.sunk | while | flops 310901248 | bytes 23654024 | solution.py:329
  590.2 11.5 all_gather.84
  606.4 4.2 all-to-all-start.6
  616.2 54.4 %while.38 = (s32[]{:T(128)}, bf16[4,128,768]{2,1,0:T(8,128)(2,1)}, bf16[4,128,768]{2,1,0:T(8,128)(2,1)}, bf16[4,512,768]{1,2,0:T(8,128)(2,1)}, s32[4,512]{1,0:T(...) while((s32[]{:T(128)}, bf16[4,128,768]{2,1,0:T(8,128)(2,1)}, ...), condition=%wide.region_35.36_spmd, body=%wide.region_34.35_spmd.sunk | while | flops 410877952 | bytes 25903864 | solution.py:341
  638.6 3.8 fusion.255
  665.9 3.9 fusion.255
  685.0 37.4 %all_to_all.157 = bf16[384,4,768]{2,0,1:T(8,128)(2,1)} all-to-all(bf16[384,4,768]{2,0,1:T(8,128)(2,1)S(1)} %bitcast.436), channel_id=1, replica_groups=mesh['wide'=8,'narrow'=4] {'narrow'}, dimensions={1} | all-to-all | bytes 4718592 | tf_op jit(solution)/shard_map/all_to_all | solution.py:403
  722.3 5.9 fusion.152
  729.3 4.2 all-to-all-start.2
  733.5 15.0 %all-gather = bf16[1,512,768]{2,1,0:T(8,128)(2,1)} all-gather(bf16[1,128,768]{2,1,0:T(8,128)(2,1)S(1)} %copy-done.24), channel_id=2, replica_groups=mesh['wide'=8,'narrow'=4] {'narrow'}, dimensions={1}, use_global_device_ids=true | all-gather | bytes 983040 | tf_op jit(solution)/shard_map/all_gather | solution.py:390
  755.7 3.9 copy.173
  759.6 24.6 %all_to_all.158 = bf16[384,4,576]{0,2,1:T(8,128)(2,1)S(1)} all-to-all(bf16[384,4,576]{0,2,1:T(8,128)(2,1)S(1)} %copy.173), channel_id=1, replica_groups=mesh['wide'=8,'narrow'=4] {'narrow'}, dimensions={1} | all-to-all | bytes 3538944 | tf_op jit(solution)/shard_map/all_to_all | solution.py:399
  792.4 7.7 all_to_all.159
  800.1 4.1 fusion.102
  805.6 12.1 all_to_all.160
  817.8 7.1 fusion.154
  826.7 8.2 reduce-scatter.17.cloned.1.call-done
  836.5 4.2 fusion.70
  840.8 4.4 fusion.59
  845.1 119.7 %all-reduce.10.cloned.1.call-done = (f32[6,768]{1,0:T(8,128)}, f32[6,768]{1,0:T(8,128)}, f32[2,768]{1,0:T(2,128)}, f32[2,768]{1,0:T(2,128)}, f32[3072]{0:T(1024)...) async-done(((f32[6,768]{1,0:T(8,128)}, f32[6,768]{1,0:T(8,128)}, f32[2,768]{1,0:T(2,128)}, f32[2,768]{1,0:T(2,128)}, f32[3072]{0:T(1024)}, /*index=5*/f32[3072]{0:T(1024)}, ...) | async-done | bytes 73784
  973.1 65.5 %reduce-scatter.23.cloned.1.call-done = f32[96,768]{1,0:T(8,128)} async-done(((f32[768,768]{1,0:T(8,128)}), f32[96,768]{1,0:T(8,128)}) %reduce-scatter.23.cloned.1.call-update) | async-done | bytes 294928 | tf_op jit(solution)/shard_map/reduce_scatter | solution.py:417
  1038.6 71.9 %reduce-scatter.21.cloned.1.call-done = f32[96,768]{1,0:T(8,128)} async-done(((f32[768,768]{1,0:T(8,128)}), f32[96,768]{1,0:T(8,128)}) %reduce-scatter.21.cloned.1.call-update) | async-done | bytes 294928 | tf_op jit(solution)/shard_map/reduce_scatter | solution.py:416
  1112.4 67.9 %reduce-scatter.31.cloned.1.call-done = f32[96,576]{1,0:T(8,128)} async-done(((f32[768,576]{1,0:T(8,128)}), f32[96,576]{1,0:T(8,128)}) %reduce-scatter.31.cloned.1.call-update) | async-done | bytes 221200
  1181.4 67.9 %reduce-scatter.29.cloned.1.call-done = f32[96,576]{1,0:T(8,128)} async-done(((f32[768,576]{1,0:T(8,128)}), f32[96,576]{1,0:T(8,128)}) %reduce-scatter.29.cloned.1.call-update) | async-done | bytes 221200
  1251.5 69.7 %reduce-scatter.27.cloned.1.call-done = f32[384,192]{0,1:T(8,128)} async-done(((f32[3072,192]{0,1:T(8,128)}), f32[384,192]{0,1:T(8,128)}) %reduce-scatter.27.cloned.1.call-update) | async-done | bytes 294928 | tf_op jit(solution)/shard_map/reduce_scatter | solution.py:419
  1321.2 71.9 %reduce-scatter.25.cloned.1.call-done = f32[384,192]{0,1:T(8,128)} async-done(((f32[3072,192]{0,1:T(8,128)}), f32[384,192]{0,1:T(8,128)}) %reduce-scatter.25.cloned.1.call-update) | async-done | bytes 294928 | tf_op jit(solution)/shard_map/reduce_scatter | solution.py:418
  (614 shorter events, 244.1 us)
Async XLA Ops:
  7.2 79.6 %all-gather.18.cloned.1.call-start = ((), (), s32[]{:S(2)}) async-start(), calls=%async_computation.17 | async-start | bytes 7299072 | tf_op jit(solution)/shard_map/all_gather | solution.py:177
  7.9 113.4 %all-gather.20.cloned.1.call-start = ((), (), s32[]{:S(2)}) async-start(), calls=%async_computation.18 | async-start | bytes 3932160 | tf_op jit(solution)/shard_map/all_gather | solution.py:199
  53.6 33.2 %copy-start.12 = (bf16[3,128,768]{2,1,0:T(8,128)(2,1)S(1)}, bf16[3,128,768]{2,1,0:T(8,128)(2,1)}, u32[]{:S(2)}) copy-start(bf16[3,128,768]{2,1,0:T(8,128)(2,1)} %param.20) | copy-start | bytes 1769476
  93.7 58.2 %all-gather.22.cloned.1.call-start = ((), (), s32[]{:S(2)}) async-start(), calls=%async_computation.19 | async-start | bytes 3932160 | tf_op jit(solution)/shard_map/all_gather | solution.py:198
  96.4 170.1 %all-gather.24.cloned.1.call-start = ((), (), s32[]{:S(2)}) async-start(), calls=%async_computation.20 | async-start | bytes 2433024 | tf_op jit(solution)/shard_map/all_gather | solution.py:178
  97.0 199.5 %all-gather.26.cloned.1.call-start = ((), (), s32[]{:S(2)}) async-start(), calls=%async_computation.21 | async-start | bytes 9732096 | tf_op jit(solution)/shard_map/all_gather | solution.py:179
  97.6 282.4 %all-gather.28.cloned.1.call-start = ((), (), s32[]{:S(2)}) async-start(), calls=%async_computation.22 | async-start | bytes 9732096 | tf_op jit(solution)/shard_map/all_gather | solution.py:180
  98.1 512.6 %all-gather.36.cloned.1.call-start = ((), (), s32[]{:S(2)}) async-start(), calls=%async_computation.26 | async-start | bytes 2949120 | tf_op jit(solution)/shard_map/all_gather | solution.py:391
  99.1 155.3 %copy-start.101 = (s32[128]{0:T(128)}, s32[128]{0:T(128)S(1)}, u32[]{:S(2)}) copy-start(s32[128]{0:T(128)S(1)} %convert_reduce_fusion.13) | copy-start | bytes 1540
  99.2 156.3 %copy-start.49 = (s32[3,128]{1,0:T(4,128)}, s32[3,128]{1,0:T(4,128)S(1)}, u32[]{:S(2)}) copy-start(s32[3,128]{1,0:T(4,128)S(1)} %convert_reduce_fusion.14) | copy-start | bytes 4612
  173.6 92.2 %copy-start.2 = (bf16[4,128,768]{1,2,0:T(8,128)(2,1)}, bf16[4,128,768]{1,2,0:T(8,128)(2,1)S(1)}, u32[]{:S(2)}) copy-start(bf16[4,128,768]{1,2,0:T(8,128)(2,1)S(1)} %get-tuple-element.948) | copy-start | bytes 2359300
  173.6 92.2 %copy-start.34 = (f32[4,12,128]{2,1,0:T(8,128)}, f32[4,12,128]{2,1,0:T(8,128)S(1)}, u32[]{:S(2)}) copy-start(f32[4,12,128]{2,1,0:T(8,128)S(1)} %get-tuple-element.842) | copy-start | bytes 73732
  173.6 92.9 %copy-start.25 = (bf16[4,128,768]{1,2,0:T(8,128)(2,1)}, bf16[4,128,768]{1,2,0:T(8,128)(2,1)S(1)}, u32[]{:S(2)}) copy-start(bf16[4,128,768]{1,2,0:T(8,128)(2,1)S(1)} %get-tuple-element.166) | copy-start | bytes 2359300
  175.0 439.3 %all-gather.30.cloned.1.call-start = ((), (), s32[]{:S(2)}) async-start(), calls=%async_computation.23 | async-start | bytes 3932160 | tf_op jit(solution)/shard_map/all_gather | solution.py:334
  265.8 39.0 %copy-start.39 = (f32[768]{0:T(1024)}, f32[768]{0:T(1024)S(1)}, u32[]{:S(2)}) copy-start(f32[768]{0:T(1024)S(1)} %get-tuple-element.438) | copy-start | bytes 9220
  268.2 111.8 %copy-start.85 = (f32[128]{0:T(128)}, f32[128]{0:T(128)S(1)}, u32[]{:S(2)}) copy-start(f32[128]{0:T(128)S(1)} %broadcast_multiply_fusion.4) | copy-start | bytes 1540
  268.4 28.1 %copy-start.96 = (f32[128]{0:T(128)}, f32[128]{0:T(128)S(1)}, u32[]{:S(2)}) copy-start(f32[128]{0:T(128)S(1)} %multiply_reduce_fusion.12) | copy-start | bytes 1540
  268.4 111.5 %copy-start.89 = (f32[128]{0:T(128)}, f32[128]{0:T(128)S(1)}, u32[]{:S(2)}) copy-start(f32[128]{0:T(128)S(1)} %fusion.127) | copy-start | bytes 1540
  296.5 83.5 %copy-start.63 = (f32[768]{0:T(1024)S(1)}, f32[768]{0:T(1024)}, u32[]{:S(2)}) copy-start(f32[768]{0:T(1024)} %get-tuple-element.443) | copy-start | bytes 9220
  296.5 83.5 %copy-start.88 = (f32[768]{0:T(1024)S(1)}, f32[768]{0:T(1024)}, u32[]{:S(2)}) copy-start(f32[768]{0:T(1024)} %get-tuple-element.442) | copy-start | bytes 9220
  296.5 83.5 %copy-start.106 = (f32[128]{0:T(128)S(1)}, f32[128]{0:T(128)}, u32[]{:S(2)}) copy-start(f32[128]{0:T(128)} %compare_convert_fusion) | copy-start | bytes 1540
  304.8 79.4 %copy-start.30 = (bf16[128,3072]{1,0:T(8,128)(2,1)}, bf16[128,3072]{1,0:T(8,128)(2,1)S(1)}, u32[]{:S(2)}) copy-start(bf16[128,3072]{1,0:T(8,128)(2,1)S(1)} %get-tuple-element.543) | copy-start | bytes 2359300
  384.2 83.9 %copy-start.3 = (f32[128,768]{1,0:T(8,128)}, f32[128,768]{1,0:T(8,128)S(1)}, u32[]{:S(2)}) copy-start(f32[128,768]{1,0:T(8,128)S(1)} %get-tuple-element.576) | copy-start | bytes 1179652
  384.2 26.4 %copy-start.75 = (f32[128]{0:T(128)}, f32[128]{0:T(128)S(1)}, u32[]{:S(2)}) copy-start(f32[128]{0:T(128)S(1)} %broadcast_multiply_fusion.3) | copy-start | bytes 1540
  384.9 25.7 %copy-start.83 = (f32[128]{0:T(128)}, f32[128]{0:T(128)S(1)}, u32[]{:S(2)}) copy-start(f32[128]{0:T(128)S(1)} %fusion.128) | copy-start | bytes 1540
  386.6 16.1 %copy-start.47 = (f32[384]{0:T(512)}, f32[384]{0:T(512)S(1)}, u32[]{:S(2)}) copy-start(f32[384]{0:T(512)S(1)} %broadcast_multiply_fusion.1) | copy-start | bytes 4612
  461.2 21.3 %all-to-all-start = ((bf16[8,12,768]{2,1,0:T(8,128)(2,1)}), bf16[8,12,768]{2,1,0:T(8,128)(2,1)S(1)}, u32[]{:S(2)}, u32[]{:S(2)}) async-start(bf16[8,12,768]{2,1,0:T(8,128)(2,1)} %reshape.828), calls=%async_computation | async-start | bytes 393216 | tf_op jit(solution)/shard_map/all_to_all | solution.py:21
  464.6 149.7 %all-gather.32.cloned.1.call-start = ((), (), s32[]{:S(2)}) async-start(), calls=%async_computation.24 | async-start | bytes 3932160 | tf_op jit(solution)/shard_map/all_gather | solution.py:335
  506.7 215.6 %all-gather.38.cloned.1.call-start = ((), (), s32[]{:S(2)}) async-start(), calls=%async_computation.29 | async-start | bytes 2949120 | tf_op jit(solution)/shard_map/all_gather | solution.py:393
  507.4 278.3 %all-gather.34.cloned.1.call-start = ((), (), s32[]{:S(2)}) async-start(), calls=%async_computation.25 | async-start | bytes 2949120 | tf_op jit(solution)/shard_map/all_gather | solution.py:389
  508.1 292.0 %all-gather.42.cloned.1.call-start = ((), (), s32[]{:S(2)}) async-start(), calls=%async_computation.34 | async-start | bytes 3932160 | tf_op jit(solution)/shard_map/all_gather | solution.py:396
  508.7 309.1 %all-gather.40.cloned.1.call-start = ((), (), s32[]{:S(2)}) async-start(), calls=%async_computation.32 | async-start | bytes 11796480 | tf_op jit(solution)/shard_map/all_gather | solution.py:395
  512.7 34.1 %copy-start.35 = (f32[4,12,128]{2,1,0:T(8,128)S(1)}, f32[4,12,128]{2,1,0:T(8,128)}, u32[]{:S(2)}) copy-start(f32[4,12,128]{2,1,0:T(8,128)} %copy-done.34) | copy-start | bytes 73732
  517.3 36.1 %all-to-all-start.4 = ((bf16[128,4,192]{0,2,1:T(8,128)(2,1)}), bf16[128,4,192]{0,2,1:T(8,128)(2,1)S(1)}, u32[]{:S(2)}, u32[]{:S(2)}) async-start(bf16[128,4,192]{0,2,1:T(8,128)(2,1)} %bitcast.78), calls=%async_computation.5 | async-start | bytes 393216 | tf_op jit(solution)/shard_map/all_to_all | solution.py:402
  520.7 306.0 %reduce-scatter.19.cloned.1.call-start = ((), (), s32[]{:S(2)}) async-start(), calls=%async_computation.28 | async-start | bytes 884736 | tf_op jit(solution)/shard_map/reduce_scatter | solution.py:415
  554.8 31.3 %copy-start.77 = (bf16[768]{0:T(1024)(128)(2,1)S(1)}, bf16[768]{0:T(1024)(128)(2,1)}, u32[]{:S(2)}) copy-start(bf16[768]{0:T(1024)(128)(2,1)} %get-tuple-element.591) | copy-start | bytes 4612
  554.8 31.9 %copy-start.74 = (bf16[768]{0:T(1024)(128)(2,1)S(1)}, bf16[768]{0:T(1024)(128)(2,1)}, u32[]{:S(2)}) copy-start(bf16[768]{0:T(1024)(128)(2,1)} %get-tuple-element.418) | copy-start | bytes 4612
  586.7 19.7 %all-to-all-start.3 = ((bf16[384,4,192]{0,2,1:T(8,128)(2,1)}), bf16[384,4,192]{0,2,1:T(8,128)(2,1)S(1)}, u32[]{:S(2)}, u32[]{:S(2)}) async-start(bf16[384,4,192]{0,2,1:T(8,128)(2,1)} %bitcast.74), calls=%async_computation.3 | async-start | bytes 1179648 | tf_op jit(solution)/shard_map/all_to_all | solution.py:401
  606.4 73.2 %all-to-all-start.6 = ((bf16[128,4,768]{2,0,1:T(8,128)(2,1)}), bf16[128,4,768]{2,0,1:T(8,128)(2,1)}, u32[]{:S(2)}, u32[]{:S(2)}) async-start(bf16[128,4,768]{2,0,1:T(8,128)(2,1)} %bitcast.338), calls=%async_computation.9 | async-start | bytes 1572864 | tf_op jit(solution)/shard_map/all_to_all | solution.py:404
  610.6 224.2 %reduce-scatter.17.cloned.1.call-start = ((), (), s32[]{:S(2)}) async-start(), calls=%async_computation.27 | async-start | bytes 884736 | tf_op jit(solution)/shard_map/reduce_scatter | solution.py:414
  614.2 350.7 %all-reduce.10.cloned.1.call-start = ((), (), s32[]{:S(2)}) async-start(), calls=%async_computation.38 | async-start | bytes 175104
  679.4 359.2 %reduce-scatter.23.cloned.1.call-start = ((), (), s32[]{:S(2)}) async-start(), calls=%async_computation.31 | async-start | bytes 2654208 | tf_op jit(solution)/shard_map/reduce_scatter | solution.py:417
  683.1 427.4 %reduce-scatter.21.cloned.1.call-start = ((), (), s32[]{:S(2)}) async-start(), calls=%async_computation.30 | async-start | bytes 2654208 | tf_op jit(solution)/shard_map/reduce_scatter | solution.py:416
  729.3 19.2 %all-to-all-start.2 = ((bf16[128,4,576]{0,2,1:T(8,128)(2,1)}), bf16[128,4,576]{0,2,1:T(8,128)(2,1)}, u32[]{:S(2)}, u32[]{:S(2)}) async-start(bf16[128,4,576]{0,2,1:T(8,128)(2,1)} %bitcast.69), calls=%async_computation.2 | async-start | bytes 1179648 | tf_op jit(solution)/shard_map/all_to_all | solution.py:400
  733.5 446.8 %reduce-scatter.31.cloned.1.call-start = ((), (), s32[]{:S(2)}) async-start(), calls=%async_computation.37 | async-start | bytes 2211840
  752.4 497.0 %reduce-scatter.29.cloned.1.call-start = ((), (), s32[]{:S(2)}) async-start(), calls=%async_computation.36 | async-start | bytes 2211840
  791.2 529.9 %reduce-scatter.27.cloned.1.call-start = ((), (), s32[]{:S(2)}) async-start(), calls=%async_computation.35 | async-start | bytes 2654208 | tf_op jit(solution)/shard_map/reduce_scatter | solution.py:419
  804.2 588.9 %reduce-scatter.25.cloned.1.call-start = ((), (), s32[]{:S(2)}) async-start(), calls=%async_computation.33 | async-start | bytes 2654208 | tf_op jit(solution)/shard_map/reduce_scatter | solution.py:418
  (104 other events, 458.1 us)
Sparse Core Ops, SparseCore 0:
  11.0 75.7 all-gather.17
  93.8 27.4 all-gather.19
  122.9 28.9 all-gather.21
  154.7 57.3 all-gather.23
  214.8 81.6 all-gather.25
  299.3 80.6 all-gather.27
  382.1 22.6 all-gather.35
  406.3 29.4 all-gather.29
  506.8 35.8 all-gather.31
  544.7 24.0 all-gather.37
  570.4 24.0 all-gather.33
  595.9 37.0 all-gather.41
  634.5 69.8 all-gather.39
  707.5 62.3 reduce-scatter.18
  773.4 61.4 reduce-scatter.16
  842.3 122.5 all-reduce.9
  968.6 69.9 reduce-scatter.22
  1042.4 68.0 reduce-scatter.20
  1114.4 65.8 reduce-scatter.30
  1183.6 65.6 reduce-scatter.28
  1253.2 67.8 reduce-scatter.26
  1325.1 67.9 reduce-scatter.24
where the time goes:
time: 1410 us; the launch traced here: 1400 us
  waiting for transfers between devices  706 us (50%)
  blocking collectives  306 us (22%)
  matrix products  160 us (11%)
  local copies, waits for them, and re-layouts  114 us (8%)
  other arithmetic  78.5 us (6%)
  starting transfers between devices  20.7 us (1%)
  between operations  16.1 us (1%)
    unnamed x25, waiting for transfers between devices  260 us
    all_gather x1, waiting for transfers between devices, body(): lax.all_gather(w_back, ('wide', 'narrow'), axis=1, tiled=True)  75.2 us
    reduce_scatter x1, waiting for transfers between devices, body(): lax.psum_scatter(partials[6], 'wide', scatter_dimension=0, tiled=True)  71.9 us
    reduce_scatter x1, waiting for transfers between devices, body(): lax.psum_scatter(partials[4], 'wide', scatter_dimension=0, tiled=True)  71.9 us
    reduce_scatter x1, waiting for transfers between devices, body(): lax.psum_scatter(partials[7], 'wide', scatter_dimension=0, tiled=True)  69.7 us
    reduce_scatter x1, waiting for transfers between devices, body(): lax.psum_scatter(partials[5], 'wide', scatter_dimension=0, tiled=True)  65.5 us
    all_gather x1, blocking collectives, body(): lax.all_gather(biases, ('wide', 'narrow'), axis=2, tiled=True)  44.8 us
    dot_general x9, matrix products, matmul(): return jnp.dot(left, right, preferred_element_type=jnp.float32)  43.4 us
  transfers between devices with their start and end apart: 27, of which 13 were waited for; matrix products, arithmetic and copies ran while one was open for 24% of the time, Pallas kernels for 0%

commit v1 on v0

v1 whole, which is shorter than its diff:
```python
import functools

import jax
import jax.numpy as jnp
from jax import lax
from jax.experimental import pallas as pl
from jax.experimental.pallas import tpu as pltpu
from jax.sharding import PartitionSpec as P

HEAD_DIM = 64
LEVELS = 4
EPSILON = 1e-05
SCORE_DIV = 12.0
MASKED = -1e30
BF = jnp.bfloat16
F32 = jnp.float32
BOTH = ("wide", "narrow")


def matmul(left, right):
    return jnp.dot(left, right, preferred_element_type=F32)


def inner_rows(left, right):
    return lax.dot_general(left, right, (((0,), (0,)), ((), ())), preferred_element_type=F32)


def inner_cols(left, right):
    return lax.dot_general(left, right, (((1,), (1,)), ((), ())), preferred_element_type=F32)


def layer_norm(inputs, gain_row, shift_row):
    row_mean = jnp.mean(inputs, axis=-1, keepdims=True)
    centered = inputs - row_mean
    row_var = jnp.mean(centered * centered, axis=-1, keepdims=True)
    return centered * lax.rsqrt(row_var + EPSILON) * gain_row + shift_row


def gelu_exact(inputs):
    return jax.nn.gelu(inputs, approximate=False)


def split_heads(matrix):
    return matrix.reshape(matrix.shape[0], matrix.shape[1] // HEAD_DIM, HEAD_DIM)


def flip(x, axis, mask):
    size = lax.axis_size(axis)
    return lax.ppermute(x, axis, [(i, i ^ mask) for i in range(size)])


def swap_levels(x, k, stride):
    pairs = []
    for i in range(stride):
        pairs += [(i, k * stride + i), (k * stride + i, i)]
    return lax.ppermute(x, "wide", pairs)


def bits_of(size):
    return [1 << b for b in range(size.bit_length() - 1)]


class Place:
    def __init__(self):
        self.wide = lax.axis_size("wide")
        self.narrow = lax.axis_size("narrow")
        self.stride = self.wide // LEVELS
        self.w = lax.axis_index("wide")
        self.n = lax.axis_index("narrow")
        self.z = self.w // self.stride
        self.y = self.w % self.stride
        self.me = self.w * self.narrow + self.n


def to_rows(place, pass_part, query_part):
    s = place.stride
    got = []
    for k in range(1, LEVELS):
        got.append(swap_levels(jnp.where(place.z == 0, pass_part[k - 1], query_part[0]), k, s))
    spare = got[0] + got[1] + got[2]
    four = [
        jnp.where(place.z == 0, query_part[0], pass_part[0]),
        jnp.where(place.z == 0, got[0], pass_part[1]),
        jnp.where(place.z == 0, got[1], pass_part[2]),
        jnp.where(place.z == 0, got[2], spare),
    ]
    mine = lax.all_to_all(jnp.stack(four), "narrow", 0, 0, tiled=True)
    return mine.reshape(-1, mine.shape[-1])


def from_rows(place, row):
    s = place.stride
    four = lax.all_to_all(
        row.reshape(place.narrow, -1, row.shape[-1]), "narrow", 0, 0, tiled=True
    )
    got = []
    for k in range(1, LEVELS):
        got.append(swap_levels(jnp.where(place.z == 0, four[k], four[3]), k, s))
    spare = got[0] + got[1] + got[2]
    pass_part = jnp.where(place.z == 0, jnp.stack(got), four[:3])
    query_part = jnp.where(place.z == 0, four[0], spare)[None]
    return pass_part, query_part


def assemble_kernel(plan, widths, me_ref, *refs):
    pieces, outs = refs[: len(plan)], refs[len(plan) :]
    me = me_ref[0]
    for piece, masks in zip(pieces, plan):
        for slot, mask in enumerate(masks):
            column = 0
            for out, width in zip(outs, widths):
                out[me ^ mask] = piece[slot, :, column : column + width]
                column += width


def assemble(place, pieces, plan, widths):
    total = place.wide * place.narrow
    rows = pieces[0].shape[1]
    vmem = pl.BlockSpec(memory_space=pltpu.VMEM)
    outs = pl.pallas_call(
        functools.partial(assemble_kernel, plan, widths),
        out_shape=[jax.ShapeDtypeStruct((total, rows, width), BF) for width in widths],
        in_specs=[pl.BlockSpec(memory_space=pltpu.SMEM)] + [vmem] * len(pieces),
        out_specs=[vmem] * len(widths),
        compiler_params=pltpu.CompilerParams(vmem_limit_bytes=32 << 20),
    )(place.me.reshape(1), *pieces)
    return [out.reshape(total * rows, out.shape[-1]) for out in outs]


def gather_tower(place, pair, widths):
    s, narrow = place.stride, place.narrow
    level = s * narrow
    slots = [jnp.where(place.z == 0, pair[1], pair[0])]
    for k in range(1, LEVELS):
        send = jnp.where((place.z ^ k) == 0, pair[1], pair[0])
        slots.append(flip(send, "wide", k * s))
    first, first_masks = jnp.stack(slots[:2]), [0, level]
    second, second_masks = jnp.stack(slots[2:]), [2 * level, 3 * level]
    pieces, plan = [], []

    def keep(piece, masks):
        pieces.append(piece)
        plan.append(tuple(masks))
        pieces.append(flip(piece, "narrow", 1))
        plan.append(tuple(m ^ 1 for m in masks))

    for b in bits_of(s):
        other = flip(first, "wide", b)
        first = jnp.concatenate([first, other])
        first_masks = first_masks + [m ^ (b * narrow) for m in first_masks]
    keep(first, first_masks)
    keep(flip(first, "narrow", 2), [m ^ 2 for m in first_masks])
    keep(second, second_masks)
    other = flip(second, "narrow", 2)
    keep(other, [m ^ 2 for m in second_masks])
    second = jnp.concatenate([second, other])
    second_masks = second_masks + [m ^ 2 for m in second_masks]
    for b in bits_of(s):
        other = flip(second, "wide", b)
        other_masks = [m ^ (b * narrow) for m in second_masks]
        keep(other, other_masks)
        second = jnp.concatenate([second, other])
        second_masks = second_masks + other_masks
    return assemble(place, pieces, plan, widths)


def pick(x, index, dim):
    return lax.dynamic_index_in_dim(x, index, dim, keepdims=False)


def halve(x, place, axis, mask, dim):
    index = place.n if axis == "narrow" else place.w
    bit = jnp.where((index & mask) != 0, 1, 0)
    got = flip(pick(x, 1 - bit, dim).astype(BF), axis, mask)
    return pick(x, bit, dim) + got.astype(F32)


def scatter_tower(place, partial):
    s = place.stride
    rows, narrow, cols = partial.shape
    per = rows // place.wide
    x = partial.reshape(rows, 2, 2, cols)
    x = halve(x, place, "narrow", 1, 2)
    x = x.reshape(LEVELS, s, per, 2, cols)
    first, second = x[:2], x[2:]

    def over_columns(part):
        for b in reversed(bits_of(s)):
            shape = part.shape
            part = part.reshape(shape[0], 2, shape[1] // 2, *shape[2:])
            part = halve(part, place, "wide", b, 1)
        return part[:, 0]

    first = over_columns(halve(first, place, "narrow", 2, 3))
    second = halve(over_columns(second), place, "narrow", 2, 2)
    levels = jnp.concatenate([first, second])
    slots = [pick(levels, place.z, 0)]
    for k in range(1, LEVELS):
        got = flip(pick(levels, place.z ^ k, 0).astype(BF), "wide", k * s)
        slots.append(got.astype(F32))
    tower0 = sum(jnp.where(place.z == k, 0.0, slots[k]) for k in range(LEVELS))
    tower1 = sum(jnp.where(place.z == k, slots[k], 0.0) for k in range(LEVELS))
    return jnp.stack([tower0, tower1])


def column_blocks(right, narrow):
    return right.reshape(right.shape[0], narrow, -1)


def grad_blocks(left, right, narrow):
    out = inner_rows(left, right)
    return out.reshape(out.shape[0], narrow, -1)


def masked_scores(query_heads, key_heads, segment):
    scores = jnp.einsum(
        "qhd,khd->hqk", query_heads, key_heads, preferred_element_type=F32
    ) * HEAD_DIM ** (-0.5)
    same_seg = segment[:, None] == segment[None, :]
    return jnp.where(same_seg[None], scores, MASKED)


def attend(query, key, value, segment):
    scores = masked_scores(split_heads(query), split_heads(key), segment)
    row_max = jnp.max(scores, axis=-1, keepdims=True)
    shifted = jnp.exp(scores - row_max)
    row_total = jnp.sum(shifted, axis=-1, keepdims=True)
    row_probs = (shifted / row_total).astype(BF)
    context = jnp.einsum("hqk,khd->qhd", row_probs, split_heads(value), preferred_element_type=F32)
    log_sum = (row_max + jnp.log(row_total))[:, :, 0]
    return context.reshape(query.shape).astype(BF), log_sum


def attend_back(query, key, value, segment, log_sum, grad):
    q, k, v, g = split_heads(query), split_heads(key), split_heads(value), split_heads(grad)
    row_probs = jnp.exp(masked_scores(q, k, segment) - log_sum[:, :, None])
    grad_probs = jnp.einsum("qhd,khd->hqk", g, v, preferred_element_type=F32)
    row_delta = jnp.sum(row_probs * grad_probs, axis=-1, keepdims=True)
    grad_scores = (row_probs * (grad_probs - row_delta)).astype(BF)
    scale = HEAD_DIM ** (-0.5)
    grad_q = jnp.einsum("hqk,khd->qhd", grad_scores, k, preferred_element_type=F32) * scale
    grad_k = jnp.einsum("hqk,qhd->khd", grad_scores, q, preferred_element_type=F32) * scale
    grad_v = jnp.einsum("hqk,qhd->khd", row_probs.astype(BF), g, preferred_element_type=F32)
    shape = query.shape
    return (
        grad_q.reshape(shape).astype(BF),
        grad_k.reshape(shape).astype(BF),
        grad_v.reshape(shape).astype(BF),
    )


def row_of(z, y, n, s):
    own = (z * s + y) * 3 + n
    spare = y * 3 + (z - 1)
    return jnp.where(z == 0, n * s + y, jnp.where(n < 3, own, spare))


def body(
    passages,
    queries,
    passage_cot,
    query_cot,
    passage_lengths,
    query_lengths,
    labels,
    w_qkv,
    w_out,
    w_in,
    w_back,
    biases,
    norm_gains,
    in_bias,
):
    place = Place()
    s, narrow, devices = place.stride, place.narrow, place.wide * place.narrow
    model_width = passages.shape[2]
    length = passages.shape[1] * narrow
    segs, qsegs = passage_lengths.shape[1] - 1, query_lengths.shape[1] - 1
    on_query = place.z == 0

    piece = model_width // devices
    small = jnp.concatenate(
        [biases.reshape(2, -1), norm_gains.reshape(2, -1), in_bias.reshape(2, -1)], axis=1
    )
    whole = jnp.concatenate(
        [passage_lengths.reshape(-1), query_lengths.reshape(-1), labels.reshape(-1)]
    )
    whole = jnp.concatenate([whole // 32, whole % 32]).astype(BF)
    to_query = (jnp.arange(devices) < s * narrow)[:, None]
    small = jnp.where(to_query, small[1][None], small[0][None])
    small = jnp.concatenate(
        [small, jnp.broadcast_to(whole[None], (devices, whole.shape[0]))], axis=1
    )
    small_count = small.shape[1] - whole.shape[0]
    small = lax.all_to_all(small, BOTH, 0, 0, tiled=True)

    inputs = to_rows(place, passages, queries)
    (w_qkv_all,) = gather_tower(place, w_qkv, (w_qkv.shape[2],))
    out_in = jnp.concatenate([w_out, w_in], axis=2)
    w_out_all, w_in_all = gather_tower(place, out_in, (w_out.shape[2], w_in.shape[2]))
    (w_back_all,) = gather_tower(place, w_back, (w_back.shape[2],))
    cot = to_rows(place, passage_cot, query_cot)

    params, ints = small[:, :small_count].astype(F32), small[:, small_count:].astype(F32)
    n_bias, n_gain = biases.shape[1], norm_gains.shape[1]

    def unpack(part, count):
        return part.reshape(devices, count, -1).transpose(1, 0, 2).reshape(count, -1)

    tower_bias = unpack(params[:, : n_bias * piece], n_bias)
    tower_gain = unpack(params[:, n_bias * piece : (n_bias + n_gain) * piece], n_gain)
    tower_in_bias = unpack(params[:, (n_bias + n_gain) * piece :], 1)
    half = ints.shape[1] // 2
    ints = (ints[::narrow, :half] * 32 + ints[::narrow, half:]).astype(jnp.int32)
    n_pass = passage_lengths.size
    n_query = query_lengths.size
    pass_lens = ints[:, :n_pass].reshape(-1, segs + 1)
    query_lens = ints[:, n_pass : n_pass + n_query].reshape(-1, qsegs + 1)
    label_all = ints[:, n_pass + n_query :].reshape(-1, qsegs)
    my_row = row_of(place.z, place.y, place.n, s)
    pass_row = pick(pass_lens, jnp.where(on_query, 0, my_row), 0)
    query_row = pick(query_lens, jnp.where(on_query, my_row, 0), 0)
    ends_p = jnp.cumsum(pass_row)[:-1]
    ends_q = jnp.cumsum(query_row)[:-1]
    ends_p = jnp.concatenate([ends_p, jnp.full((qsegs - segs,), length + 1, jnp.int32)])
    starts_p = jnp.concatenate([jnp.zeros((1,), jnp.int32), ends_p[:-1]])
    starts_p = jnp.where(jnp.arange(qsegs) < segs, starts_p, length + 1)
    starts_q = jnp.concatenate([jnp.zeros((1,), jnp.int32), ends_q[:-1]])
    ends = jnp.where(on_query, ends_q, ends_p)
    starts = jnp.where(on_query, starts_q, starts_p)
    seg_count = jnp.where(on_query, qsegs, segs)
    position = jnp.arange(length, dtype=jnp.int32)
    segment = jnp.sum((position[:, None] >= ends[None, :]).astype(jnp.int32), axis=1)
    valid = (segment < seg_count).astype(F32)[:, None]
    first_hot = starts[:, None] == position[None, :]

    projected = matmul(inputs, w_qkv_all)
    query = (projected[:, :model_width] + tower_bias[0]).astype(BF)
    key = projected[:, model_width : 2 * model_width].astype(BF)
    value = (projected[:, 2 * model_width :] + tower_bias[1]).astype(BF)
    context, log_sum = attend(query, key, value, segment)
    branch = matmul(context, w_out_all) + tower_bias[2]
    residual = inputs.astype(F32) + branch
    normed = layer_norm(residual, tower_gain[0], tower_bias[3])
    normed_low = normed.astype(BF)
    hidden_pre = matmul(normed_low, w_in_all) + tower_in_bias[0]
    active = gelu_exact(hidden_pre).astype(BF)
    ffn_out = matmul(active, w_back_all) + tower_bias[4]
    residual_two = normed + ffn_out
    output_low = layer_norm(residual_two, tower_gain[1], tower_bias[5]).astype(BF)
    stats = jnp.stack(
        [
            jnp.sum(valid * residual * residual),
            jnp.sum(valid * branch * branch),
            jnp.sum(valid * residual_two * residual_two),
            jnp.sum(valid * ffn_out * ffn_out),
            jnp.sum(valid),
        ]
    )
    passage_out, query_out = from_rows(place, output_low)

    pooled = matmul(first_hot.astype(BF), output_low).astype(BF)
    seen = [pooled]
    for k in range(1, LEVELS):
        seen.append(flip(pooled, "wide", k * s))
    column = []
    for level in range(LEVELS):
        rows = qsegs if level == 0 else segs
        part = jnp.zeros((rows, model_width), BF)
        for k in range(LEVELS):
            part = jnp.where((place.z ^ k) == level, seen[k][:rows], part)
        column.append(part)
    columns = jnp.concatenate(column)[None]
    masks = [0]
    for axis, step, mask in (
        [("wide", b, b * narrow) for b in bits_of(s)]
        + [("narrow", b, b) for b in reversed(bits_of(narrow))]
    ):
        columns = jnp.concatenate([columns, flip(columns, axis, step)])
        masks = masks + [m ^ mask for m in masks]
    here = place.y * narrow + place.n
    there = here ^ jnp.array(masks, jnp.int32)
    their_y, their_n = there // narrow, there % narrow
    every_query = columns[:, :qsegs].reshape(-1, model_width)
    every_pass = columns[:, qsegs:].reshape(-1, model_width)
    label_rows = label_all[row_of(jnp.int32(0), their_y, their_n, s)].reshape(-1)
    levels = jnp.arange(1, LEVELS)
    pass_rows = row_of(levels[None, :], their_y[:, None], their_n[:, None], s)
    pass_ids = (pass_rows[:, :, None] * segs + jnp.arange(segs)).reshape(-1)
    match = inner_cols(every_query, every_pass) / SCORE_DIV
    match_max = jnp.max(match, axis=1, keepdims=True)
    match_exp = jnp.exp(match - match_max)
    match_probs = match_exp / jnp.sum(match_exp, axis=1, keepdims=True)
    label_hot = (label_rows[:, None] == pass_ids[None, :]).astype(F32)
    grad_match = ((match_probs - label_hot) / SCORE_DIV).astype(BF)
    grad_query_pool = matmul(grad_match[:qsegs], every_pass)
    my_cols = lax.dynamic_slice_in_dim(
        grad_match, jnp.maximum(place.z - 1, 0) * segs, segs, axis=1
    )
    grad_pass_pool = inner_rows(my_cols, every_query)
    grad_pool = jnp.where(
        on_query,
        grad_query_pool,
        jnp.concatenate([grad_pass_pool, jnp.zeros((qsegs - segs, model_width), F32)]),
    )

    grad_output = cot.astype(F32) * valid
    grad_output = grad_output + lax.dot_general(
        first_hot.astype(F32),
        grad_pool,
        (((0,), (0,)), ((), ())),
        precision=lax.Precision.HIGHEST,
    )
    norm_two_back = jax.vjp(layer_norm, residual_two, tower_gain[1], tower_bias[5])[1]
    grad_resid_two, grad_gain_two, grad_shift_two = norm_two_back(grad_output)
    grad_ffn = grad_resid_two.astype(BF)
    grad_ffn_bias = jnp.sum(grad_ffn.astype(F32), axis=0)
    grad_w_back = scatter_tower(place, grad_blocks(active, grad_ffn, narrow))
    grad_active = inner_cols(grad_ffn, w_back_all)
    gelu_back = jax.vjp(gelu_exact, hidden_pre)[1]
    grad_hidden = gelu_back(grad_active)[0].astype(BF)
    grad_in_bias = jnp.sum(grad_hidden.astype(F32), axis=0)
    grad_normed = grad_resid_two + inner_cols(grad_hidden, w_in_all)
    norm_one_back = jax.vjp(layer_norm, residual, tower_gain[0], tower_bias[3])[1]
    grad_residual, grad_gain_one, grad_shift_one = norm_one_back(grad_normed)
    grad_branch = grad_residual.astype(BF)
    grad_out_bias = jnp.sum(grad_branch.astype(F32), axis=0)
    grad_out_in = scatter_tower(
        place,
        jnp.concatenate(
            [
                grad_blocks(context, grad_branch, narrow),
                grad_blocks(normed_low, grad_hidden, narrow),
            ],
            axis=2,
        ),
    )
    grad_context = inner_cols(grad_branch, w_out_all).astype(BF)
    grad_q, grad_k, grad_v = attend_back(query, key, value, segment, log_sum, grad_context)
    grad_qkv = jnp.concatenate([grad_q, grad_k, grad_v], axis=-1)
    grad_w_qkv = scatter_tower(place, grad_blocks(inputs, grad_qkv, narrow))
    input_grad = (grad_residual + inner_cols(grad_qkv, w_qkv_all)).astype(BF)
    passage_grad, query_grad = from_rows(place, input_grad)
    out_cols = w_out.shape[2] // narrow
    grad_w_out, grad_w_in = grad_out_in[:, :, :out_cols], grad_out_in[:, :, out_cols:]

    def share(rows):
        count = rows.shape[0]
        return rows.reshape(count, devices, -1).transpose(1, 0, 2).reshape(devices, -1)

    bias_rows = jnp.stack(
        [
            jnp.sum(grad_q.astype(F32), axis=0),
            jnp.sum(grad_v.astype(F32), axis=0),
            grad_out_bias,
            grad_shift_one,
            grad_ffn_bias,
            grad_shift_two,
            grad_gain_one,
            grad_gain_two,
        ]
    )
    shares = jnp.concatenate(
        [
            share(bias_rows),
            share(grad_in_bias[None]),
            jnp.broadcast_to(stats[None], (devices, stats.shape[0])),
        ],
        axis=1,
    )
    shares = lax.all_to_all(shares, BOTH, 0, 0, tiled=True)
    shares = shares.reshape(LEVELS, -1, shares.shape[1]).sum(axis=1)
    shares = jnp.stack([shares[1] + shares[2] + shares[3], shares[0]])
    grad_biases = shares[:, : n_bias * piece].reshape(2, n_bias, piece)
    grad_gains = shares[:, n_bias * piece : (n_bias + n_gain) * piece].reshape(2, n_gain, piece)
    grad_inb = shares[:, (n_bias + n_gain) * piece : -stats.shape[0]]
    totals = shares[:, -stats.shape[0] :]
    rms_stats = jnp.sqrt(totals[:, :4] / (totals[:, 4:] * model_width))
    return (
        passage_out,
        query_out,
        passage_grad,
        query_grad,
        grad_w_qkv,
        grad_w_out,
        grad_w_in,
        grad_w_back,
        grad_biases,
        grad_gains,
        grad_inb,
        rms_stats,
    )


def solution(mesh):
    return jax.shard_map(
        body,
        mesh=mesh,
        in_specs=(
            P("wide", "narrow", None),
            P("wide", "narrow", None),
            P("wide", "narrow", None),
            P("wide", "narrow", None),
            P("wide", None),
            P("wide", None),
            P("wide"),
            P(None, ("wide", "narrow"), None),
            P(None, ("wide", "narrow"), None),
            P(None, ("wide", "narrow"), None),
            P(None, ("wide", "narrow"), None),
            P(None, None, ("wide", "narrow")),
            P(None, None, ("wide", "narrow")),
            P(None, ("wide", "narrow")),
        ),
        out_specs=(
            P("wide", "narrow", None),
            P("wide", "narrow", None),
            P("wide", "narrow", None),
            P("wide", "narrow", None),
            P(None, "wide", "narrow"),
            P(None, "wide", "narrow"),
            P(None, "wide", "narrow"),
            P(None, "wide", "narrow"),
            P(None, None, ("wide", "narrow")),
            P(None, None, ("wide", "narrow")),
            P(None, ("wide", "narrow")),
            P(),
        ),
        check_vma=False,
    )
```

time: 1410 us -> 527 us (0.37)
  waiting for transfers between devices: 706 us -> 84.3 us
  blocking collectives: 306 us -> 0 us
  starting transfers between devices: 20.7 us -> 132 us
  matrix products: 160 us -> 109 us
  local copies, waits for them, and re-layouts: 114 us -> 91.5 us
  other arithmetic: 78.5 us -> 97.8 us
    reduce_scatter x6 -> x0, waiting for transfers between devices: 287 us -> none  [the longest x1 71.9 us: body(): lax.psum_scatter(partials[6], 'wide', scatter_dimension=0, tiled=True)]
    unnamed x25 -> x0, waiting for transfers between devices: 260 us -> none
    all_gather x9 -> x0, blocking collectives: 210 us -> none  [the longest x1 44.8 us: body(): lax.all_gather(biases, ('wide', 'narrow'), axis=2, tiled=True)]
    all_gather x13 -> x0, waiting for transfers between devices: 158 us -> none  [the longest x1 75.2 us: body(): lax.all_gather(w_back, ('wide', 'narrow'), axis=1, tiled=True)]
    ppermute x0 -> x78, starting transfers between devices: none -> 105 us  [the longest x66 72.7 us: flip(): return lax.ppermute(x, axis, [(i, i ^ mask) for i in range(size)])]
    all_to_all x4 -> x0, blocking collectives: 81.8 us -> none  [the longest x1 37.4 us: body(): lax.all_to_all(grad_hidden_list[0], 'narrow', split_axis=1, concat_axis=0...]
    ppermute x0 -> x78, waiting for transfers between devices: none -> 74.2 us  [the longest x66 60 us: flip(): return lax.ppermute(x, axis, [(i, i ^ mask) for i in range(size)])]
    dynamic_slice x40 -> x2, local copies, waits for them, and re-layouts: 34.2 us -> 4.09 us  [pick(): return lax.dynamic_index_in_dim(x, index, dim, keepdims=False)]
  transfers between devices with their start and end apart: 27 -> 84, of which waited for: 13 -> 25; matrix products, arithmetic and copies ran while one was open for 24% -> 40% of each run, Pallas kernels for 0% -> 1%
where the time goes in v1:
time: 527 us; the launch traced here: 521 us
  starting transfers between devices  132 us (25%)
  matrix products  109 us (21%)
  other arithmetic  97.8 us (19%)
  local copies, waits for them, and re-layouts  91.5 us (17%)
  waiting for transfers between devices  84.3 us (16%)
    ppermute x66, starting transfers between devices, flip(): return lax.ppermute(x, axis, [(i, i ^ mask) for i in range(size)])  72.7 us
    ppermute x66, waiting for transfers between devices, flip(): return lax.ppermute(x, axis, [(i, i ^ mask) for i in range(size)])  60 us
    ppermute x12, starting transfers between devices, swap_levels(): return lax.ppermute(x, 'wide', pairs)  31.8 us
    dot_general x6, matrix products, matmul(): return jnp.dot(left, right, preferred_element_type=F32)  30.5 us
    slice x8, local copies, waits for them, and re-layouts, scatter_tower(): first, second = (x[:2], x[2:])  22.2 us
    convert_element_type x14, local copies, waits for them, and re-layouts, halve(): got = flip(pick(x, 1 - bit, dim).astype(BF), axis, mask)  21.5 us
    dot_general x5, matrix products, inner_cols(): lax.dot_general(left, right, (((1,), (1,)), ((), ())), preferred_element_...  21.2 us
    add x13, other arithmetic, halve(): return pick(x, bit, dim) + got.astype(F32)  19.9 us
  transfers between devices with their start and end apart: 84, of which 25 were waited for; matrix products, arithmetic and copies ran while one was open for 40% of the time, Pallas kernels for 1%

profile of v1, /device:TPU:0, one launch (start us, length us, event | category | flops | bytes accessed | tf_op | source)
XLA Modules:
  0.0 521.3 jit_solution(16494848768986978251)
XLA Ops:
  6.7 7.3 %all-to-all-start.1 = ((bf16[32,2,192]{2,1,0:T(2,128)(2,1)}), bf16[32,2,192]{2,1,0:T(2,128)(2,1)S(1)}, u32[]{:S(2)}, u32[]{:S(2)}) async-start(bf16[32,2,192]{2,1,0:T(2,128)(2,1)} %reshape.702), calls=%async_computation.1 | async-start | bytes 65536 | tf_op jit(solution)/shard_map/all_to_all | solution.py:295
  41.3 3.1 collective-permute-done.8
  47.3 8.4 %collective-permute-start.27 = (bf16[96,768]{1,0:T(8,128)(2,1)S(1)}, bf16[96,768]{1,0:T(8,128)(2,1)S(1)}, u32[]{:S(2)}, u32[]{:S(2)}) collective-permute-start(bf16[96,768]{1,0:T(8,128)(2,1)S(1)} %get-tuple-element.189), channel_id=1, source_target_pairs={{0,8},{4,12},{8,0},{12,4},{16,24},{20,28},{24,16},{28,20},{1,9},{5... | collective-permute-start | bytes 442376 | tf_op jit(solution)/shard_map/ppermute | solution.py:49
  56.5 6.7 %collective-permute-start.1 = (bf16[128,768]{1,0:T(8,128)(2,1)}, bf16[128,768]{1,0:T(8,128)(2,1)S(1)}, u32[]{:S(2)}, u32[]{:S(2)}) collective-permute-start(bf16[128,768]{1,0:T(8,128)(2,1)} %get-tuple-element.171), channel_id=1, source_target_pairs={{0,16},{16,0},{4,20},{20,4},{1,17},{17,1},{5,21},{21,5},{2,18},{18... | collective-permute-start | bytes 589832 | tf_op jit(solution)/shard_map/ppermute | solution.py:56
  80.7 4.5 all-to-all-start
  98.9 6.3 %collective-permute-done.23.refs_6_ = bf16[2,24,3840]{2,1,0:T(8,128)(2,1)S(1)} collective-permute-done((bf16[2,24,3840]{2,1,0:T(8,128)(2,1)S(1)}, bf16[2,24,3840]{2,1,0:T(8,128)(2,1)S(1)}, u32[]{:S(2)}, u32[]{:S(2)}) %collective-permute-start.23) | collective-permute-done | bytes 368672 | tf_op jit(solution)/shard_map/ppermute | solution.py:49
  105.2 3.1 collective-permute-done.13.refs_8_
  108.3 5.9 %collective-permute-done.6.refs_2_ = bf16[4,24,2304]{2,1,0:T(8,128)(2,1)S(1)} collective-permute-done((bf16[4,24,2304]{2,1,0:T(8,128)(2,1)S(1)}, bf16[4,24,2304]{2,1,0:T(8,128)(2,1)S(1)}, u32[]{:S(2)}, u32[]{:S(2)}) %collective-permute-start.6) | collective-permute-done | bytes 442400 | tf_op jit(solution)/shard_map/ppermute | solution.py:49
  120.7 3.7 fusion.149
  128.1 6.6 %fusion.17 = (f32[12,512]{1,0:T(8,128)S(1)}, f32[12,512,512]{1,2,0:T(8,128)}) fusion(pred[512,512]{0,1:T(8,128)(4,1)S(1)} %copy-done.27, bf16[512,12,64]{0,2,1:T(8,128)(2,1)S(1)} %bitcast.379, bf16[512,12,64]{0,2,1:T(8,128)(2,1)S(1)} %bitcast.372), kind=kOutput, calls=%fused_computation.41 | convolution fusion | flops 412084224 | bytes 14442496 | tf_op jit(solution)/shard_map/qhd,khd->hqk/dot_general | solution.py:216
  137.4 7.2 %fusion = f32[12,512]{1,0:T(8,128)S(1)} fusion(f32[12,512]{1,0:T(8,128)S(1)} %get-tuple-element.206, f32[12,512,512]{1,2,0:T(8,128)} %get-tuple-element.207, pred[512,512]{0,1:T(8,128)(4,1)S(1)} %copy-done.27), kind=kLoop, calls=%fused_computation.11 | loop fusion | flops 12576768 | bytes 12894208 | tf_op jit(solution)/shard_map/reduce_sum | solution.py:227
  144.8 8.8 %collective-permute-done.25.refs_8_ = bf16[4,24,3840]{2,1,0:T(8,128)(2,1)S(1)} collective-permute-done((bf16[4,24,3840]{2,1,0:T(8,128)(2,1)S(1)}, bf16[4,24,3840]{2,1,0:T(8,128)(2,1)S(1)}, u32[]{:S(2)}, u32[]{:S(2)}) %collective-permute-start.25) | collective-permute-done | bytes 737312 | tf_op jit(solution)/shard_map/ppermute | solution.py:49
  154.6 7.1 %fusion.31 = bf16[12,64,512]{2,1,0:T(8,128)(2,1)S(1)} fusion(bf16[512,12,64]{0,2,1:T(8,128)(2,1)S(1)} %bitcast.392, f32[12,512]{1,0:T(8,128)S(1)} %fusion, f32[12,512]{1,0:T(8,128)S(1)} %get-tuple-element.206, f32[12,512,512]{1,2,0:T(8,128)} %get-tuple-element.207, pred[512,512]{0,1:T(8,128)(4,1)S(1)} %copy-done.27), kind=kOutput, calls=%fused_computation.116 | convolution fusion | flops 418775040 | bytes 14467072 | tf_op jit(solution)/shard_map/hqk,khd->qhd/dot_general | solution.py:229
  172.0 18.4 %multiply_convert_fusion.1 = (bf16[512,3072]{1,0:T(8,128)(2,1)S(1)}, f32[512,3072]{1,0:T(8,128)}, f32[512,3072]{1,0:T(8,128)}) fusion(f32[3072]{0:T(1024)S(1)} %copy-done.76, bf16[768,3072]{1,0:T(8,128)(2,1)S(1)} %bitcast.362, f32[512,768]{1,0:T(8,128)S(1)} %get-tuple-element.138, f32[768]{0:T(1024)S(1)} %copy-done.81, f32[768]{0:T(1024)S(1)} %copy-done.74, ...), kind=kOutput, calls=%fused_computation.19 | convolution fusion | flops 2521694208 | bytes 22042624 | tf_op jit(solution)/shard_map/dot_general | solution.py:21
  190.4 3.7 fusion.24
  196.1 4.3 collective-permute-start.46
  215.1 4.4 all-to-all-start.3
  231.2 3.7 multiply_reduce_fusion.1
  235.8 9.4 %convert_reduce_fusion = (f32[3072]{0:T(1024)}, bf16[512,3072]{1,0:T(8,128)(2,1)}) fusion(f32[512,3072]{1,0:T(8,128)} %get-tuple-element.136, f32[512,3072]{1,0:T(8,128)} %get-tuple-element.209, f32[3072]{0:T(1024)S(1)} %copy-done.77, bf16[512,768]{1,0:T(8,128)(2,1)S(1)} %get-tuple-element.115, bf16[3072,768]{1,0:T(8,128)(2,1)S(1)} %bitcast.357), kind=kOutput, calls=%fused_computation.16 | convolution fusion | flops 2442654720 | bytes 21258240 | tf_op jit(solution)/shard_map/dot_general | solution.py:29
  245.3 5.9 %multiply_reduce_fusion.2 = (f32[768]{0:T(1024)}, f32[512]{0:T(512)S(1)}, f32[]{:T(128)}, f32[768]{0:T(1024)S(1)}, f32[512,768]{1,0:T(8,128)S(1)}) fusion(f32[512,768]{1,0:T(8,128)S(1)} %copy-done.16, f32[512]{0:T(512)S(1)} %copy-done.80, f32[512]{0:T(512)S(1)} %copy-done.63, f32[768]{0:T(1024)S(1)} %copy-done.75, f32[512]{0:T(512)S(1)} %copy-done.89, ...), kind=kOutput, calls=%fused_computation.85 | convolution fusion | flops 2421028864 | bytes 12602372 | tf_op jit(solution)/shard_map/dot_general | solution.py:29
  251.2 5.4 %fusion.131 = f32[768,3072]{0,1:T(8,128)} fusion(bf16[512,3072]{1,0:T(8,128)(2,1)S(1)} %copy-done.94, f32[512,768]{1,0:T(8,128)S(1)} %copy-done.16, f32[768]{0:T(1024)S(1)} %copy-done.82, f32[768]{0:T(1024)S(1)} %copy-done.75, f32[512]{0:T(512)S(1)} %copy-done.80, f32[512]{0:T(512)S(1)} %copy-done.63), kind=kOutput, calls=%fused_computation.410 | convolution fusion | flops 2417885184 | bytes 14166016 | tf_op jit(solution)/shard_map/concatenate | solution.py:430
  256.6 5.2 fusion.152
  266.8 6.6 %convert_reduce_fusion.3 = (f32[12,64]{1,0:T(8,128)S(1)}, bf16[12,64,512]{2,1,0:T(8,128)(2,1)S(1)}) fusion(bf16[512,12,64]{0,2,1:T(8,128)(2,1)S(1)} %bitcast.394, f32[12,512]{1,0:T(8,128)} %log_add_fusion, f32[12,512,512]{1,2,0:T(8,128)} %get-tuple-element.207, pred[512,512]{0,1:T(8,128)(4,1)S(1)} %copy-done.27), kind=kOutput, calls=%fused_computation.88 | convolution fusion | flops 416414976 | bytes 14445568 | tf_op jit(solution)/shard_map/hqk,qhd->khd/dot_general | solution.py:243
  273.4 9.6 %multiply_reduce_fusion = (f32[12,512]{1,0:T(8,128)S(1)}, f32[12,512,512]{1,2,0:T(8,128)}) fusion(f32[12,512]{1,0:T(8,128)S(1)} %copy-done.52, f32[12,512,512]{1,2,0:T(8,128)} %get-tuple-element.207, pred[512,512]{0,1:T(8,128)(4,1)S(1)} %copy-done.27, bf16[512,12,64]{0,2,1:T(8,128)(2,1)S(1)} %bitcast.395, bf16[512,12,64]{0,2,1:T(8,128)(2,1)S(1)} %bitcast.393), kind=kOutput, calls=%fused_computation.4 | convolution fusion | flops 418375680 | bytes 27049984 | tf_op jit(solution)/shard_map/qhd,khd->hqk/dot_general | solution.py:237
  283.1 7.5 %multiply_convert_fusion = bf16[12,512,512]{1,2,0:T(8,128)(2,1)S(1)} fusion(f32[12,512,512]{1,2,0:T(8,128)} %get-tuple-element.215, f32[12,512]{1,0:T(8,128)S(1)} %get-tuple-element.214, f32[12,512]{1,0:T(8,128)S(1)} %copy-done.52, f32[12,512,512]{1,2,0:T(8,128)S(1)} %bitcast.367, pred[512,512]{0,1:T(8,128)(4,1)S(1)} %copy-done.27), kind=kLoop, calls=%fused_computation.3 | loop fusion | flops 18874368 | bytes 31768576 | tf_op jit(solution)/shard_map/convert_element_type | solution.py:239
  294.6 3.0 add_convert_fusion.1
  303.2 4.2 fusion.18
  307.4 4.1 fusion.19
  311.8 3.3 stack.228
  316.0 4.5 all-to-all-start.5
  320.5 6.8 %fusion.150 = f32[768,2,2,576]{0,3,2,1:T(8,128)} fusion(bf16[512,768,1,1]{1,0,3,2:T(8,128)(2,1)} %bitcast.83, bf16[2,2,576,512]{3,2,1,0:T(8,128)(2,1)} %bitcast.378), kind=kOutput, calls=%fused_computation.425 | convolution fusion | flops 1811939328 | bytes 10223616 | tf_op jit(solution)/shard_map/dot_general | solution.py:25
  327.3 3.4 fusion.20
  331.0 3.5 all-to-all-start.2
  336.1 10.0 %all-to-all-done.2 = bf16[4,128,768]{2,1,0:T(8,128)(2,1)S(1)} async-done(((bf16[4,128,768]{2,1,0:T(8,128)(2,1)}), bf16[4,128,768]{2,1,0:T(8,128)(2,1)S(1)}, u32[]{:S(2)}, u32[]{:S(2)}) %all-to-all-start.2) | async-done | bytes 786464 | tf_op jit(solution)/shard_map/all_to_all | solution.py:93
  347.0 3.5 all-to-all-start.4
  352.1 5.4 %collective-permute-start.41 = (bf16[128,768]{1,0:T(8,128)(2,1)}, bf16[128,768]{1,0:T(8,128)(2,1)S(1)}, u32[]{:S(2)}, u32[]{:S(2)}) collective-permute-start(bf16[128,768]{1,0:T(8,128)(2,1)} %slice_bitcast_fusion.6), channel_id=1, source_target_pairs={{0,24},{24,0},{4,28},{28,4},{1,25},{25,1},{5,29},{29,5},{2,26},{26... | collective-permute-start | bytes 589832 | tf_op jit(solution)/shard_map/ppermute | solution.py:56
  364.8 8.0 %collective-permute-done.39 = bf16[128,768]{1,0:T(8,128)(2,1)} collective-permute-done((bf16[128,768]{1,0:T(8,128)(2,1)}, bf16[128,768]{1,0:T(8,128)(2,1)}, u32[]{:S(2)}, u32[]{:S(2)}) %collective-permute-start.39) | collective-permute-done | bytes 196640 | tf_op jit(solution)/shard_map/ppermute | solution.py:56
  384.1 2.9 bitcast_add_fusion.1
  388.9 3.0 copy.288
  410.5 5.9 %collective-permute-done.57 = bf16[2,1,96,2,576]{4,2,0,3,1:T(8,128)(2,1)S(1)} collective-permute-done((bf16[2,1,96,2,576]{4,2,0,3,1:T(8,128)(2,1)S(1)}, bf16[2,1,96,2,576]{4,2,0,3,1:T(8,128)(2,1)S(1)}, u32[]{:S(2)}, u32[]{:S(2)}) %collective-permute-start.57) | collective-permute-done | bytes 442400 | tf_op jit(solution)/shard_map/ppermute | solution.py:49
  418.6 3.7 bitcast_add_fusion
  424.8 3.9 slice.358
  431.9 4.0 reshape.678
  459.4 4.3 collective-permute-done.73
  470.9 3.5 copy.294
  487.6 3.4 fusion.71
  492.3 3.3 collective-permute-start.77
  500.5 4.4 collective-permute-done.64
  (595 shorter events, 253.3 us)
Async XLA Ops:
  6.7 23.7 %all-to-all-start.1 = ((bf16[32,2,192]{2,1,0:T(2,128)(2,1)}), bf16[32,2,192]{2,1,0:T(2,128)(2,1)S(1)}, u32[]{:S(2)}, u32[]{:S(2)}) async-start(bf16[32,2,192]{2,1,0:T(2,128)(2,1)} %reshape.702), calls=%async_computation.1 | async-start | bytes 65536 | tf_op jit(solution)/shard_map/all_to_all | solution.py:295
  16.8 49.8 %collective-permute-start.20 = (bf16[24,3840]{1,0:T(8,128)(2,1)}, bf16[24,3840]{1,0:T(8,128)(2,1)S(1)}, u32[]{:S(2)}, u32[]{:S(2)}) collective-permute-start(bf16[24,3840]{1,0:T(8,128)(2,1)} %get-tuple-element.182), channel_id=1, source_target_pairs={{0,16},{4,20},{8,24},{12,28},{16,0},{20,4},{24,8},{28,12},{1,17},{... | collective-permute-start | bytes 552968 | tf_op jit(solution)/shard_map/ppermute | solution.py:49
  19.5 49.0 %collective-permute-start.21 = (bf16[24,3840]{1,0:T(8,128)(2,1)}, bf16[24,3840]{1,0:T(8,128)(2,1)S(1)}, u32[]{:S(2)}, u32[]{:S(2)}) collective-permute-start(bf16[24,3840]{1,0:T(8,128)(2,1)} %get-tuple-element.183), channel_id=1, source_target_pairs={{0,24},{4,28},{8,16},{12,20},{16,8},{20,12},{24,0},{28,4},{1,25},{... | collective-permute-start | bytes 552968 | tf_op jit(solution)/shard_map/ppermute | solution.py:49
  22.6 21.8 %collective-permute-start.8 = (bf16[24,2304]{1,0:T(8,128)(2,1)}, bf16[24,2304]{1,0:T(8,128)(2,1)S(1)}, u32[]{:S(2)}, u32[]{:S(2)}) collective-permute-start(bf16[24,2304]{1,0:T(8,128)(2,1)} %get-tuple-element.190), channel_id=1, source_target_pairs={{0,16},{4,20},{8,24},{12,28},{16,0},{20,4},{24,8},{28,12},{1,17},{... | collective-permute-start | bytes 331784 | tf_op jit(solution)/shard_map/ppermute | solution.py:49
  24.1 20.3 %collective-permute-start.9 = (bf16[24,2304]{1,0:T(8,128)(2,1)}, bf16[24,2304]{1,0:T(8,128)(2,1)S(1)}, u32[]{:S(2)}, u32[]{:S(2)}) collective-permute-start(bf16[24,2304]{1,0:T(8,128)(2,1)} %get-tuple-element.191), channel_id=1, source_target_pairs={{0,24},{4,28},{8,16},{12,20},{16,8},{20,12},{24,0},{28,4},{1,25},{... | collective-permute-start | bytes 331784 | tf_op jit(solution)/shard_map/ppermute | solution.py:49
  25.0 22.3 %collective-permute-start.3 = (bf16[24,2304]{1,0:T(8,128)(2,1)S(1)}, bf16[24,2304]{1,0:T(8,128)(2,1)S(1)}, u32[]{:S(2)}, u32[]{:S(2)}) collective-permute-start(bf16[24,2304]{1,0:T(8,128)(2,1)S(1)} %get-tuple-element.193), channel_id=1, source_target_pairs={{0,8},{4,12},{8,0},{12,4},{16,24},{20,28},{24,16},{28,20},{1,9},{5... | collective-permute-start | bytes 331784 | tf_op jit(solution)/shard_map/ppermute | solution.py:49
  47.3 16.6 %collective-permute-start.27 = (bf16[96,768]{1,0:T(8,128)(2,1)S(1)}, bf16[96,768]{1,0:T(8,128)(2,1)S(1)}, u32[]{:S(2)}, u32[]{:S(2)}) collective-permute-start(bf16[96,768]{1,0:T(8,128)(2,1)S(1)} %get-tuple-element.189), channel_id=1, source_target_pairs={{0,8},{4,12},{8,0},{12,4},{16,24},{20,28},{24,16},{28,20},{1,9},{5... | collective-permute-start | bytes 442376 | tf_op jit(solution)/shard_map/ppermute | solution.py:49
  56.5 14.5 %collective-permute-start.1 = (bf16[128,768]{1,0:T(8,128)(2,1)}, bf16[128,768]{1,0:T(8,128)(2,1)S(1)}, u32[]{:S(2)}, u32[]{:S(2)}) collective-permute-start(bf16[128,768]{1,0:T(8,128)(2,1)} %get-tuple-element.171), channel_id=1, source_target_pairs={{0,16},{16,0},{4,20},{20,4},{1,17},{17,1},{5,21},{21,5},{2,18},{18... | collective-permute-start | bytes 589832 | tf_op jit(solution)/shard_map/ppermute | solution.py:56
  68.5 19.3 %collective-permute-start.11 = (bf16[2,24,2304]{2,1,0:T(8,128)(2,1)S(1)}, bf16[2,24,2304]{2,1,0:T(8,128)(2,1)S(1)}, u32[]{:S(2)}, u32[]{:S(2)}) collective-permute-start(bf16[2,24,2304]{2,1,0:T(8,128)(2,1)S(1)} %pad_maximum_fusion.18.refs_4_), channel_id=1, source_target_pairs={{0,2},{1,3},{2,0},{3,1},{4,6},{5,7},{6,4},{7,5},{8,10},{9,11},{10,... | collective-permute-start | bytes 663560 | tf_op jit(solution)/shard_map/ppermute | solution.py:49
  70.1 45.0 %collective-permute-start.10 = (bf16[2,24,2304]{2,1,0:T(8,128)(2,1)S(1)}, bf16[2,24,2304]{2,1,0:T(8,128)(2,1)S(1)}, u32[]{:S(2)}, u32[]{:S(2)}) collective-permute-start(bf16[2,24,2304]{2,1,0:T(8,128)(2,1)S(1)} %pad_maximum_fusion.18.refs_4_), channel_id=1, source_target_pairs={{0,1},{1,0},{2,3},{3,2},{4,5},{5,4},{6,7},{7,6},{8,9},{9,8},{10,11... | collective-permute-start | bytes 663560 | tf_op jit(solution)/shard_map/ppermute | solution.py:49
  74.0 15.9 %collective-permute-start.28 = (bf16[2,96,768]{2,1,0:T(8,128)(2,1)}, bf16[2,96,768]{2,1,0:T(8,128)(2,1)}, u32[]{:S(2)}, u32[]{:S(2)}) collective-permute-start(bf16[2,96,768]{2,1,0:T(8,128)(2,1)} %pad_maximum_fusion.15), channel_id=1, source_target_pairs={{0,4},{4,0},{8,12},{12,8},{16,20},{20,16},{24,28},{28,24},{1,5},{5... | collective-permute-start | bytes 884744 | tf_op jit(solution)/shard_map/ppermute | solution.py:49
  80.7 40.0 %all-to-all-start = ((bf16[4,128,768]{2,1,0:T(8,128)(2,1)}), bf16[4,128,768]{2,1,0:T(8,128)(2,1)}, u32[]{:S(2)}, u32[]{:S(2)}) async-start(bf16[4,128,768]{2,1,0:T(8,128)(2,1)} %pad_maximum_fusion.1), calls=%async_computation | async-start | bytes 1572864 | tf_op jit(solution)/shard_map/all_to_all | solution.py:87
  87.8 17.3 %collective-permute-start.23 = (bf16[2,24,3840]{2,1,0:T(8,128)(2,1)S(1)}, bf16[2,24,3840]{2,1,0:T(8,128)(2,1)S(1)}, u32[]{:S(2)}, u32[]{:S(2)}) collective-permute-start(bf16[2,24,3840]{2,1,0:T(8,128)(2,1)S(1)} %pad_maximum_fusion.14.refs_4_), channel_id=1, source_target_pairs={{0,2},{1,3},{2,0},{3,1},{4,6},{5,7},{6,4},{7,5},{8,10},{9,11},{10,... | collective-permute-start | bytes 1105928 | tf_op jit(solution)/shard_map/ppermute | solution.py:49
  90.0 24.2 %collective-permute-start.6 = (bf16[4,24,2304]{2,1,0:T(8,128)(2,1)S(1)}, bf16[4,24,2304]{2,1,0:T(8,128)(2,1)S(1)}, u32[]{:S(2)}, u32[]{:S(2)}) collective-permute-start(bf16[4,24,2304]{2,1,0:T(8,128)(2,1)S(1)} %pad_maximum_fusion.10.refs_0_), channel_id=1, source_target_pairs={{0,2},{1,3},{2,0},{3,1},{4,6},{5,7},{6,4},{7,5},{8,10},{9,11},{10,... | collective-permute-start | bytes 1327112 | tf_op jit(solution)/shard_map/ppermute | solution.py:49
  91.9 24.9 %collective-permute-start.5 = (bf16[4,24,2304]{2,1,0:T(8,128)(2,1)S(1)}, bf16[4,24,2304]{2,1,0:T(8,128)(2,1)S(1)}, u32[]{:S(2)}, u32[]{:S(2)}) collective-permute-start(bf16[4,24,2304]{2,1,0:T(8,128)(2,1)S(1)} %pad_maximum_fusion.10.refs_0_), channel_id=1, source_target_pairs={{0,1},{1,0},{2,3},{3,2},{4,5},{5,4},{6,7},{7,6},{8,9},{9,8},{10,11... | collective-permute-start | bytes 1327112 | tf_op jit(solution)/shard_map/ppermute | solution.py:49
  115.8 19.0 %collective-permute-start.34 = (bf16[2,96,768]{2,1,0:T(8,128)(2,1)}, bf16[2,96,768]{2,1,0:T(8,128)(2,1)}, u32[]{:S(2)}, u32[]{:S(2)}) collective-permute-start(bf16[2,96,768]{2,1,0:T(8,128)(2,1)} %pad_maximum_fusion.16.refs_4_), channel_id=1, source_target_pairs={{0,1},{1,0},{2,3},{3,2},{4,5},{5,4},{6,7},{7,6},{8,9},{9,8},{10,11... | collective-permute-start | bytes 884744 | tf_op jit(solution)/shard_map/ppermute | solution.py:49
  116.3 20.6 %collective-permute-start.30 = (bf16[4,96,768]{2,1,0:T(8,128)(2,1)}, bf16[4,96,768]{2,1,0:T(8,128)(2,1)}, u32[]{:S(2)}, u32[]{:S(2)}) collective-permute-start(bf16[4,96,768]{2,1,0:T(8,128)(2,1)} %pad_maximum_fusion.6.refs_0_), channel_id=1, source_target_pairs={{0,2},{1,3},{2,0},{3,1},{4,6},{5,7},{6,4},{7,5},{8,10},{9,11},{10,... | collective-permute-start | bytes 1769480 | tf_op jit(solution)/shard_map/ppermute | solution.py:49
  116.8 27.8 %collective-permute-start.29 = (bf16[4,96,768]{2,1,0:T(8,128)(2,1)}, bf16[4,96,768]{2,1,0:T(8,128)(2,1)}, u32[]{:S(2)}, u32[]{:S(2)}) collective-permute-start(bf16[4,96,768]{2,1,0:T(8,128)(2,1)} %pad_maximum_fusion.6.refs_0_), channel_id=1, source_target_pairs={{0,1},{1,0},{2,3},{3,2},{4,5},{5,4},{6,7},{7,6},{8,9},{9,8},{10,11... | collective-permute-start | bytes 1769480 | tf_op jit(solution)/shard_map/ppermute | solution.py:49
  116.8 20.1 %collective-permute-start.37 = (bf16[4,96,768]{2,1,0:T(8,128)(2,1)}, bf16[4,96,768]{2,1,0:T(8,128)(2,1)}, u32[]{:S(2)}, u32[]{:S(2)}) collective-permute-start(bf16[4,96,768]{2,1,0:T(8,128)(2,1)} %pad_maximum_fusion.7), channel_id=1, source_target_pairs={{0,4},{4,0},{8,12},{12,8},{16,20},{20,16},{24,28},{28,24},{1,5},{5... | collective-permute-start | bytes 1769480 | tf_op jit(solution)/shard_map/ppermute | solution.py:49
  118.4 17.0 %collective-permute-start.36 = (bf16[2,96,768]{2,1,0:T(8,128)(2,1)}, bf16[2,96,768]{2,1,0:T(8,128)(2,1)}, u32[]{:S(2)}, u32[]{:S(2)}) collective-permute-start(bf16[2,96,768]{2,1,0:T(8,128)(2,1)} %collective-permute-done.35.refs_6_), channel_id=1, source_target_pairs={{0,1},{1,0},{2,3},{3,2},{4,5},{5,4},{6,7},{7,6},{8,9},{9,8},{10,11... | collective-permute-start | bytes 884744 | tf_op jit(solution)/shard_map/ppermute | solution.py:49
  134.8 18.8 %collective-permute-start.25 = (bf16[4,24,3840]{2,1,0:T(8,128)(2,1)S(1)}, bf16[4,24,3840]{2,1,0:T(8,128)(2,1)S(1)}, u32[]{:S(2)}, u32[]{:S(2)}) collective-permute-start(bf16[4,24,3840]{2,1,0:T(8,128)(2,1)S(1)} %copy-done.47), channel_id=1, source_target_pairs={{0,4},{4,0},{8,12},{12,8},{16,20},{20,16},{24,28},{28,24},{1,5},{5... | collective-permute-start | bytes 2211848 | tf_op jit(solution)/shard_map/ppermute | solution.py:49
  135.4 18.5 %collective-permute-start.18 = (bf16[4,24,3840]{2,1,0:T(8,128)(2,1)S(1)}, bf16[4,24,3840]{2,1,0:T(8,128)(2,1)S(1)}, u32[]{:S(2)}, u32[]{:S(2)}) collective-permute-start(bf16[4,24,3840]{2,1,0:T(8,128)(2,1)S(1)} %copy-done.3), channel_id=1, source_target_pairs={{0,2},{1,3},{2,0},{3,1},{4,6},{5,7},{6,4},{7,5},{8,10},{9,11},{10,... | collective-permute-start | bytes 2211848 | tf_op jit(solution)/shard_map/ppermute | solution.py:49
  136.9 17.2 %collective-permute-start.38 = (bf16[4,96,768]{2,1,0:T(8,128)(2,1)}, bf16[4,96,768]{2,1,0:T(8,128)(2,1)S(1)}, u32[]{:S(2)}, u32[]{:S(2)}) collective-permute-start(bf16[4,96,768]{2,1,0:T(8,128)(2,1)} %collective-permute-done.37.refs_8_), channel_id=1, source_target_pairs={{0,1},{1,0},{2,3},{3,2},{4,5},{5,4},{6,7},{7,6},{8,9},{9,8},{10,11... | collective-permute-start | bytes 1769480 | tf_op jit(solution)/shard_map/ppermute | solution.py:49
  136.9 17.5 %collective-permute-start.31 = (bf16[4,96,768]{2,1,0:T(8,128)(2,1)}, bf16[4,96,768]{2,1,0:T(8,128)(2,1)S(1)}, u32[]{:S(2)}, u32[]{:S(2)}) collective-permute-start(bf16[4,96,768]{2,1,0:T(8,128)(2,1)} %collective-permute-done.30.refs_2_), channel_id=1, source_target_pairs={{0,1},{1,0},{2,3},{3,2},{4,5},{5,4},{6,7},{7,6},{8,9},{9,8},{10,11... | collective-permute-start | bytes 1769480 | tf_op jit(solution)/shard_map/ppermute | solution.py:49
  144.6 19.7 %collective-permute-start.22 = (bf16[2,24,3840]{2,1,0:T(8,128)(2,1)S(1)}, bf16[2,24,3840]{2,1,0:T(8,128)(2,1)S(1)}, u32[]{:S(2)}, u32[]{:S(2)}) collective-permute-start(bf16[2,24,3840]{2,1,0:T(8,128)(2,1)S(1)} %copy-done.5), channel_id=1, source_target_pairs={{0,1},{1,0},{2,3},{3,2},{4,5},{5,4},{6,7},{7,6},{8,9},{9,8},{10,11... | collective-permute-start | bytes 1105928 | tf_op jit(solution)/shard_map/ppermute | solution.py:49
  153.6 14.8 %collective-permute-start.17 = (bf16[4,24,3840]{2,1,0:T(8,128)(2,1)S(1)}, bf16[4,24,3840]{2,1,0:T(8,128)(2,1)S(1)}, u32[]{:S(2)}, u32[]{:S(2)}) collective-permute-start(bf16[4,24,3840]{2,1,0:T(8,128)(2,1)S(1)} %copy-done.3), channel_id=1, source_target_pairs={{0,1},{1,0},{2,3},{3,2},{4,5},{5,4},{6,7},{7,6},{8,9},{9,8},{10,11... | collective-permute-start | bytes 2211848 | tf_op jit(solution)/shard_map/ppermute | solution.py:49
  154.1 14.3 %collective-permute-start.26 = (bf16[4,24,3840]{2,1,0:T(8,128)(2,1)S(1)}, bf16[4,24,3840]{2,1,0:T(8,128)(2,1)S(1)}, u32[]{:S(2)}, u32[]{:S(2)}) collective-permute-start(bf16[4,24,3840]{2,1,0:T(8,128)(2,1)S(1)} %collective-permute-done.25.refs_8_), channel_id=1, source_target_pairs={{0,1},{1,0},{2,3},{3,2},{4,5},{5,4},{6,7},{7,6},{8,9},{9,8},{10,11... | collective-permute-start | bytes 2211848 | tf_op jit(solution)/shard_map/ppermute | solution.py:49
  164.4 44.6 %collective-permute-start.43 = (bf16[128,768]{1,0:T(8,128)(2,1)}, bf16[128,768]{1,0:T(8,128)(2,1)}, u32[]{:S(2)}, u32[]{:S(2)}) collective-permute-start(bf16[128,768]{1,0:T(8,128)(2,1)} %get-tuple-element.166), channel_id=1, source_target_pairs={{0,16},{16,0},{4,20},{20,4},{1,17},{17,1},{5,21},{21,5},{2,18},{18... | collective-permute-start | bytes 589832 | tf_op jit(solution)/shard_map/ppermute | solution.py:56
  166.3 42.7 %collective-permute-start.44 = (bf16[128,768]{1,0:T(8,128)(2,1)}, bf16[128,768]{1,0:T(8,128)(2,1)}, u32[]{:S(2)}, u32[]{:S(2)}) collective-permute-start(bf16[128,768]{1,0:T(8,128)(2,1)} %get-tuple-element.167), channel_id=1, source_target_pairs={{0,24},{24,0},{4,28},{28,4},{1,25},{25,1},{5,29},{29,5},{2,26},{26... | collective-permute-start | bytes 589832 | tf_op jit(solution)/shard_map/ppermute | solution.py:56
  215.1 16.1 %all-to-all-start.3 = ((bf16[4,128,768]{2,1,0:T(8,128)(2,1)}), bf16[4,128,768]{2,1,0:T(8,128)(2,1)}, u32[]{:S(2)}, u32[]{:S(2)}) async-start(bf16[4,128,768]{2,1,0:T(8,128)(2,1)} %pad_maximum_fusion.2), calls=%async_computation.3 | async-start | bytes 1572864 | tf_op jit(solution)/shard_map/all_to_all | solution.py:87
  307.4 159.1 %collective-permute-start.62 = (bf16[768,2,960]{0,2,1:T(8,128)(2,1)}, bf16[768,2,960]{0,2,1:T(8,128)(2,1)}, u32[]{:S(2)}, u32[]{:S(2)}) collective-permute-start(bf16[768,2,960]{0,2,1:T(8,128)(2,1)} %fusion.18), channel_id=1, source_target_pairs={{0,1},{1,0},{2,3},{3,2},{4,5},{5,4},{6,7},{7,6},{8,9},{9,8},{10,11... | collective-permute-start | bytes 8847368 | tf_op jit(solution)/shard_map/ppermute | solution.py:49
  316.0 15.1 %all-to-all-start.5 = ((f32[32,1,293]{2,1,0:T(1,128)}), f32[32,1,293]{2,1,0:T(1,128)S(1)}, u32[]{:S(2)}, u32[]{:S(2)}) async-start(f32[32,1,293]{2,1,0:T(1,128)} %copy.305), calls=%async_computation.5 | async-start | bytes 98304 | tf_op jit(solution)/shard_map/all_to_all | solution.py:471
  330.8 51.4 %collective-permute-start.54 = (bf16[768,2,576]{0,2,1:T(8,128)(2,1)}, bf16[768,2,576]{0,2,1:T(8,128)(2,1)}, u32[]{:S(2)}, u32[]{:S(2)}) collective-permute-start(bf16[768,2,576]{0,2,1:T(8,128)(2,1)} %fusion.20), channel_id=1, source_target_pairs={{0,1},{1,0},{2,3},{3,2},{4,5},{5,4},{6,7},{7,6},{8,9},{9,8},{10,11... | collective-permute-start | bytes 5308424 | tf_op jit(solution)/shard_map/ppermute | solution.py:49
  331.0 15.1 %all-to-all-start.2 = ((bf16[4,128,768]{2,1,0:T(8,128)(2,1)}), bf16[4,128,768]{2,1,0:T(8,128)(2,1)S(1)}, u32[]{:S(2)}, u32[]{:S(2)}) async-start(bf16[4,128,768]{2,1,0:T(8,128)(2,1)} %bitcast.381), calls=%async_computation.2 | async-start | bytes 1572864 | tf_op jit(solution)/shard_map/all_to_all | solution.py:93
  347.0 29.8 %all-to-all-start.4 = ((bf16[4,128,768]{2,1,0:T(8,128)(2,1)}), bf16[4,128,768]{2,1,0:T(8,128)(2,1)S(1)}, u32[]{:S(2)}, u32[]{:S(2)}) async-start(bf16[4,128,768]{2,1,0:T(8,128)(2,1)} %bitcast.406), calls=%async_computation.4 | async-start | bytes 1572864 | tf_op jit(solution)/shard_map/all_to_all | solution.py:93
  364.6 53.9 %collective-permute-start.70 = (bf16[3072,2,192]{0,2,1:T(8,128)(2,1)}, bf16[3072,2,192]{0,2,1:T(8,128)(2,1)}, u32[]{:S(2)}, u32[]{:S(2)}) collective-permute-start(bf16[3072,2,192]{0,2,1:T(8,128)(2,1)} %fusion.19), channel_id=1, source_target_pairs={{0,1},{1,0},{2,3},{3,2},{4,5},{5,4},{6,7},{7,6},{8,9},{9,8},{10,11... | collective-permute-start | bytes 7077896 | tf_op jit(solution)/shard_map/ppermute | solution.py:49
  377.5 16.4 %collective-permute-start.53 = (bf16[128,768]{1,0:T(8,128)(2,1)}, bf16[128,768]{1,0:T(8,128)(2,1)S(1)}, u32[]{:S(2)}, u32[]{:S(2)}) collective-permute-start(bf16[128,768]{1,0:T(8,128)(2,1)} %slice_bitcast_fusion.2), channel_id=1, source_target_pairs={{0,24},{24,0},{4,28},{28,4},{1,25},{25,1},{5,29},{29,5},{2,26},{26... | collective-permute-start | bytes 589832 | tf_op jit(solution)/shard_map/ppermute | solution.py:56
  380.2 15.9 %collective-permute-start.51 = (bf16[128,768]{1,0:T(8,128)(2,1)}, bf16[128,768]{1,0:T(8,128)(2,1)}, u32[]{:S(2)}, u32[]{:S(2)}) collective-permute-start(bf16[128,768]{1,0:T(8,128)(2,1)} %get-tuple-element.164), channel_id=1, source_target_pairs={{0,8},{8,0},{4,12},{12,4},{1,9},{9,1},{5,13},{13,5},{2,10},{10,2},... | collective-permute-start | bytes 589832 | tf_op jit(solution)/shard_map/ppermute | solution.py:56
  409.0 30.4 %collective-permute-start.56 = (bf16[2,1,96,576]{3,2,1,0:T(8,128)(2,1)}, bf16[2,1,96,576]{3,2,1,0:T(8,128)(2,1)}, u32[]{:S(2)}, u32[]{:S(2)}) collective-permute-start(bf16[2,1,96,576]{3,2,1,0:T(8,128)(2,1)} %dynamic-slice_convert_fusion.9), channel_id=1, source_target_pairs={{0,4},{4,0},{8,12},{12,8},{16,20},{20,16},{24,28},{28,24},{1,5},{5... | collective-permute-start | bytes 663560 | tf_op jit(solution)/shard_map/ppermute | solution.py:49
  417.3 23.5 %collective-permute-start.58 = (bf16[2,96,576]{2,1,0:T(8,128)(2,1)}, bf16[2,96,576]{2,1,0:T(8,128)(2,1)}, u32[]{:S(2)}, u32[]{:S(2)}) collective-permute-start(bf16[2,96,576]{2,1,0:T(8,128)(2,1)} %fusion.80), channel_id=1, source_target_pairs={{0,2},{1,3},{2,0},{3,1},{4,6},{5,7},{6,4},{7,5},{8,10},{9,11},{10,... | collective-permute-start | bytes 663560 | tf_op jit(solution)/shard_map/ppermute | solution.py:49
  431.2 23.1 %collective-permute-start.71 = (bf16[2,2,384,192]{2,1,0,3:T(2,128)(2,1)}, bf16[2,2,384,192]{2,1,0,3:T(2,128)(2,1)}, u32[]{:S(2)}, u32[]{:S(2)}) collective-permute-start(bf16[2,2,384,192]{2,1,0,3:T(2,128)(2,1)} %fusion.35), channel_id=1, source_target_pairs={{0,2},{1,3},{2,0},{3,1},{4,6},{5,7},{6,4},{7,5},{8,10},{9,11},{10,... | collective-permute-start | bytes 1769480 | tf_op jit(solution)/shard_map/ppermute | solution.py:49
  457.9 25.9 %collective-permute-start.72 = (bf16[2,1,384,192]{2,3,1,0:T(8,128)(2,1)}, bf16[2,1,384,192]{2,3,1,0:T(8,128)(2,1)}, u32[]{:S(2)}, u32[]{:S(2)}) collective-permute-start(bf16[2,1,384,192]{2,3,1,0:T(8,128)(2,1)} %copy.298), channel_id=1, source_target_pairs={{0,4},{4,0},{8,12},{12,8},{16,20},{20,16},{24,28},{28,24},{1,5},{5... | collective-permute-start | bytes 884744 | tf_op jit(solution)/shard_map/ppermute | solution.py:49
  465.6 20.2 %collective-permute-start.74 = (bf16[2,384,192]{1,0,2:T(2,128)(2,1)}, bf16[2,384,192]{1,0,2:T(2,128)(2,1)}, u32[]{:S(2)}, u32[]{:S(2)}) collective-permute-start(bf16[2,384,192]{1,0,2:T(2,128)(2,1)} %fusion.64), channel_id=1, source_target_pairs={{0,2},{1,3},{2,0},{3,1},{4,6},{5,7},{6,4},{7,5},{8,10},{9,11},{10,... | collective-permute-start | bytes 884744 | tf_op jit(solution)/shard_map/ppermute | solution.py:49
  476.9 18.8 %collective-permute-start.63 = (bf16[2,2,96,960]{3,2,1,0:T(8,128)(2,1)}, bf16[2,2,96,960]{3,2,1,0:T(8,128)(2,1)}, u32[]{:S(2)}, u32[]{:S(2)}) collective-permute-start(bf16[2,2,96,960]{3,2,1,0:T(8,128)(2,1)} %fusion.33), channel_id=1, source_target_pairs={{0,2},{1,3},{2,0},{3,1},{4,6},{5,7},{6,4},{7,5},{8,10},{9,11},{10,... | collective-permute-start | bytes 2211848 | tf_op jit(solution)/shard_map/ppermute | solution.py:49
  482.2 16.3 %collective-permute-start.65 = (bf16[2,1,96,2,960]{4,2,0,3,1:T(8,128)(2,1)S(1)}, bf16[2,1,96,2,960]{4,2,0,3,1:T(8,128)(2,1)S(1)}, u32[]{:S(2)}, u32[]{:S(2)}) collective-permute-start(bf16[2,1,96,2,960]{4,2,0,3,1:T(8,128)(2,1)S(1)} %fusion.34), channel_id=1, source_target_pairs={{0,4},{4,0},{8,12},{12,8},{16,20},{20,16},{24,28},{28,24},{1,5},{5... | collective-permute-start | bytes 2211848 | tf_op jit(solution)/shard_map/ppermute | solution.py:49
  491.2 17.6 %collective-permute-start.76 = (bf16[384,192]{0,1:T(8,128)(2,1)S(1)}, bf16[384,192]{0,1:T(8,128)(2,1)S(1)}, u32[]{:S(2)}, u32[]{:S(2)}) collective-permute-start(bf16[384,192]{0,1:T(8,128)(2,1)S(1)} %bitcast.432), channel_id=1, source_target_pairs={{0,16},{4,20},{8,24},{12,28},{16,0},{20,4},{24,8},{28,12},{1,17},{... | collective-permute-start | bytes 442376 | tf_op jit(solution)/shard_map/ppermute | solution.py:49
  492.3 19.2 %collective-permute-start.75 = (bf16[384,192]{0,1:T(8,128)(2,1)S(1)}, bf16[384,192]{0,1:T(8,128)(2,1)S(1)}, u32[]{:S(2)}, u32[]{:S(2)}) collective-permute-start(bf16[384,192]{0,1:T(8,128)(2,1)S(1)} %bitcast.431), channel_id=1, source_target_pairs={{0,8},{4,12},{8,0},{12,4},{16,24},{20,28},{24,16},{28,20},{1,9},{5... | collective-permute-start | bytes 442376 | tf_op jit(solution)/shard_map/ppermute | solution.py:49
  492.3 19.2 %collective-permute-start.77 = (bf16[384,192]{0,1:T(8,128)(2,1)S(1)}, bf16[384,192]{0,1:T(8,128)(2,1)S(1)}, u32[]{:S(2)}, u32[]{:S(2)}) collective-permute-start(bf16[384,192]{0,1:T(8,128)(2,1)S(1)} %bitcast.430), channel_id=1, source_target_pairs={{0,24},{4,28},{8,16},{12,20},{16,8},{20,12},{24,0},{28,4},{1,25},{... | collective-permute-start | bytes 442376 | tf_op jit(solution)/shard_map/ppermute | solution.py:49
  (141 other events, 1466.7 us)

commit v2 on v1

v2 whole, which is shorter than its diff:
```python
import functools
import math

import jax
import jax.numpy as jnp
from jax import lax
from jax.experimental import pallas as pl
from jax.experimental.pallas import tpu as pltpu
from jax.sharding import PartitionSpec as P

HEAD_DIM = 64
LEVELS = 4
GROUP = 4
POOL = 32
VMEM = 58 << 20
OTHERS = ((1, 1), (1, 0), (0, 1))


def cost(us):
    return pl.CostEstimate(flops=int(us * 1.15e9), bytes_accessed=1024, transcendentals=0)


EPSILON = 1e-05
SCORE_DIV = 12.0
MASKED = -1e30
BF = jnp.bfloat16
F32 = jnp.float32
BOTH = ("wide", "narrow")


def matmul(left, right):
    return jnp.dot(left, right, preferred_element_type=F32)


def inner_rows(left, right):
    return lax.dot_general(left, right, (((0,), (0,)), ((), ())), preferred_element_type=F32)


def inner_cols(left, right):
    return lax.dot_general(left, right, (((1,), (1,)), ((), ())), preferred_element_type=F32)


def flip(x, axis, mask):
    size = lax.axis_size(axis)
    return lax.ppermute(x, axis, [(i, i ^ mask) for i in range(size)])


def flip_both(x, wide_mask, narrow_mask):
    wide, narrow = lax.axis_size("wide"), lax.axis_size("narrow")
    mask = wide_mask * narrow + narrow_mask
    return lax.ppermute(x, BOTH, [(i, i ^ mask) for i in range(wide * narrow)])


def phase(*values):
    return lax.optimization_barrier(values)


def across_levels(x, stride):
    groups = [[k * stride + i for k in range(LEVELS)] for i in range(stride)]
    return lax.all_to_all(x, "wide", 0, 0, axis_index_groups=groups, tiled=True)


def swap_levels(x, k, stride):
    pairs = []
    for i in range(stride):
        pairs += [(i, k * stride + i), (k * stride + i, i)]
    return lax.ppermute(x, "wide", pairs)


def bits_of(size):
    return [1 << b for b in range(size.bit_length() - 1)]


class Place:
    def __init__(self):
        self.wide = lax.axis_size("wide")
        self.narrow = lax.axis_size("narrow")
        self.stride = self.wide // LEVELS
        self.w = lax.axis_index("wide")
        self.n = lax.axis_index("narrow")
        self.z = self.w // self.stride
        self.y = self.w % self.stride
        self.me = self.w * self.narrow + self.n


def swap_in(place, pass_part, query_part):
    query = jnp.broadcast_to(query_part, (LEVELS, *query_part.shape[1:]))
    first = jnp.concatenate([query_part, pass_part])
    return across_levels(jnp.where(place.z == 0, first, query), place.stride)


def swap_in_directly(place, pass_part, query_part):
    got = [
        swap_levels(jnp.where(place.z == 0, pass_part[k - 1], query_part[0]), k, place.stride)
        for k in range(1, LEVELS)
    ]
    first = jnp.where(place.z == 0, query_part[0], got[0] + got[1] + got[2])
    return jnp.stack([first] + got)


def to_row(place, pass_part, query_part, got):
    four = jnp.where(place.z == 0, got, jnp.concatenate([pass_part, got[:1]]))
    mine = lax.all_to_all(four, "narrow", 0, 0, tiled=True)
    return mine.reshape(-1, mine.shape[-1])


def row_pieces(place, row):
    return lax.all_to_all(
        row.reshape(place.narrow, -1, row.shape[-1]), "narrow", 0, 0, tiled=True
    )


def swap_out(place, four):
    last = jnp.broadcast_to(four[3:], four.shape)
    return across_levels(jnp.where(place.z == 0, four, last), place.stride)


def from_row(place, four, got):
    pass_part = jnp.where(place.z == 0, got[1:], four[:3])
    query_part = jnp.where(place.z == 0, four[:1], got[:1])
    return pass_part, query_part


def assemble_kernel(plan, parts, me_ref, *refs):
    pieces, outs, sems = refs[: len(plan)], refs[len(plan) : -1], refs[-1]
    me = me_ref[0]
    copies = []
    for piece, masks in zip(pieces, plan):
        width = piece.shape[2] // sum(parts)
        for slot, mask in enumerate(masks):
            column = 0
            for out, count in zip(outs, parts):
                for part in range(count):
                    source = piece.at[slot, :, pl.ds(column, width)]
                    target = out.at[part, me ^ mask]
                    copies.append(pltpu.make_async_copy(source, target, sems.at[len(copies)]))
                    column += width
    for copy in copies:
        copy.start()
    for copy in copies:
        copy.wait()


def assemble(place, pieces, plan, parts):
    total = place.wide * place.narrow
    rows = pieces[0].shape[1]
    width = pieces[0].shape[2] // sum(parts)
    outs = pl.pallas_call(
        functools.partial(assemble_kernel, plan, parts),
        out_shape=[jax.ShapeDtypeStruct((count, total, rows, width), BF) for count in parts],
        in_specs=[pl.BlockSpec(memory_space=pltpu.SMEM)]
        + [pl.BlockSpec(memory_space=pl.ANY)] * len(pieces),
        out_specs=[pl.BlockSpec(memory_space=pltpu.VMEM)] * len(parts),
        scratch_shapes=[pltpu.SemaphoreType.DMA((total * sum(parts),))],
        cost_estimate=cost(5),
        compiler_params=pltpu.CompilerParams(vmem_limit_bytes=VMEM),
    )(place.me.reshape(1), *pieces)
    return [out.reshape(out.shape[0], total * rows, width) for out in outs]


def gather_levels(place, pair):
    slots = {0: jnp.where(place.z == 0, pair[1], pair[0])}
    for k in (3, 2, 1):
        send = jnp.where((place.z ^ k) == 0, pair[1], pair[0])
        slots[k] = flip(send, "wide", k * place.stride)
    return jnp.stack([slots[k] for k in range(LEVELS)])


def gather_columns(place, levels):
    s, narrow = place.stride, place.narrow
    own = [k * s * narrow for k in range(LEVELS)]
    pieces, plan = [levels], [own]
    if s == 2:
        for wide_mask, narrow_mask in ((1, 2), (0, 2), (1, 0)):
            pieces.append(flip_both(levels, wide_mask, narrow_mask))
            plan.append([m ^ (wide_mask * narrow + narrow_mask) for m in own])
    else:
        for b in bits_of(s):
            for i in range(len(pieces)):
                pieces.append(flip(pieces[i], "wide", b))
                plan.append([m ^ (b * narrow) for m in plan[i]])
        for i in range(len(pieces)):
            pieces.append(flip(pieces[i], "narrow", 2))
            plan.append([m ^ 2 for m in plan[i]])
    return pieces, plan


def gather_cores(pieces, plan):
    others = [flip(piece, "narrow", 1) for piece in pieces]
    return list(pieces) + others, plan + [[m ^ 1 for m in masks] for masks in plan]


def pick(x, index, dim):
    return lax.dynamic_index_in_dim(x, index, dim, keepdims=False)


def halve(x, place, axis, mask, dim):
    index = place.n if axis == "narrow" else place.w
    bit = jnp.where((index & mask) != 0, 1, 0)
    got = flip(pick(x, 1 - bit, dim).astype(BF), axis, mask)
    return pick(x, bit, dim) + got.astype(F32)


def scatter_tower(place, partial):
    s = place.stride
    rows, narrow, cols = partial.shape
    per = rows // place.wide
    x = partial.reshape(rows, 2, 2, cols)
    x = halve(x, place, "narrow", 1, 2)
    x = x.reshape(LEVELS, s, per, 2, cols)
    first, second = x[:2], x[2:]

    def over_columns(part):
        for b in reversed(bits_of(s)):
            shape = part.shape
            part = part.reshape(shape[0], 2, shape[1] // 2, *shape[2:])
            part = halve(part, place, "wide", b, 1)
        return part[:, 0]

    first = over_columns(halve(first, place, "narrow", 2, 3))
    second = halve(over_columns(second), place, "narrow", 2, 2)
    return jnp.stack(sum_levels(place, send_levels(place, jnp.concatenate([first, second]))))


def send_levels(place, levels):
    slots = [None] * LEVELS
    slots[0] = pick(levels, place.z, 0)
    for k in (3, 2, 1):
        slots[k] = flip(pick(levels, place.z ^ k, 0).astype(BF), "wide", k * place.stride)
    return slots


def sum_levels(place, slots):
    tower0 = sum(jnp.where(place.z == k, 0.0, slots[k].astype(F32)) for k in range(LEVELS))
    tower1 = sum(jnp.where(place.z == k, slots[k].astype(F32), 0.0) for k in range(LEVELS))
    return tower0, tower1


def share_kernel(at_ref, keep_ref, got_ref, own_ref, *sent_refs):
    x, y = at_ref[0], at_ref[1]

    def share(dx, dy):
        at = (x ^ dx, 0, y ^ dy)
        return keep_ref[at].astype(F32) + got_ref[at].astype(F32)

    own_ref[0] = share(0, 0)
    for ref, (dx, dy) in zip(sent_refs, OTHERS):
        ref[0] = share(dx, dy).astype(BF)


def column_shares(place, keep, got):
    r, c = got.shape[2:]
    block = pl.BlockSpec((2, 1, place.stride, r, c), lambda i, at: (0, i, 0, 0, 0))
    out = pl.BlockSpec((1, r, c), lambda i, at: (i, 0, 0))
    shape = (2, LEVELS, place.stride, r, c)
    return pl.pallas_call(
        share_kernel,
        grid_spec=pltpu.PrefetchScalarGridSpec(
            num_scalar_prefetch=1, grid=(LEVELS,), in_specs=[block] * 2, out_specs=[out] * 4
        ),
        out_shape=[jax.ShapeDtypeStruct((LEVELS, r, c), F32)]
        + [jax.ShapeDtypeStruct((LEVELS, r, c), BF)] * 3,
        compiler_params=pltpu.CompilerParams(vmem_limit_bytes=VMEM),
        cost_estimate=cost(6),
    )(jnp.stack([place.n // 2, place.y]), keep.reshape(shape), got.reshape(shape))


def send_columns(shares):
    return [shares[0]] + [
        flip_both(sent, dy, 2 * dx) for sent, (dx, dy) in zip(shares[1:], OTHERS)
    ]


def level_kernel(z_ref, own_ref, *refs):
    got_refs, (sum_ref, *sent_refs) = refs[:3], refs[3:]
    for k in range(LEVELS):
        at = z_ref[0] ^ k
        total = own_ref[at]
        for ref in got_refs:
            total = total + ref[at].astype(F32)
        if k == 0:
            sum_ref[...] = total
        else:
            sent_refs[k - 1][...] = total.astype(BF)


def level_shares(place, columns):
    r, c = columns[0].shape[1:]
    vmem = pl.BlockSpec(memory_space=pltpu.VMEM)
    return pl.pallas_call(
        level_kernel,
        in_specs=[pl.BlockSpec(memory_space=pltpu.SMEM)] + [vmem] * 4,
        out_specs=[vmem] * 4,
        out_shape=[jax.ShapeDtypeStruct((r, c), F32)] + [jax.ShapeDtypeStruct((r, c), BF)] * 3,
        compiler_params=pltpu.CompilerParams(vmem_limit_bytes=VMEM),
        cost_estimate=cost(3),
    )(place.z.reshape(1), *columns)


def swap_shares(place, shares):
    slots = [shares[0], None, None, None]
    for k in (3, 2, 1):
        slots[k] = flip(shares[k], "wide", k * place.stride)
    return slots


def product_kernel(step, me_ref, *refs):
    send_ref, keep_ref = refs[-2:]
    left_refs = refs[:-2]
    to_send = pl.program_id(0) < 2

    @pl.when(to_send)
    def _():
        step(left_refs, lambda at, v: send_ref.__setitem__((0, *at), v.astype(BF)))

    @pl.when(jnp.logical_not(to_send))
    def _():
        step(left_refs, lambda at, v: keep_ref.__setitem__((0, *at), v.astype(BF)))


def products(place, step, operands, specs, block):
    def target(j, me):
        return (j % 2) * 2 + jnp.where(j < 2, 1 - me[0] % 2, me[0] % 2)

    wide = place.wide
    grid_spec = pltpu.PrefetchScalarGridSpec(
        num_scalar_prefetch=1,
        grid=(4,),
        in_specs=specs(target),
        out_specs=[
            pl.BlockSpec((1, wide, *block), lambda j, me: (jnp.minimum(j, 1), 0, 0, 0)),
            pl.BlockSpec((1, wide, *block), lambda j, me: (jnp.maximum(j - 2, 0), 0, 0, 0)),
        ],
    )
    return pl.pallas_call(
        functools.partial(product_kernel, step),
        grid_spec=grid_spec,
        out_shape=[
            jax.ShapeDtypeStruct((2, wide, *block), BF),
            jax.ShapeDtypeStruct((2, wide, *block), BF),
        ],
        compiler_params=pltpu.CompilerParams(vmem_limit_bytes=VMEM),
        cost_estimate=cost(8),
    )(place.n.reshape(1), *operands)


def whole(shape):
    return pl.BlockSpec(shape, lambda j, me: (0,) * len(shape))


def grad_blocks(left, right, narrow):
    out = inner_rows(left, right)
    return out.reshape(out.shape[0], narrow, -1)


def products_back(place, active, blocks):
    t, ff = active.shape
    cols, rows = blocks.shape[2], ff // place.wide

    def step(refs, store):
        left, right = refs
        value = inner_rows(right[0], left[...])
        for w in range(place.wide):
            store((w,), value[:, w * rows : (w + 1) * rows])

    return products(
        place,
        step,
        (active, blocks),
        lambda target: [
            whole((t, ff)),
            pl.BlockSpec((1, t, cols), lambda j, me: (target(j, me), 0, 0)),
        ],
        (cols, rows),
    )


def finish_back(place, slots):
    return jnp.stack([part.T for part in sum_levels(place, slots)])


def products_out_in(place, context, blocks, normed, grad_hidden):
    narrow = place.narrow
    t, d = context.shape
    rows = d // place.wide
    cols_out, cols_in = blocks.shape[2], grad_hidden.shape[1] // narrow
    fold = cols_in // cols_out
    low = rows // fold

    def step(refs, store):
        context_ref, branch_ref, normed_ref, hidden_ref = refs
        value = inner_rows(normed_ref[...], hidden_ref[...])
        for w in range(place.wide):
            store((w, slice(0, rows)), value[w * rows : (w + 1) * rows])
        value = inner_rows(context_ref[...], branch_ref[0])
        for w in range(place.wide):
            for g in range(fold):
                store(
                    (w, slice(rows, rows + low), slice(g * cols_out, (g + 1) * cols_out)),
                    value[w * rows + g * low : w * rows + (g + 1) * low],
                )

    return products(
        place,
        step,
        (context, blocks, normed, grad_hidden),
        lambda target: [
            whole((t, d)),
            pl.BlockSpec((1, t, cols_out), lambda j, me: (target(j, me), 0, 0)),
            whole((t, d)),
            pl.BlockSpec((t, cols_in), lambda j, me: (0, target(j, me))),
        ],
        (rows + low, cols_in),
    )


def finish_out_in(place, slots, rows):
    parts = sum_levels(place, slots)
    low, cols = parts[0].shape[0] - rows, parts[0].shape[1]
    fold = rows // low
    grad_in = jnp.stack([part[:rows] for part in parts])
    grad_out = [
        jnp.moveaxis(part[rows:].reshape(low, fold, -1), 1, 0).reshape(rows, -1) for part in parts
    ]
    return jnp.stack(grad_out), grad_in


def products_qkv(place, inputs, blocks):
    t, d = inputs.shape
    rows, cols = d // place.wide, blocks.shape[2]
    half = rows // 2

    def step(refs, store):
        left, right = refs
        value = inner_rows(left[...], right[0])
        for w in range(place.wide):
            for g in range(2):
                store(
                    (w, slice(None), slice(g * cols, (g + 1) * cols)),
                    value[w * rows + g * half : w * rows + (g + 1) * half],
                )

    return products(
        place,
        step,
        (inputs, blocks),
        lambda target: [
            whole((t, d)),
            pl.BlockSpec((1, t, cols), lambda j, me: (target(j, me), 0, 0)),
        ],
        (half, 2 * cols),
    )


def finish_qkv(place, slots):
    parts = sum_levels(place, slots)
    cols = parts[0].shape[1] // 2
    return jnp.stack([jnp.concatenate([p[:, :cols], p[:, cols:]]) for p in parts])


def attend_kernel(x_ref, w_ref, rows_ref, seg_row_ref, seg_col_ref, qkv_ref, ctx_ref, lse_ref):
    x = x_ref[...]
    same = seg_col_ref[...] == seg_row_ref[...]
    qkv_ref[0] = (matmul(x, w_ref[0]) + rows_ref[0:1]).astype(BF)
    qkv_ref[1] = matmul(x, w_ref[1]).astype(BF)
    qkv_ref[2] = (matmul(x, w_ref[2]) + rows_ref[1:2]).astype(BF)
    for h in range(GROUP):
        lanes = slice(h * HEAD_DIM, (h + 1) * HEAD_DIM)
        q, k, v = qkv_ref[0, :, lanes], qkv_ref[1, :, lanes], qkv_ref[2, :, lanes]
        scores = jnp.where(same, inner_cols(k, q) * HEAD_DIM ** (-0.5), MASKED)
        top = jnp.max(scores, axis=0, keepdims=True)
        shifted = jnp.exp(scores - top)
        total = jnp.sum(shifted, axis=0, keepdims=True)
        probs = (shifted * (1.0 / total)).astype(BF)
        ctx_ref[:, lanes] = inner_rows(probs, v).astype(BF)
        lse_ref[0, h : h + 1, :] = top + jnp.log(total)


def attend(x, w_qkv, rows, segment):
    t, d = x.shape
    width = GROUP * HEAD_DIM
    steps = d // width
    return pl.pallas_call(
        attend_kernel,
        grid=(steps,),
        in_specs=[
            pl.BlockSpec((t, d), lambda j: (0, 0)),
            pl.BlockSpec((3, d, width), lambda j: (0, 0, j)),
            pl.BlockSpec((8, width), lambda j: (0, j)),
            pl.BlockSpec((1, t), lambda j: (0, 0)),
            pl.BlockSpec((t, 1), lambda j: (0, 0)),
        ],
        out_specs=[
            pl.BlockSpec((3, t, width), lambda j: (0, 0, j)),
            pl.BlockSpec((t, width), lambda j: (0, j)),
            pl.BlockSpec((1, GROUP, t), lambda j: (j, 0, 0)),
        ],
        out_shape=[
            jax.ShapeDtypeStruct((3, t, d), BF),
            jax.ShapeDtypeStruct((t, d), BF),
            jax.ShapeDtypeStruct((steps, GROUP, t), F32),
        ],
        compiler_params=pltpu.CompilerParams(vmem_limit_bytes=VMEM),
        cost_estimate=cost(11),
    )(x, w_qkv, rows, segment.reshape(1, t), segment.reshape(t, 1))


def attend_back_kernel(
    gb_ref, w_ref, qkv_ref, lse_ref, seg_row_ref, seg_col_ref, out_ref, blocks_ref, sums_ref
):
    scale = HEAD_DIM ** (-0.5)
    same = seg_col_ref[...] == seg_row_ref[...]
    grad = inner_cols(gb_ref[...], w_ref[...]).astype(BF)
    for h in range(GROUP):
        lanes = slice(h * HEAD_DIM, (h + 1) * HEAD_DIM)
        q, k, v = qkv_ref[0, :, lanes], qkv_ref[1, :, lanes], qkv_ref[2, :, lanes]
        g = grad[:, lanes]
        scores = jnp.where(same, inner_cols(k, q) * scale, MASKED)
        probs = jnp.exp(scores - lse_ref[0, h : h + 1, :])
        grad_probs = inner_cols(v, g)
        delta = jnp.sum(probs * grad_probs, axis=0, keepdims=True)
        grad_scores = (probs * (grad_probs - delta)).astype(BF)
        out_ref[0, :, lanes] = (inner_rows(grad_scores, k) * scale).astype(BF)
        out_ref[1, :, lanes] = (matmul(grad_scores, q) * scale).astype(BF)
        out_ref[2, :, lanes] = matmul(probs.astype(BF), g).astype(BF)
    sums_ref[0:1] = jnp.sum(out_ref[0].astype(F32), axis=0, keepdims=True)
    sums_ref[1:2] = jnp.sum(out_ref[2].astype(F32), axis=0, keepdims=True)
    per_block = blocks_ref.shape[2] // HEAD_DIM
    heads = blocks_ref.shape[0] * per_block // 3
    for step in range(heads // GROUP):

        @pl.when(pl.program_id(0) == step)
        def _(step=step):
            for part in range(3):
                for h in range(GROUP):
                    block, at = divmod(part * heads + step * GROUP + h, per_block)
                    blocks_ref[block, :, at * HEAD_DIM : (at + 1) * HEAD_DIM] = out_ref[
                        part, :, h * HEAD_DIM : (h + 1) * HEAD_DIM
                    ]


def attend_back(grad_branch, w_out, qkv, lse, segment, narrow):
    t, d = grad_branch.shape
    width = GROUP * HEAD_DIM
    return pl.pallas_call(
        attend_back_kernel,
        grid=(d // width,),
        in_specs=[
            pl.BlockSpec((t, d), lambda j: (0, 0)),
            pl.BlockSpec((width, d), lambda j: (j, 0)),
            pl.BlockSpec((3, t, width), lambda j: (0, 0, j)),
            pl.BlockSpec((1, GROUP, t), lambda j: (j, 0, 0)),
            pl.BlockSpec((1, t), lambda j: (0, 0)),
            pl.BlockSpec((t, 1), lambda j: (0, 0)),
        ],
        out_specs=[
            pl.BlockSpec((3, t, width), lambda j: (0, 0, j)),
            pl.BlockSpec((narrow, t, 3 * d // narrow), lambda j: (0, 0, 0)),
            pl.BlockSpec((2, width), lambda j: (0, j)),
        ],
        out_shape=[
            jax.ShapeDtypeStruct((3, t, d), BF),
            jax.ShapeDtypeStruct((narrow, t, 3 * d // narrow), BF),
            jax.ShapeDtypeStruct((2, d), F32),
        ],
        compiler_params=pltpu.CompilerParams(vmem_limit_bytes=VMEM),
        cost_estimate=cost(20),
    )(grad_branch, w_out, qkv, lse, segment.reshape(1, t), segment.reshape(t, 1))


def hidden_kernel(x_ref, w_ref, bias_ref, active_ref, slope_ref):
    pre = matmul(x_ref[...], w_ref[0]) + bias_ref[...]
    below = 0.5 + 0.5 * lax.erf(pre * 0.5**0.5)
    active_ref[...] = (pre * below).astype(BF)
    density = jnp.exp(-0.5 * pre * pre) * (2.0 * math.pi) ** (-0.5)
    slope_ref[...] = (below + pre * density).astype(BF)


def hidden_layer(x, w_in, in_bias):
    t, d = x.shape
    parts, _, width = w_in.shape
    block = pl.BlockSpec((t, width), lambda j: (0, j))
    shape = jax.ShapeDtypeStruct((t, parts * width), BF)
    return pl.pallas_call(
        hidden_kernel,
        grid=(parts,),
        in_specs=[
            pl.BlockSpec((t, d), lambda j: (0, 0)),
            pl.BlockSpec((1, d, width), lambda j: (j, 0, 0)),
            pl.BlockSpec((1, width), lambda j: (0, j)),
        ],
        out_specs=[block, block],
        out_shape=[shape, shape],
        compiler_params=pltpu.CompilerParams(vmem_limit_bytes=VMEM),
        cost_estimate=cost(8),
    )(x, w_in, in_bias)


def norm_parts(value):
    mean = jnp.mean(value, axis=-1, keepdims=True)
    centered = value - mean
    scale = lax.rsqrt(jnp.mean(centered * centered, axis=-1, keepdims=True) + EPSILON)
    return centered * scale, scale


def norm_back(grad, unit, scale, gain):
    e = grad * gain
    part = jnp.mean(e * unit, axis=-1, keepdims=True)
    return (e - jnp.mean(e, axis=-1, keepdims=True) - unit * part) * scale


def total(value):
    return jnp.sum(jnp.sum(value, axis=0, keepdims=True), axis=1, keepdims=True)


def column_sum(value):
    return jnp.sum(value, axis=0, keepdims=True)


def store_blocks(ref, value):
    count, _, width = ref.shape
    for i in range(count):
        ref[i] = value[:, i * width : (i + 1) * width]


def calls(kernel, outs, us, **kwargs):
    return pl.pallas_call(
        kernel,
        out_shape=[jax.ShapeDtypeStruct(shape, dtype) for shape, dtype in outs],
        compiler_params=pltpu.CompilerParams(vmem_limit_bytes=VMEM),
        cost_estimate=cost(us),
        **kwargs,
    )


def branch_kernel(ctx, w, x, rows, valid, normed, low, unit, scale, stats):
    branch = matmul(ctx[...], w[0]) + rows[2:3]
    residual = x[...].astype(F32) + branch
    unit[...], scale[...] = norm_parts(residual)
    normed[...] = unit[...] * rows[6:7] + rows[3:4]
    low[...] = normed[...].astype(BF)
    for i, value in enumerate((residual, branch)):
        stats[i : i + 1] = jnp.broadcast_to(total(valid[...] * value * value), (1, 128))


def branch_layer(context, w_out, inputs, rows, valid):
    t, d = inputs.shape
    outs = [((t, d), F32), ((t, d), BF), ((t, d), F32), ((t, 1), F32), ((2, 128), F32)]
    return calls(branch_kernel, outs, 5)(context, w_out, inputs, rows, valid)


def output_kernel(active, w, normed, rows, valid, hot, low, unit, scale, pooled, stats, acc):
    step = pl.program_id(0)
    product = matmul(active[...], w[...])

    @pl.when(step == 0)
    def _():
        acc[...] = product

    @pl.when(step > 0)
    def _():
        acc[...] += product

    @pl.when(step == pl.num_programs(0) - 1)
    def _():
        ffn_out = acc[...] + rows[4:5]
        residual = normed[...] + ffn_out
        unit[...], scale[...] = norm_parts(residual)
        low[...] = (unit[...] * rows[7:8] + rows[5:6]).astype(BF)
        pooled[...] = matmul(hot[...].astype(BF), low[...]).astype(BF)
        sums = (valid[...] * residual * residual, valid[...] * ffn_out * ffn_out, valid[...])
        for i, value in enumerate(sums):
            stats[i : i + 1] = jnp.broadcast_to(total(value), (1, 128))


def all_of(shape):
    return pl.BlockSpec(shape, lambda j: (0,) * len(shape))


def output_layer(active, w_back, normed, rows, valid, hot):
    t, ff = active.shape
    d = w_back.shape[1]
    steps = ff // d
    outs = [((t, d), BF), ((t, d), F32), ((t, 1), F32), ((hot.shape[0], d), BF), ((3, 128), F32)]
    return calls(
        output_kernel,
        outs,
        9,
        grid=(steps,),
        in_specs=[
            pl.BlockSpec((t, d), lambda j: (0, j)),
            pl.BlockSpec((d, d), lambda j: (j, 0)),
        ]
        + [all_of(a.shape) for a in (normed, rows, valid, hot)],
        out_specs=[all_of(shape) for shape, _ in outs],
        scratch_shapes=[pltpu.VMEM((t, d), F32)],
    )(active, w_back, normed, rows, valid, hot)


def output_back_kernel(cot, valid, hot, pool, unit, scale, rows, grad, low, blocks, sums):
    grad_out = cot[...].astype(F32) * valid[...] + lax.dot_general(
        hot[...],
        pool[...],
        (((0,), (0,)), ((), ())),
        precision=lax.Precision.HIGHEST,
        preferred_element_type=F32,
    )
    sums[0:1] = column_sum(grad_out * unit[...])
    sums[1:2] = column_sum(grad_out)
    grad[...] = norm_back(grad_out, unit[...], scale[...], rows[7:8])
    low[...] = grad[...].astype(BF)
    sums[2:3] = column_sum(low[...].astype(F32))
    store_blocks(blocks, low[...])


def output_back(cot, valid, hot, pool, unit, scale, rows, narrow):
    t, d = cot.shape
    outs = [((t, d), F32), ((t, d), BF), ((narrow, t, d // narrow), BF), ((3, d), F32)]
    return calls(output_back_kernel, outs, 6)(cot, valid, hot, pool, unit, scale, rows)


def hidden_back_kernel(
    low, w_back, slope, w_in, grad, unit, scale, rows, hidden, inb, residual, branch, blocks, sums, acc
):
    step = pl.program_id(0)
    hidden[...] = (inner_cols(low[...], w_back[...]) * slope[...].astype(F32)).astype(BF)
    inb[...] = column_sum(hidden[...].astype(F32))
    product = inner_cols(hidden[...], w_in[0])

    @pl.when(step == 0)
    def _():
        acc[...] = grad[...] + product

    @pl.when(step > 0)
    def _():
        acc[...] += product

    @pl.when(step == pl.num_programs(0) - 1)
    def _():
        value = acc[...]
        sums[0:1] = column_sum(value * unit[...])
        sums[1:2] = column_sum(value)
        residual[...] = norm_back(value, unit[...], scale[...], rows[6:7])
        branch[...] = residual[...].astype(BF)
        sums[2:3] = column_sum(branch[...].astype(F32))
        store_blocks(blocks, branch[...])


def hidden_back(low, w_back, slope, w_in, grad, unit, scale, rows, narrow):
    t, d = low.shape
    ff = slope.shape[1]
    tile = pl.BlockSpec((t, d), lambda j: (0, j))
    outs = [
        ((t, ff), BF),
        ((1, ff), F32),
        ((t, d), F32),
        ((t, d), BF),
        ((narrow, t, d // narrow), BF),
        ((3, d), F32),
    ]
    return calls(
        hidden_back_kernel,
        outs,
        14,
        grid=(ff // d,),
        in_specs=[
            all_of(low.shape),
            pl.BlockSpec((d, d), lambda j: (j, 0)),
            tile,
            pl.BlockSpec((1, d, d), lambda j: (j, 0, 0)),
        ]
        + [all_of(a.shape) for a in (grad, unit, scale, rows)],
        out_specs=[tile, pl.BlockSpec((1, d), lambda j: (0, j))]
        + [all_of(shape) for shape, _ in outs[2:]],
        scratch_shapes=[pltpu.VMEM((t, d), F32)],
    )(low, w_back, slope, w_in, grad, unit, scale, rows)


def input_back_kernel(grad, w, residual, out, acc):
    step = pl.program_id(0)
    product = inner_cols(grad[0], w[0])

    @pl.when(step == 0)
    def _():
        acc[...] = residual[...] + product

    @pl.when(step == 1)
    def _():
        acc[...] += product

    @pl.when(step == 2)
    def _():
        out[...] = (acc[...] + product).astype(BF)


def input_back(grad_qkv, w_qkv, residual):
    _, t, d = grad_qkv.shape
    return calls(
        input_back_kernel,
        [((t, d), BF)],
        6,
        grid=(3,),
        in_specs=[
            pl.BlockSpec((1, t, d), lambda j: (j, 0, 0)),
            pl.BlockSpec((1, d, d), lambda j: (j, 0, 0)),
            all_of((t, d)),
        ],
        out_specs=[all_of((t, d))],
        scratch_shapes=[pltpu.VMEM((t, d), F32)],
    )(grad_qkv, w_qkv, residual)[0]


def spread_masks(count, width):
    total_cols = count * width
    column = lax.broadcasted_iota(jnp.int32, (count, total_cols), 1)
    first = lax.broadcasted_iota(jnp.int32, (count, total_cols), 0) * width
    own = (column >= first) & (column < first + width)
    owner = jnp.sum(jnp.where(own, first, 0), axis=0, keepdims=True)
    within = lax.broadcasted_iota(jnp.int32, (width, total_cols), 1) - owner
    spread = within == lax.broadcasted_iota(jnp.int32, (width, total_cols), 0)
    return own, spread.astype(F32)


def unpack_kernel(small, rows, inb):
    count = small.shape[0]
    width = rows.shape[1] // count
    value = small[...].astype(F32)

    def unpack(part, own, spread):
        placed = matmul(part.astype(BF), spread.astype(BF))
        return column_sum(jnp.where(own, placed, 0.0))

    masks = spread_masks(count, width)
    for r in range(8):
        rows[r : r + 1] = unpack(value[:, r * width : (r + 1) * width], *masks)
    masks = spread_masks(count, inb.shape[1] // count)
    inb[...] = unpack(value[:, 8 * width : 8 * width + inb.shape[1] // count], *masks)


def unpack_params(small, d, ff):
    return calls(unpack_kernel, [((8, d), F32), ((1, ff), F32)], 2)(small)


def pack_kernel(attn, out, ffn, inb, stats_a, stats_b, packed):
    count = packed.shape[0]
    width = out.shape[1] // count
    vectors = (
        attn[0:1], attn[1:2], out[2:3], out[1:2], ffn[2:3], ffn[1:2], out[0:1], ffn[0:1], inb[...]
    )
    packed[...] = jnp.zeros(packed.shape, F32)
    at = 0
    for i, vector in enumerate(vectors):
        if i in (0, 8):
            width = vector.shape[1] // count
            own, spread = spread_masks(count, width)
        packed[:, at : at + width] = lax.dot_general(
            jnp.where(own, vector, 0.0),
            spread,
            (((1,), (1,)), ((), ())),
            precision=lax.Precision.HIGHEST,
            preferred_element_type=F32,
        )
        at += width
    for i, row in enumerate((stats_a[0:1], stats_a[1:2], stats_b[0:1], stats_b[1:2], stats_b[2:3])):
        packed[:, at + i : at + i + 1] = jnp.broadcast_to(row[:, :1], (count, 1))


def pack_sums(count, attn, out, ffn, inb, stats_a, stats_b):
    return calls(pack_kernel, [((count, 384), F32)], 4)(attn, out, ffn, inb, stats_a, stats_b)[0]


def match_grads(rows, label_rows, label_cols):
    is_query, is_pass = label_rows >= 0, label_cols >= 0
    match = jnp.where(is_pass, inner_cols(rows, rows) / SCORE_DIV, MASKED)
    shifted = jnp.exp(match - jnp.max(match, axis=1, keepdims=True))
    probs = shifted / jnp.sum(shifted, axis=1, keepdims=True)
    hot = (label_rows == label_cols).astype(F32)
    grad = jnp.where(is_query & is_pass, (probs - hot) / SCORE_DIV, 0.0).astype(BF)
    return matmul(grad[:POOL], rows) + inner_rows(grad[:, :POOL], rows)


def match_kernel(rows, label_rows, label_cols, out):
    out[...] = match_grads(rows[...], label_rows[...], label_cols[...])


def row_of(z, y, n, s):
    own = (z * s + y) * 3 + n
    spare = y * 3 + (z - 1)
    return jnp.where(z == 0, n * s + y, jnp.where(n < 3, own, spare))


def body(
    passages,
    queries,
    passage_cot,
    query_cot,
    passage_lengths,
    query_lengths,
    labels,
    w_qkv,
    w_out,
    w_in,
    w_back,
    biases,
    norm_gains,
    in_bias,
):
    place = Place()
    s, narrow, devices = place.stride, place.narrow, place.wide * place.narrow
    model_width = passages.shape[2]
    length = passages.shape[1] * narrow
    segs, qsegs = passage_lengths.shape[1] - 1, query_lengths.shape[1] - 1
    on_query = place.z == 0

    piece = model_width // devices
    small = jnp.concatenate(
        [biases.reshape(2, -1), norm_gains.reshape(2, -1), in_bias.reshape(2, -1)], axis=1
    )
    whole = jnp.concatenate(
        [passage_lengths.reshape(-1), query_lengths.reshape(-1), labels.reshape(-1)]
    )
    whole = jnp.concatenate([whole // 32, whole % 32]).astype(BF)
    small_count = small.shape[1]
    to_query = (jnp.arange(devices) < s * narrow)[:, None]
    small = jnp.where(to_query, small[1][None], small[0][None])
    small = jnp.concatenate([small, jnp.broadcast_to(whole, (devices, whole.shape[0]))], axis=1)

    in_parts = w_in.shape[2] // w_out.shape[2]
    levels_qkv = gather_levels(place, w_qkv)
    swapped = swap_in_directly(place, passages, queries)
    out_in = jnp.concatenate([w_out, w_in], axis=2)
    levels_qkv, swapped, out_in, small = phase(levels_qkv, swapped, out_in, small)

    pieces_qkv, plan = gather_columns(place, levels_qkv)
    inputs = to_row(place, passages, queries, swapped)
    levels_out_in = gather_levels(place, out_in)
    pieces_qkv, inputs, levels_out_in = phase(pieces_qkv, inputs, levels_out_in)

    cores_qkv, core_plan = gather_cores(pieces_qkv, plan)
    cores_qkv, levels_out_in, w_back, small = phase(cores_qkv, levels_out_in, w_back, small)

    pieces_out_in, _ = gather_columns(place, levels_out_in)
    levels_back = gather_levels(place, w_back)
    (w_qkv_all,) = assemble(place, cores_qkv, core_plan, (3,))
    small = lax.all_to_all(small, BOTH, 0, 0, tiled=True)

    n_bias, n_gain = biases.shape[1], norm_gains.shape[1]
    ff = in_bias.shape[1] * devices
    if s == 2:
        rows, inb_row = unpack_params(small, model_width, ff)
    else:
        params = small[:, :small_count].astype(F32)
        vectors = params[:, : (n_bias + n_gain) * piece].reshape(devices, n_bias + n_gain, piece)
        rows = vectors.transpose(1, 0, 2).reshape(n_bias + n_gain, -1)
        inb_row = params[:, (n_bias + n_gain) * piece :].reshape(1, -1)
    ints = small[:, small_count : small_count + whole.shape[0]].astype(F32)
    half = ints.shape[1] // 2
    ints = (ints[::narrow, :half] * 32 + ints[::narrow, half:]).astype(jnp.int32)
    n_pass = passage_lengths.size
    n_query = query_lengths.size
    pass_lens = ints[:, :n_pass].reshape(-1, segs + 1)
    query_lens = ints[:, n_pass : n_pass + n_query].reshape(-1, qsegs + 1)
    label_all = ints[:, n_pass + n_query :].reshape(-1, qsegs)
    my_row = row_of(place.z, place.y, place.n, s)
    pass_row = pick(pass_lens, jnp.where(on_query, 0, my_row), 0)
    query_row = pick(query_lens, jnp.where(on_query, my_row, 0), 0)
    ends_p = jnp.cumsum(pass_row)[:-1]
    ends_q = jnp.cumsum(query_row)[:-1]
    starts_p, starts_q = ends_p - pass_row[:-1], ends_q - query_row[:-1]
    ends_p = jnp.concatenate([ends_p, jnp.full((qsegs - segs,), length + 1, jnp.int32)])
    ends = jnp.where(on_query, ends_q, ends_p)
    seg_count = jnp.where(on_query, qsegs, segs)
    position = jnp.arange(length, dtype=jnp.int32)
    segment = jnp.sum((position[:, None] >= ends[None, :]).astype(jnp.int32), axis=1)
    valid = (segment < seg_count).astype(F32)[:, None]
    slot = jnp.arange(POOL)
    starts = jnp.where(on_query, jnp.concatenate([starts_q, jnp.full((qsegs,), -1)]), -1)
    for z in range(1, LEVELS):
        here = (place.z == z) & (slot >= qsegs + segs * (z - 1)) & (slot < qsegs + segs * z)
        starts = jnp.where(here, jnp.tile(starts_p, POOL // segs), starts)
    hot = (starts[:, None] == position[None, :]).astype(F32)
    masks = [0]
    if s == 2:
        masks += [dy * narrow + 2 * dx for dx, dy in OTHERS]
        masks += [m ^ 1 for m in masks]
    else:
        for mask in [b * narrow for b in bits_of(s)] + [b for b in reversed(bits_of(narrow))]:
            masks = masks + [m ^ mask for m in masks]
    there = (place.y * narrow + place.n) ^ jnp.array(masks, jnp.int32)
    their_y, their_n = there // narrow, there % narrow
    label_rows = label_all[row_of(jnp.int32(0), their_y, their_n, s)]
    label_rows = jnp.pad(label_rows, ((0, 0), (0, POOL - qsegs)), constant_values=-1)
    levels = jnp.arange(1, LEVELS)
    pass_rows = row_of(levels[None, :], their_y[:, None], their_n[:, None], s)
    pass_ids = (pass_rows[:, :, None] * segs + jnp.arange(segs)).reshape(len(masks), -1)
    spare = POOL - qsegs - pass_ids.shape[1]
    label_cols = jnp.pad(pass_ids, ((0, 0), (qsegs, spare)), constant_values=-1)
    label_rows, label_cols = label_rows.reshape(-1, 1), label_cols.reshape(1, -1)

    qkv, context, log_sum = attend(inputs, w_qkv_all, rows, segment)
    tables = (rows, inb_row, segment, valid, hot, label_rows, label_cols)
    context, pieces_out_in, levels_back, cots, tables = phase(
        context, pieces_out_in, levels_back, (passage_cot, query_cot), tables
    )
    rows, inb_row, segment, valid, hot, label_rows, label_cols = tables

    cores_out_in, _ = gather_cores(pieces_out_in, plan)
    cores_out_in, levels_back, cots = phase(cores_out_in, levels_back, cots)

    pieces_back, _ = gather_columns(place, levels_back)
    swapped = swap_in(place, *cots)
    w_out_all, w_in_all = assemble(place, cores_out_in, core_plan, (1, in_parts))
    normed, normed_low, unit_one, scale_one, stats_one = branch_layer(
        context, w_out_all, inputs, rows, valid
    )
    active, slope = hidden_layer(normed_low, w_in_all, inb_row)
    active, pieces_back, swapped = phase(active, pieces_back, swapped)

    cores_back, _ = gather_cores(pieces_back, plan)
    cot = to_row(place, passage_cot, query_cot, swapped)
    w_back_all = assemble(place, cores_back, core_plan, (1,))[0][0]
    output_low, unit_two, scale_two, pooled, stats_two = output_layer(
        active, w_back_all, normed, rows, valid, hot
    )
    pooled, cot = phase(pooled, cot)

    column = sum([flip(pooled, "wide", k * s).astype(F32) for k in (3, 2, 1)], pooled.astype(F32))
    seen = column.astype(BF)[None]
    if s == 2:
        seen = jnp.concatenate([seen] + [flip_both(seen, dy, 2 * dx) for dx, dy in OTHERS])
        seen = jnp.concatenate([seen, flip(seen, "narrow", 1)])
    else:
        for axis, step in [("wide", b) for b in bits_of(s)] + [
            ("narrow", b) for b in reversed(bits_of(narrow))
        ]:
            seen = jnp.concatenate([seen, flip(seen, axis, step)])
    seen = seen.reshape(-1, model_width)
    if s == 2:
        (grad_pool,) = calls(match_kernel, [((POOL, model_width), F32)], 3)(
            seen, label_rows, label_cols
        )
    else:
        grad_pool = match_grads(seen, label_rows, label_cols)

    grad_resid_two, grad_ffn, blocks_c, sums_two = output_back(
        cot, valid, hot, grad_pool, unit_two, scale_two, rows, narrow
    )
    if s == 2:
        send_c, keep_c = products_back(place, active, blocks_c)
        send_c, output_low = phase(send_c, output_low)
        got_c = flip(send_c, "narrow", 1)
        out_four = row_pieces(place, output_low)
        shares_c = column_shares(place, keep_c, got_c)
        shares_c, grad_ffn = phase(shares_c, grad_ffn)

        columns_c = send_columns(shares_c)
    grad_hidden, inb_sums, grad_residual, grad_branch, blocks_b, sums_one = hidden_back(
        grad_ffn, w_back_all, slope, w_in_all, grad_resid_two, unit_one, scale_one, rows, narrow
    )
    if s == 2:
        send_b, keep_b = products_out_in(place, context, blocks_b, normed_low, grad_hidden)
        send_b, columns_c, out_four = phase(send_b, columns_c, out_four)

        got_b = flip(send_b, "narrow", 1)
        level_c = level_shares(place, columns_c)
        shares_b = column_shares(place, keep_b, got_b)
        shares_b, level_c, grad_branch, out_four = phase(shares_b, level_c, grad_branch, out_four)

        columns_b = send_columns(shares_b)
        levels_c = swap_shares(place, level_c)
        swapped = swap_out(place, out_four)
    grad_qkv, blocks_a, sums_qkv = attend_back(
        grad_branch, w_out_all[0], qkv, log_sum, segment, narrow
    )
    if s == 2:
        send_a, keep_a = products_qkv(place, inputs, blocks_a)
        send_a, grad_qkv, columns_b, levels_c, swapped = phase(
            send_a, grad_qkv, columns_b, levels_c, swapped
        )
        passage_out, query_out = from_row(place, out_four, swapped)

        got_a = flip(send_a, "narrow", 1)
        level_b = level_shares(place, columns_b)
    input_grad = input_back(grad_qkv, w_qkv_all, grad_residual)
    packed = pack_sums(devices, sums_qkv, sums_one, sums_two, inb_sums, stats_one, stats_two)
    if s == 2:
        shares_a = column_shares(place, keep_a, got_a)
        shares_a, level_b, input_grad = phase(shares_a, level_b, input_grad)

        columns_a = send_columns(shares_a)
        levels_b = swap_shares(place, level_b)
        in_four = row_pieces(place, input_grad)
        grad_w_back = finish_back(place, levels_c)
        columns_a, levels_b, in_four, packed = phase(columns_a, levels_b, in_four, packed)

        levels_a = swap_shares(place, level_shares(place, columns_a))
        swapped = swap_out(place, in_four)
        packed = lax.all_to_all(packed, BOTH, 0, 0, tiled=True)
        grad_w_out, grad_w_in = finish_out_in(place, levels_b, model_width // place.wide)
        grad_w_qkv = finish_qkv(place, levels_a)
        passage_grad, query_grad = from_row(place, in_four, swapped)
    else:
        packed = lax.all_to_all(packed, BOTH, 0, 0, tiled=True)
        grad_w_back = scatter_tower(place, grad_blocks(active, grad_ffn, narrow))
        grad_w_out = scatter_tower(place, grad_blocks(context, grad_branch, narrow))
        grad_w_in = scatter_tower(place, grad_blocks(normed_low, grad_hidden, narrow))
        flat = jnp.moveaxis(grad_qkv, 0, 1).reshape(length, -1)
        grad_w_qkv = scatter_tower(place, grad_blocks(inputs, flat, narrow))
        out_four, in_four = row_pieces(place, output_low), row_pieces(place, input_grad)
        passage_out, query_out = from_row(place, out_four, swap_out(place, out_four))
        passage_grad, query_grad = from_row(place, in_four, swap_out(place, in_four))

    packed = packed.reshape(LEVELS, -1, packed.shape[1]).sum(axis=1)
    packed = jnp.stack([packed[1] + packed[2] + packed[3], packed[0]])
    edges = [n_bias * piece, (n_bias + n_gain) * piece]
    edges.append(edges[1] + in_bias.shape[1])
    grad_biases = packed[:, : edges[0]].reshape(2, n_bias, piece)
    grad_gains = packed[:, edges[0] : edges[1]].reshape(2, n_gain, piece)
    grad_inb = packed[:, edges[1] : edges[2]]
    totals = packed[:, edges[2] : edges[2] + 5]
    rms_stats = jnp.sqrt(totals[:, :4] / (totals[:, 4:] * model_width))
    return (
        passage_out,
        query_out,
        passage_grad,
        query_grad,
        grad_w_qkv,
        grad_w_out,
        grad_w_in,
        grad_w_back,
        grad_biases,
        grad_gains,
        grad_inb,
        rms_stats,
    )


def solution(mesh):
    return jax.shard_map(
        body,
        mesh=mesh,
        in_specs=(
            P("wide", "narrow", None),
            P("wide", "narrow", None),
            P("wide", "narrow", None),
            P("wide", "narrow", None),
            P("wide", None),
            P("wide", None),
            P("wide"),
            P(None, ("wide", "narrow"), None),
            P(None, ("wide", "narrow"), None),
            P(None, ("wide", "narrow"), None),
            P(None, ("wide", "narrow"), None),
            P(None, None, ("wide", "narrow")),
            P(None, None, ("wide", "narrow")),
            P(None, ("wide", "narrow")),
        ),
        out_specs=(
            P("wide", "narrow", None),
            P("wide", "narrow", None),
            P("wide", "narrow", None),
            P("wide", "narrow", None),
            P(None, "wide", "narrow"),
            P(None, "wide", "narrow"),
            P(None, "wide", "narrow"),
            P(None, "wide", "narrow"),
            P(None, None, ("wide", "narrow")),
            P(None, None, ("wide", "narrow")),
            P(None, ("wide", "narrow")),
            P(),
        ),
        check_vma=False,
    )
```

time: 527 us -> 425 us (0.81)
  Pallas kernels: 3.17 us -> 151 us
  matrix products: 109 us -> 0 us
  local copies, waits for them, and re-layouts: 91.5 us -> 15.7 us
  other arithmetic: 97.8 us -> 25.3 us
  waiting for transfers between devices: 84.3 us -> 111 us
  starting transfers between devices: 132 us -> 118 us
    pallas_call x3 -> x23, Pallas kernels: 3.17 us -> 151 us  [the longest x3 22.3 us: products(): pl.pallas_call(functools.partial(product_kernel, step), grid_spec=grid_sp...]
    dot_general x22 -> x0, matrix products: 104 us -> none  [the longest x6 30.5 us: matmul(): return jnp.dot(left, right, preferred_element_type=F32)]
    ppermute x66 -> x37, starting transfers between devices: 72.7 us -> 36.3 us  [flip(): return lax.ppermute(x, axis, [(i, i ^ mask) for i in range(size)])]
    ppermute x0 -> x21, waiting for transfers between devices: none -> 30.8 us  [flip_both(): return lax.ppermute(x, BOTH, [(i, i ^ mask) for i in range(wide * narrow)])]
    ppermute x0 -> x21, starting transfers between devices: none -> 24.8 us  [flip_both(): return lax.ppermute(x, BOTH, [(i, i ^ mask) for i in range(wide * narrow)])]
    slice x29 -> x5, local copies, waits for them, and re-layouts: 25 us -> 0.17 us  [the longest x1 0.13 us: finish_qkv(): p[:, :cols]]
    convert_element_type x17 -> x0, local copies, waits for them, and re-layouts: 24.7 us -> none  [the longest x14 21.5 us: halve(): got = flip(pick(x, 1 - bit, dim).astype(BF), axis, mask)]
    ppermute x66 -> x37, waiting for transfers between devices: 60 us -> 35.8 us  [flip(): return lax.ppermute(x, axis, [(i, i ^ mask) for i in range(size)])]
  transfers between devices with their start and end apart: 84 -> 70, of which waited for: 25 -> 27; matrix products, arithmetic and copies ran while one was open for 40% -> 7% of each run, Pallas kernels for 1% -> 29%
where the time goes in v2:
time: 425 us; the launch traced here: 423 us
  Pallas kernels  151 us (36%)
  starting transfers between devices  118 us (28%)
  waiting for transfers between devices  111 us (26%)
  other arithmetic  25.3 us (6%)
  local copies, waits for them, and re-layouts  15.7 us (4%)
    ppermute x37, starting transfers between devices, flip(): return lax.ppermute(x, axis, [(i, i ^ mask) for i in range(size)])  36.3 us
    ppermute x37, waiting for transfers between devices, flip(): return lax.ppermute(x, axis, [(i, i ^ mask) for i in range(size)])  35.8 us
    ppermute x21, waiting for transfers between devices, flip_both(): return lax.ppermute(x, BOTH, [(i, i ^ mask) for i in range(wide * narrow)])  30.8 us
    ppermute x21, starting transfers between devices, flip_both(): return lax.ppermute(x, BOTH, [(i, i ^ mask) for i in range(wide * narrow)])  24.8 us
    pallas_call x3, Pallas kernels, products(): pl.pallas_call(functools.partial(product_kernel, step), grid_spec=grid_sp...  22.3 us
    pallas_call x1, Pallas kernels, attend_back(): pl.pallas_call(attend_back_kernel, grid=(d // width,), in_specs=[pl.Block...  19.7 us
    all_to_all x2, starting transfers between devices, row_pieces(): lax.all_to_all(row.reshape(place.narrow, -1, row.shape[-1]), 'narrow', 0,...  19.3 us
    all_to_all x1, waiting for transfers between devices, body(): small = lax.all_to_all(small, BOTH, 0, 0, tiled=True)  18.2 us
  transfers between devices with their start and end apart: 70, of which 27 were waited for; matrix products, arithmetic and copies ran while one was open for 7% of the time, Pallas kernels for 29%

profile of v2, /device:TPU:0, one launch (start us, length us, event | category | flops | bytes accessed | tf_op | source)
XLA Modules:
  0.0 422.7 jit_solution(8273553788739862000)
XLA Ops:
  2.0 4.9 %collective-permute-start.3 = (bf16[128,768]{1,0:T(8,128)(2,1)S(1)}, bf16[128,768]{1,0:T(8,128)(2,1)S(1)}, u32[]{:S(2)}, u32[]{:S(2)}) collective-permute-start(bf16[128,768]{1,0:T(8,128)(2,1)S(1)} %get-tuple-element.415), channel_id=1, source_target_pairs={{0,8},{8,0},{4,12},{12,4},{1,9},{9,1},{5,13},{13,5},{2,10},{10,2},... | collective-permute-start | bytes 589832 | tf_op jit(solution)/shard_map/ppermute | solution.py:67
  10.0 3.0 collective-permute-start.1
  20.6 4.3 %collective-permute-start.5 = (bf16[128,768]{1,0:T(8,128)(2,1)S(1)}, bf16[128,768]{1,0:T(8,128)(2,1)S(1)}, u32[]{:S(2)}, u32[]{:S(2)}) collective-permute-start(bf16[128,768]{1,0:T(8,128)(2,1)S(1)} %get-tuple-element.417), channel_id=1, source_target_pairs={{0,24},{24,0},{4,28},{28,4},{1,25},{25,1},{5,29},{29,5},{2,26},{26... | collective-permute-start | bytes 589832 | tf_op jit(solution)/shard_map/ppermute | solution.py:67
  25.1 5.4 %collective-permute-done.5 = bf16[128,768]{1,0:T(8,128)(2,1)S(1)} collective-permute-done((bf16[128,768]{1,0:T(8,128)(2,1)S(1)}, bf16[128,768]{1,0:T(8,128)(2,1)S(1)}, u32[]{:S(2)}, u32[]{:S(2)}) %collective-permute-start.5) | collective-permute-done | bytes 196640 | tf_op jit(solution)/shard_map/ppermute | solution.py:67
  30.9 2.5 collective-permute-start.10
  36.3 3.5 all-to-all-start
  39.8 3.1 collective-permute-start.6
  43.5 3.7 collective-permute-done.10
  47.4 15.1 %collective-permute-done.6.refs_1_ = bf16[4,24,2304]{2,1,0:T(8,128)(2,1)S(1)} collective-permute-done((bf16[4,24,2304]{2,1,0:T(8,128)(2,1)S(1)}, bf16[4,24,2304]{2,1,0:T(8,128)(2,1)S(1)}, u32[]{:S(2)}, u32[]{:S(2)}) %collective-permute-start.6) | collective-permute-done | bytes 442400 | tf_op jit(solution)/shard_map/ppermute | solution.py:51
  62.5 8.0 %collective-permute-done.7.refs_2_ = bf16[4,24,2304]{2,1,0:T(8,128)(2,1)} collective-permute-done((bf16[4,24,2304]{2,1,0:T(8,128)(2,1)S(1)}, bf16[4,24,2304]{2,1,0:T(8,128)(2,1)}, u32[]{:S(2)}, u32[]{:S(2)}) %collective-permute-start.7) | collective-permute-done | bytes 442400 | tf_op jit(solution)/shard_map/ppermute | solution.py:51
  80.0 3.3 all-to-all-start.1
  87.6 4.7 %shard_map.238 = bf16[3,32,24,768]{3,2,1,0:T(8,128)(2,1)} custom-call(s32[1]{0:T(128)} %bitcast.25.me_ref, bf16[4,24,2304]{2,1,0:T(8,128)(2,1)} %copy-done.9, bf16[4,24,2304]{2,1,0:T(8,128)(2,1)} %copy-done.34, bf16[4,24,2304]{2,1,0:T(8,128)(2,1)} %collective-permute-done.7.refs_2_, bf16[4,24,2304]{2,1,0:T(8,128)(2,1)} %collective-permute-done.8.refs_3_, ...), custom_call_target="tpu_custom_call" | custom-call | flops 5750000128 | bytes 1024 | tf_op jit(solution)/shard_map/pallas_call | solution.py:148
  92.3 18.2 %all-to-all-done.1 = bf16[32,2,192]{2,1,0:T(2,128)(2,1)S(1)} async-done(((bf16[32,2,192]{2,1,0:T(2,128)(2,1)}), bf16[32,2,192]{2,1,0:T(2,128)(2,1)S(1)}, u32[]{:S(2)}, u32[]{:S(2)}) %all-to-all-start.1) | async-done | bytes 24608 | tf_op jit(solution)/shard_map/all_to_all | solution.py:945
  115.5 11.2 %shard_map.240 = (bf16[3,512,768]{2,1,0:T(8,128)(2,1)}, bf16[512,768]{1,0:T(8,128)(2,1)}, f32[3,4,512]{2,1,0:T(4,128)}) custom-call(bf16[512,768]{1,0:T(8,128)(2,1)} %bitcast.126, bf16[3,768,768]{2,1,0:T(8,128)(2,1)} %bitcast.161, f32[8,768]{1,0:T(8,128)} %get-tuple-element.223.rows_ref.rows, s32[1,512]{1,0:T(1,128)} %bitcast.150, s32[512,1]{1,0:T(8,128)} %copy.67.seg_col_ref), custom_call_target="tpu_custom_call" | custom-call | flops 12650000384 | bytes 1024 | tf_op jit(solution)/shard_map/pallas_call | solution.py:483
  130.1 5.2 %collective-permute-done.21 = bf16[96,768]{1,0:T(8,128)(2,1)S(1)} collective-permute-done((bf16[96,768]{1,0:T(8,128)(2,1)S(1)}, bf16[96,768]{1,0:T(8,128)(2,1)S(1)}, u32[]{:S(2)}, u32[]{:S(2)}) %collective-permute-start.21) | collective-permute-done | bytes 147488 | tf_op jit(solution)/shard_map/ppermute | solution.py:45
  145.6 3.8 all-to-all-start.2
  149.4 6.7 %shard_map.241 = (bf16[1,32,24,768]{3,2,1,0:T(8,128)(2,1)}, bf16[4,32,24,768]{3,2,1,0:T(8,128)(2,1)}) custom-call(s32[1]{0:T(128)} %bitcast.25.me_ref, bf16[4,24,3840]{2,1,0:T(8,128)(2,1)} %copy-done.7, bf16[4,24,3840]{2,1,0:T(8,128)(2,1)} %copy-done.23, bf16[4,24,3840]{2,1,0:T(8,128)(2,1)} %collective-permute-done.17.refs_2_, ...), custom_call_target="tpu_custom_call" | custom-call | flops 5750000128 | bytes 1024 | tf_op jit(solution)/shard_map/pallas_call | solution.py:148
  156.1 5.3 %shard_map.242 = (f32[512,768]{1,0:T(8,128)}, bf16[512,768]{1,0:T(8,128)(2,1)}, f32[512,768]{1,0:T(8,128)}, f32[512,1]{1,0:T(8,128)}, f32[2,128]{1,0:T(2,128)}) custom-call(bf16[512,768]{1,0:T(8,128)(2,1)} %get-tuple-element.206.ctx.refs_0_, bf16[1,768,768]{2,1,0:T(8,128)(2,1)} %bitcast.166, bf16[512,768]{1,0:T(8,128)(2,1)} %bitcast.127, ...), custom_call_target="tpu_custom_call" | custom-call | flops 5750000128 | bytes 1024 | tf_op jit(solution)/shard_map/pallas_call | solution.py:649
  161.4 8.3 %shard_map.243 = (bf16[512,3072]{1,0:T(8,128)(2,1)}, bf16[512,3072]{1,0:T(8,128)(2,1)}) custom-call(bf16[512,768]{1,0:T(8,128)(2,1)} %get-tuple-element.225.x_ref.refs_2_, bf16[4,768,768]{2,1,0:T(8,128)(2,1)} %bitcast.157, f32[1,3072]{1,0:T(1,128)} %get-tuple-element.227.bias_ref), custom_call_target="tpu_custom_call" | custom-call | flops 9200000000 | bytes 1024 | tf_op jit(solution)/shard_map/pallas_call | solution.py:584
  172.3 3.5 all-to-all-start.3
  175.8 5.0 %shard_map.244 = bf16[1,32,96,768]{3,2,1,0:T(8,128)(2,1)} custom-call(s32[1]{0:T(128)} %bitcast.25.me_ref, bf16[4,96,768]{2,1,0:T(8,128)(2,1)} %copy-done.8, bf16[4,96,768]{2,1,0:T(8,128)(2,1)} %copy-done.30, bf16[4,96,768]{2,1,0:T(8,128)(2,1)} %collective-permute-done.27.refs_2_, bf16[4,96,768]{2,1,0:T(8,128)(2,1)} %collective-permute-done.28.refs_3_, ...), custom_call_target="tpu_custom_call" | custom-call | flops 5750000128 | bytes 1024 | tf_op jit(solution)/shard_map/pallas_call | solution.py:148
  180.8 9.1 %shard_map.245 = (bf16[512,768]{1,0:T(8,128)(2,1)}, f32[512,768]{1,0:T(8,128)}, f32[512,1]{1,0:T(8,128)}, bf16[32,768]{1,0:T(8,128)(2,1)}, f32[3,128]{1,0:T(4,128)}) custom-call(bf16[512,3072]{1,0:T(8,128)(2,1)} %get-tuple-element.232.active.refs_0_, bf16[3072,768]{1,0:T(8,128)(2,1)} %bitcast.159, f32[512,768]{1,0:T(8,128)} %get-tuple-element.237.normed, ...), custom_call_target="tpu_custom_call" | custom-call | flops 10350000128 | bytes 1024 | tf_op jit(solution)/shard_map/pallas_call | solution.py:685
  189.9 3.5 collective-permute-start.33
  196.2 2.6 collective-permute-done.34
  199.6 2.7 collective-permute-start.36
  209.0 2.6 shard_map.246.pool
  211.6 5.9 %shard_map.247 = (f32[512,768]{1,0:T(8,128)}, bf16[512,768]{1,0:T(8,128)(2,1)}, bf16[4,512,192]{2,1,0:T(8,128)(2,1)}, f32[3,768]{1,0:T(4,128)}) custom-call(bf16[512,768]{1,0:T(8,128)(2,1)} %bitcast.129, f32[512,1]{1,0:T(8,128)} %compare_convert_fusion.valid, f32[32,512]{1,0:T(8,128)} %fusion.21.hot, f32[32,768]{1,0:T(8,128)} %shard_map.246.pool, ...), custom_call_target="tpu_custom_call" | custom-call | flops 6899999744 | bytes 1024 | tf_op jit(solution)/shard_map/pallas_call | solution.py:719
  217.5 7.2 %shard_map.248 = (bf16[2,8,192,384]{3,2,1,0:T(8,128)(2,1)}, bf16[2,8,192,384]{3,2,1,0:T(8,128)(2,1)}) custom-call(s32[1]{0:T(128)} %bitcast.me_ref, bf16[512,3072]{1,0:T(8,128)(2,1)} %get-tuple-element.232.active.refs_0_, bf16[4,512,192]{2,1,0:T(8,128)(2,1)} %get-tuple-element.247.refs_1_), custom_call_target="tpu_custom_call" | custom-call | flops 9200000000 | bytes 1024 | tf_op jit(solution)/shard_map/pallas_call | solution.py:335
  225.4 15.6 %all-to-all-start.4 = ((bf16[4,128,768]{2,1,0:T(8,128)(2,1)}), bf16[4,128,768]{2,1,0:T(8,128)(2,1)S(1)}, u32[]{:S(2)}, u32[]{:S(2)}) async-start(bf16[4,128,768]{2,1,0:T(8,128)(2,1)} %bitcast.52), calls=%async_computation.4 | async-start | bytes 1572864 | tf_op jit(solution)/shard_map/all_to_all | solution.py:108
  242.4 5.1 %shard_map.249 = (f32[4,192,384]{2,1,0:T(8,128)}, bf16[4,192,384]{2,1,0:T(8,128)(2,1)}, bf16[4,192,384]{2,1,0:T(8,128)(2,1)}, bf16[4,192,384]{2,1,0:T(8,128)(2,1)}) custom-call(s32[2]{0:T(128)} %pad_add_fusion.1.at_ref, bf16[2,4,2,192,384]{4,3,2,1,0:T(8,128)(2,1)} %bitcast.164, bf16[2,4,2,192,384]{4,3,2,1,0:T(8,128)(2,1)} %bitcast.155), custom_call_target="tpu_custom_call" | custom-call | flops 6899999744 | bytes 1024 | tf_op jit(solution)/shard_map/pallas_call | solution.py:256
  251.0 14.1 %shard_map.250 = (bf16[512,3072]{1,0:T(8,128)(2,1)}, f32[1,3072]{1,0:T(1,128)}, f32[512,768]{1,0:T(8,128)}, bf16[512,768]{1,0:T(8,128)(2,1)}, bf16[4,512,192]{2,1,0:T(8,128)(2,1)}, /*index=5*/f32[3,768]{1,0:T(4,128)}) custom-call(bf16[512,768]{1,0:T(8,128)(2,1)} %get-tuple-element.257.low, bf16[3072,768]{1,0:T(8,128)(2,1)} %bitcast.160, ...), custom_call_target="tpu_custom_call" | custom-call | flops 16099999744 | bytes 1024 | tf_op jit(solution)/shard_map/pallas_call | solution.py:761
  265.1 8.4 %shard_map.251 = (bf16[2,8,120,768]{3,2,1,0:T(8,128)(2,1)}, bf16[2,8,120,768]{3,2,1,0:T(8,128)(2,1)}) custom-call(s32[1]{0:T(128)} %bitcast.me_ref, bf16[512,768]{1,0:T(8,128)(2,1)} %get-tuple-element.206.ctx.refs_0_, bf16[4,512,192]{2,1,0:T(8,128)(2,1)} %get-tuple-element.262.refs_1_, bf16[512,768]{1,0:T(8,128)(2,1)} %get-tuple-element.225.x_ref.refs_2_, ...), custom_call_target="tpu_custom_call" | custom-call | flops 9200000000 | bytes 1024 | tf_op jit(solution)/shard_map/pallas_call | solution.py:335
  273.6 4.4 %collective-permute-done.42.refs_1_ = bf16[4,192,384]{2,1,0:T(8,128)(2,1)S(1)} collective-permute-done((bf16[4,192,384]{2,1,0:T(8,128)(2,1)}, bf16[4,192,384]{2,1,0:T(8,128)(2,1)S(1)}, u32[]{:S(2)}, u32[]{:S(2)}) %collective-permute-start.42) | collective-permute-done | bytes 589856 | tf_op jit(solution)/shard_map/ppermute | solution.py:51
  279.1 2.8 shard_map.253
  283.8 5.7 %shard_map.252 = (f32[4,120,768]{2,1,0:T(8,128)}, bf16[4,120,768]{2,1,0:T(8,128)(2,1)}, bf16[4,120,768]{2,1,0:T(8,128)(2,1)}, bf16[4,120,768]{2,1,0:T(8,128)(2,1)}) custom-call(s32[2]{0:T(128)} %pad_add_fusion.1.at_ref, bf16[2,4,2,120,768]{4,3,2,1,0:T(8,128)(2,1)} %bitcast.163, bf16[2,4,2,120,768]{4,3,2,1,0:T(8,128)(2,1)} %bitcast.53.got_ref), custom_call_target="tpu_custom_call" | custom-call | flops 6899999744 | bytes 1024 | tf_op jit(solution)/shard_map/pallas_call | solution.py:256
  290.5 3.5 all-to-all-start.5
  301.9 19.7 %shard_map.254 = (bf16[3,512,768]{2,1,0:T(8,128)(2,1)}, bf16[4,512,576]{2,1,0:T(8,128)(2,1)}, f32[2,768]{1,0:T(2,128)}) custom-call(bf16[512,768]{1,0:T(8,128)(2,1)} %get-tuple-element.286.gb_ref, bf16[768,768]{1,0:T(8,128)(2,1)} %bitcast.167, bf16[3,512,768]{2,1,0:T(8,128)(2,1)} %get-tuple-element.287.qkv_ref, f32[3,4,512]{2,1,0:T(4,128)} %get-tuple-element.288.lse_ref, ...), custom_call_target="tpu_custom_call" | custom-call | flops 23000000512 | bytes 1024 | tf_op jit(solution)/shard_map/pallas_call | solution.py:545
  321.7 6.7 %shard_map.255 = (bf16[2,8,48,1152]{3,2,1,0:T(8,128)(2,1)}, bf16[2,8,48,1152]{3,2,1,0:T(8,128)(2,1)}) custom-call(s32[1]{0:T(128)} %bitcast.me_ref, bf16[512,768]{1,0:T(8,128)(2,1)} %bitcast.128, bf16[4,512,576]{2,1,0:T(8,128)(2,1)} %get-tuple-element.290.refs_1_), custom_call_target="tpu_custom_call" | custom-call | flops 9200000000 | bytes 1024 | tf_op jit(solution)/shard_map/pallas_call | solution.py:335
  329.9 3.6 shard_map.259
  334.4 3.1 shard_map.257
  337.5 6.3 %shard_map.258 = bf16[512,768]{1,0:T(8,128)(2,1)} custom-call(bf16[3,512,768]{2,1,0:T(8,128)(2,1)} %get-tuple-element.317.grad, bf16[3,768,768]{2,1,0:T(8,128)(2,1)} %bitcast.162, f32[512,768]{1,0:T(8,128)} %get-tuple-element.318.residual), custom_call_target="tpu_custom_call" | custom-call | flops 6899999744 | bytes 1024 | tf_op jit(solution)/shard_map/pallas_call | solution.py:798
  345.0 4.8 %shard_map.256 = (f32[4,48,1152]{2,1,0:T(8,128)}, bf16[4,48,1152]{2,1,0:T(8,128)(2,1)}, bf16[4,48,1152]{2,1,0:T(8,128)(2,1)}, bf16[4,48,1152]{2,1,0:T(8,128)(2,1)}) custom-call(s32[2]{0:T(128)} %pad_add_fusion.1.at_ref, bf16[2,4,2,48,1152]{4,3,2,1,0:T(8,128)(2,1)} %bitcast.165, bf16[2,4,2,48,1152]{4,3,2,1,0:T(8,128)(2,1)} %bitcast.156), custom_call_target="tpu_custom_call" | custom-call | flops 6899999744 | bytes 1024 | tf_op jit(solution)/shard_map/pallas_call | solution.py:256
  355.0 3.7 all-to-all-start.6
  364.2 12.2 %collective-permute-done.56 = bf16[120,768]{1,0:T(8,128)(2,1)S(1)} collective-permute-done((bf16[120,768]{1,0:T(8,128)(2,1)S(1)}, bf16[120,768]{1,0:T(8,128)(2,1)S(1)}, u32[]{:S(2)}, u32[]{:S(2)}) %collective-permute-start.56) | collective-permute-done | bytes 184352 | tf_op jit(solution)/shard_map/ppermute | solution.py:45
  376.5 4.6 %all-to-all-done.6 = bf16[4,128,768]{2,1,0:T(8,128)(2,1)S(1)} async-done(((bf16[4,128,768]{2,1,0:T(8,128)(2,1)}), bf16[4,128,768]{2,1,0:T(8,128)(2,1)S(1)}, u32[]{:S(2)}, u32[]{:S(2)}) %all-to-all-start.6) | async-done | bytes 786464 | tf_op jit(solution)/shard_map/all_to_all | solution.py:108
  382.1 4.4 %all-to-all-start.8 = ((f32[32,1,384]{2,1,0:T(1,128)}), f32[32,1,384]{2,1,0:T(1,128)S(1)}, u32[]{:S(2)}, u32[]{:S(2)}) async-start(f32[32,1,384]{2,1,0:T(1,128)} %copy.74), calls=%async_computation.8 | async-start | bytes 98304 | tf_op jit(solution)/shard_map/all_to_all | solution.py:1098
  396.2 4.9 %all-to-all-start.7 = ((bf16[4,128,768]{2,1,0:T(8,128)(2,1)}), bf16[4,128,768]{2,1,0:T(8,128)(2,1)S(1)}, u32[]{:S(2)}, u32[]{:S(2)}) async-start(bf16[4,128,768]{2,1,0:T(8,128)(2,1)} %broadcast_select_fusion), calls=%async_computation.7 | async-start | bytes 1572864 | tf_op jit(solution)/shard_map/all_to_all | solution.py:60
  405.2 15.7 %all-to-all-done.7 = bf16[4,128,768]{2,1,0:T(8,128)(2,1)S(1)} async-done(((bf16[4,128,768]{2,1,0:T(8,128)(2,1)}), bf16[4,128,768]{2,1,0:T(8,128)(2,1)S(1)}, u32[]{:S(2)}, u32[]{:S(2)}) %all-to-all-start.7) | async-done | bytes 786464 | tf_op jit(solution)/shard_map/all_to_all | solution.py:60
  (317 shorter events, 109.0 us)
Async XLA Ops:
  2.0 23.1 %collective-permute-start.3 = (bf16[128,768]{1,0:T(8,128)(2,1)S(1)}, bf16[128,768]{1,0:T(8,128)(2,1)S(1)}, u32[]{:S(2)}, u32[]{:S(2)}) collective-permute-start(bf16[128,768]{1,0:T(8,128)(2,1)S(1)} %get-tuple-element.415), channel_id=1, source_target_pairs={{0,8},{8,0},{4,12},{12,4},{1,9},{9,1},{5,13},{13,5},{2,10},{10,2},... | collective-permute-start | bytes 589832 | tf_op jit(solution)/shard_map/ppermute | solution.py:67
  6.9 18.2 %collective-permute-start.4 = (bf16[128,768]{1,0:T(8,128)(2,1)S(1)}, bf16[128,768]{1,0:T(8,128)(2,1)S(1)}, u32[]{:S(2)}, u32[]{:S(2)}) collective-permute-start(bf16[128,768]{1,0:T(8,128)(2,1)S(1)} %get-tuple-element.416), channel_id=1, source_target_pairs={{0,16},{16,0},{4,20},{20,4},{1,17},{17,1},{5,21},{21,5},{2,18},{18... | collective-permute-start | bytes 589832 | tf_op jit(solution)/shard_map/ppermute | solution.py:67
  9.9 10.8 %collective-permute-start = (bf16[24,2304]{1,0:T(8,128)(2,1)S(1)}, bf16[24,2304]{1,0:T(8,128)(2,1)S(1)}, u32[]{:S(2)}, u32[]{:S(2)}) collective-permute-start(bf16[24,2304]{1,0:T(8,128)(2,1)S(1)} %get-tuple-element.437), channel_id=1, source_target_pairs={{0,8},{4,12},{8,0},{12,4},{16,24},{20,28},{24,16},{28,20},{1,9},{5... | collective-permute-start | bytes 331784 | tf_op jit(solution)/shard_map/ppermute | solution.py:45
  10.0 15.0 %collective-permute-start.1 = (bf16[24,2304]{1,0:T(8,128)(2,1)S(1)}, bf16[24,2304]{1,0:T(8,128)(2,1)S(1)}, u32[]{:S(2)}, u32[]{:S(2)}) collective-permute-start(bf16[24,2304]{1,0:T(8,128)(2,1)S(1)} %get-tuple-element.435), channel_id=1, source_target_pairs={{0,16},{4,20},{8,24},{12,28},{16,0},{20,4},{24,8},{28,12},{1,17},{... | collective-permute-start | bytes 331784 | tf_op jit(solution)/shard_map/ppermute | solution.py:45
  12.9 12.1 %collective-permute-start.2 = (bf16[24,2304]{1,0:T(8,128)(2,1)S(1)}, bf16[24,2304]{1,0:T(8,128)(2,1)S(1)}, u32[]{:S(2)}, u32[]{:S(2)}) collective-permute-start(bf16[24,2304]{1,0:T(8,128)(2,1)S(1)} %get-tuple-element.436), channel_id=1, source_target_pairs={{0,24},{4,28},{8,16},{12,20},{16,8},{20,12},{24,0},{28,4},{1,25},{... | collective-permute-start | bytes 331784 | tf_op jit(solution)/shard_map/ppermute | solution.py:45
  20.6 9.9 %collective-permute-start.5 = (bf16[128,768]{1,0:T(8,128)(2,1)S(1)}, bf16[128,768]{1,0:T(8,128)(2,1)S(1)}, u32[]{:S(2)}, u32[]{:S(2)}) collective-permute-start(bf16[128,768]{1,0:T(8,128)(2,1)S(1)} %get-tuple-element.417), channel_id=1, source_target_pairs={{0,24},{24,0},{4,28},{28,4},{1,25},{25,1},{5,29},{29,5},{2,26},{26... | collective-permute-start | bytes 589832 | tf_op jit(solution)/shard_map/ppermute | solution.py:67
  30.7 12.3 %collective-permute-start.9 = (bf16[24,3840]{1,0:T(8,128)(2,1)S(1)}, bf16[24,3840]{1,0:T(8,128)(2,1)S(1)}, u32[]{:S(2)}, u32[]{:S(2)}) collective-permute-start(bf16[24,3840]{1,0:T(8,128)(2,1)S(1)} %get-tuple-element.425), channel_id=1, source_target_pairs={{0,8},{4,12},{8,0},{12,4},{16,24},{20,28},{24,16},{28,20},{1,9},{5... | collective-permute-start | bytes 552968 | tf_op jit(solution)/shard_map/ppermute | solution.py:45
  30.9 16.4 %collective-permute-start.10 = (bf16[24,3840]{1,0:T(8,128)(2,1)S(1)}, bf16[24,3840]{1,0:T(8,128)(2,1)S(1)}, u32[]{:S(2)}, u32[]{:S(2)}) collective-permute-start(bf16[24,3840]{1,0:T(8,128)(2,1)S(1)} %get-tuple-element.423), channel_id=1, source_target_pairs={{0,16},{4,20},{8,24},{12,28},{16,0},{20,4},{24,8},{28,12},{1,17},{... | collective-permute-start | bytes 552968 | tf_op jit(solution)/shard_map/ppermute | solution.py:45
  33.3 14.0 %collective-permute-start.11 = (bf16[24,3840]{1,0:T(8,128)(2,1)S(1)}, bf16[24,3840]{1,0:T(8,128)(2,1)S(1)}, u32[]{:S(2)}, u32[]{:S(2)}) collective-permute-start(bf16[24,3840]{1,0:T(8,128)(2,1)S(1)} %get-tuple-element.424), channel_id=1, source_target_pairs={{0,24},{4,28},{8,16},{12,20},{16,8},{20,12},{24,0},{28,4},{1,25},{... | collective-permute-start | bytes 552968 | tf_op jit(solution)/shard_map/ppermute | solution.py:45
  36.3 34.2 %all-to-all-start = ((bf16[4,128,768]{2,1,0:T(8,128)(2,1)}), bf16[4,128,768]{2,1,0:T(8,128)(2,1)S(1)}, u32[]{:S(2)}, u32[]{:S(2)}) async-start(bf16[4,128,768]{2,1,0:T(8,128)(2,1)} %maximum_select_fusion), calls=%async_computation | async-start | bytes 1572864 | tf_op jit(solution)/shard_map/all_to_all | solution.py:103
  39.8 22.8 %collective-permute-start.6 = (bf16[4,24,2304]{2,1,0:T(8,128)(2,1)S(1)}, bf16[4,24,2304]{2,1,0:T(8,128)(2,1)S(1)}, u32[]{:S(2)}, u32[]{:S(2)}) collective-permute-start(bf16[4,24,2304]{2,1,0:T(8,128)(2,1)S(1)} %pad_maximum_fusion.6.refs_0_), channel_id=1, source_target_pairs={{0,6},{1,7},{2,4},{3,5},{4,2},{5,3},{6,0},{7,1},{8,14},{9,15},{10,... | collective-permute-start | bytes 1327112 | tf_op jit(solution)/shard_map/ppermute | solution.py:51
  42.9 27.6 %collective-permute-start.7 = (bf16[4,24,2304]{2,1,0:T(8,128)(2,1)S(1)}, bf16[4,24,2304]{2,1,0:T(8,128)(2,1)}, u32[]{:S(2)}, u32[]{:S(2)}) collective-permute-start(bf16[4,24,2304]{2,1,0:T(8,128)(2,1)S(1)} %pad_maximum_fusion.6.refs_0_), channel_id=1, source_target_pairs={{0,2},{1,3},{2,0},{3,1},{4,6},{5,7},{6,4},{7,5},{8,10},{9,11},{10,... | collective-permute-start | bytes 1327112 | tf_op jit(solution)/shard_map/ppermute | solution.py:51
  43.1 27.4 %collective-permute-start.8 = (bf16[4,24,2304]{2,1,0:T(8,128)(2,1)S(1)}, bf16[4,24,2304]{2,1,0:T(8,128)(2,1)}, u32[]{:S(2)}, u32[]{:S(2)}) collective-permute-start(bf16[4,24,2304]{2,1,0:T(8,128)(2,1)S(1)} %pad_maximum_fusion.6.refs_0_), channel_id=1, source_target_pairs={{0,4},{1,5},{2,6},{3,7},{4,0},{5,1},{6,2},{7,3},{8,12},{9,13},{10,... | collective-permute-start | bytes 1327112 | tf_op jit(solution)/shard_map/ppermute | solution.py:51
  74.6 60.8 %collective-permute-start.16 = (bf16[4,24,3840]{2,1,0:T(8,128)(2,1)S(1)}, bf16[4,24,3840]{2,1,0:T(8,128)(2,1)S(1)}, u32[]{:S(2)}, u32[]{:S(2)}) collective-permute-start(bf16[4,24,3840]{2,1,0:T(8,128)(2,1)S(1)} %pad_maximum_fusion.1.refs_0_), channel_id=1, source_target_pairs={{0,6},{1,7},{2,4},{3,5},{4,2},{5,3},{6,0},{7,1},{8,14},{9,15},{10,... | collective-permute-start | bytes 2211848 | tf_op jit(solution)/shard_map/ppermute | solution.py:51
  76.1 59.3 %collective-permute-start.17 = (bf16[4,24,3840]{2,1,0:T(8,128)(2,1)S(1)}, bf16[4,24,3840]{2,1,0:T(8,128)(2,1)}, u32[]{:S(2)}, u32[]{:S(2)}) collective-permute-start(bf16[4,24,3840]{2,1,0:T(8,128)(2,1)S(1)} %pad_maximum_fusion.1.refs_0_), channel_id=1, source_target_pairs={{0,2},{1,3},{2,0},{3,1},{4,6},{5,7},{6,4},{7,5},{8,10},{9,11},{10,... | collective-permute-start | bytes 2211848 | tf_op jit(solution)/shard_map/ppermute | solution.py:51
  77.8 57.6 %collective-permute-start.18 = (bf16[4,24,3840]{2,1,0:T(8,128)(2,1)S(1)}, bf16[4,24,3840]{2,1,0:T(8,128)(2,1)}, u32[]{:S(2)}, u32[]{:S(2)}) collective-permute-start(bf16[4,24,3840]{2,1,0:T(8,128)(2,1)S(1)} %pad_maximum_fusion.1.refs_0_), channel_id=1, source_target_pairs={{0,4},{1,5},{2,6},{3,7},{4,0},{5,1},{6,2},{7,3},{8,12},{9,13},{10,... | collective-permute-start | bytes 2211848 | tf_op jit(solution)/shard_map/ppermute | solution.py:51
  80.0 30.6 %all-to-all-start.1 = ((bf16[32,2,192]{2,1,0:T(2,128)(2,1)}), bf16[32,2,192]{2,1,0:T(2,128)(2,1)S(1)}, u32[]{:S(2)}, u32[]{:S(2)}) async-start(bf16[32,2,192]{2,1,0:T(2,128)(2,1)} %reshape.373), calls=%async_computation.1 | async-start | bytes 65536 | tf_op jit(solution)/shard_map/all_to_all | solution.py:945
  83.4 44.1 %collective-permute-start.19 = (bf16[96,768]{1,0:T(8,128)(2,1)S(1)}, bf16[96,768]{1,0:T(8,128)(2,1)S(1)}, u32[]{:S(2)}, u32[]{:S(2)}) collective-permute-start(bf16[96,768]{1,0:T(8,128)(2,1)S(1)} %get-tuple-element.429), channel_id=1, source_target_pairs={{0,8},{4,12},{8,0},{12,4},{16,24},{20,28},{24,16},{28,20},{1,9},{5... | collective-permute-start | bytes 442376 | tf_op jit(solution)/shard_map/ppermute | solution.py:45
  85.2 44.9 %collective-permute-start.20 = (bf16[96,768]{1,0:T(8,128)(2,1)S(1)}, bf16[96,768]{1,0:T(8,128)(2,1)S(1)}, u32[]{:S(2)}, u32[]{:S(2)}) collective-permute-start(bf16[96,768]{1,0:T(8,128)(2,1)S(1)} %get-tuple-element.427), channel_id=1, source_target_pairs={{0,16},{4,20},{8,24},{12,28},{16,0},{20,4},{24,8},{28,12},{1,17},{... | collective-permute-start | bytes 442376 | tf_op jit(solution)/shard_map/ppermute | solution.py:45
  141.1 28.6 %collective-permute-start.26 = (bf16[4,96,768]{2,1,0:T(8,128)(2,1)S(1)}, bf16[4,96,768]{2,1,0:T(8,128)(2,1)S(1)}, u32[]{:S(2)}, u32[]{:S(2)}) collective-permute-start(bf16[4,96,768]{2,1,0:T(8,128)(2,1)S(1)} %pad_maximum_fusion.2.refs_0_), channel_id=1, source_target_pairs={{0,6},{1,7},{2,4},{3,5},{4,2},{5,3},{6,0},{7,1},{8,14},{9,15},{10,... | collective-permute-start | bytes 1769480 | tf_op jit(solution)/shard_map/ppermute | solution.py:51
  142.3 27.8 %collective-permute-start.27 = (bf16[4,96,768]{2,1,0:T(8,128)(2,1)S(1)}, bf16[4,96,768]{2,1,0:T(8,128)(2,1)}, u32[]{:S(2)}, u32[]{:S(2)}) collective-permute-start(bf16[4,96,768]{2,1,0:T(8,128)(2,1)S(1)} %pad_maximum_fusion.2.refs_0_), channel_id=1, source_target_pairs={{0,2},{1,3},{2,0},{3,1},{4,6},{5,7},{6,4},{7,5},{8,10},{9,11},{10,... | collective-permute-start | bytes 1769480 | tf_op jit(solution)/shard_map/ppermute | solution.py:51
  144.0 26.1 %collective-permute-start.28 = (bf16[4,96,768]{2,1,0:T(8,128)(2,1)S(1)}, bf16[4,96,768]{2,1,0:T(8,128)(2,1)}, u32[]{:S(2)}, u32[]{:S(2)}) collective-permute-start(bf16[4,96,768]{2,1,0:T(8,128)(2,1)S(1)} %pad_maximum_fusion.2.refs_0_), channel_id=1, source_target_pairs={{0,4},{1,5},{2,6},{3,7},{4,0},{5,1},{6,2},{7,3},{8,12},{9,13},{10,... | collective-permute-start | bytes 1769480 | tf_op jit(solution)/shard_map/ppermute | solution.py:51
  145.6 24.5 %all-to-all-start.2 = ((bf16[4,128,768]{2,1,0:T(8,128)(2,1)}), bf16[4,128,768]{2,1,0:T(8,128)(2,1)S(1)}, u32[]{:S(2)}, u32[]{:S(2)}) async-start(bf16[4,128,768]{2,1,0:T(8,128)(2,1)} %maximum_select_fusion.1), calls=%async_computation.2 | async-start | bytes 1572864 | tf_op jit(solution)/shard_map/all_to_all | solution.py:60
  172.3 17.7 %all-to-all-start.3 = ((bf16[4,128,768]{2,1,0:T(8,128)(2,1)}), bf16[4,128,768]{2,1,0:T(8,128)(2,1)S(1)}, u32[]{:S(2)}, u32[]{:S(2)}) async-start(bf16[4,128,768]{2,1,0:T(8,128)(2,1)} %maximum_select_fusion.2), calls=%async_computation.3 | async-start | bytes 1572864 | tf_op jit(solution)/shard_map/all_to_all | solution.py:103
  224.6 16.4 %collective-permute-start.40 = (bf16[2,8,192,384]{3,2,1,0:T(8,128)(2,1)}, bf16[2,8,192,384]{3,2,1,0:T(8,128)(2,1)S(1)}, u32[]{:S(2)}, u32[]{:S(2)}) collective-permute-start(bf16[2,8,192,384]{3,2,1,0:T(8,128)(2,1)} %get-tuple-element.251), channel_id=1, source_target_pairs={{0,1},{1,0},{2,3},{3,2},{4,5},{5,4},{6,7},{7,6},{8,9},{9,8},{10,11... | collective-permute-start | bytes 7077896 | tf_op jit(solution)/shard_map/ppermute | solution.py:45
  225.4 48.2 %all-to-all-start.4 = ((bf16[4,128,768]{2,1,0:T(8,128)(2,1)}), bf16[4,128,768]{2,1,0:T(8,128)(2,1)S(1)}, u32[]{:S(2)}, u32[]{:S(2)}) async-start(bf16[4,128,768]{2,1,0:T(8,128)(2,1)} %bitcast.52), calls=%async_computation.4 | async-start | bytes 1572864 | tf_op jit(solution)/shard_map/all_to_all | solution.py:108
  247.5 26.0 %collective-permute-start.41 = (bf16[4,192,384]{2,1,0:T(8,128)(2,1)}, bf16[4,192,384]{2,1,0:T(8,128)(2,1)S(1)}, u32[]{:S(2)}, u32[]{:S(2)}) collective-permute-start(bf16[4,192,384]{2,1,0:T(8,128)(2,1)} %get-tuple-element.267), channel_id=1, source_target_pairs={{0,6},{1,7},{2,4},{3,5},{4,2},{5,3},{6,0},{7,1},{8,14},{9,15},{10,... | collective-permute-start | bytes 1769480 | tf_op jit(solution)/shard_map/ppermute | solution.py:51
  249.4 28.6 %collective-permute-start.42 = (bf16[4,192,384]{2,1,0:T(8,128)(2,1)}, bf16[4,192,384]{2,1,0:T(8,128)(2,1)S(1)}, u32[]{:S(2)}, u32[]{:S(2)}) collective-permute-start(bf16[4,192,384]{2,1,0:T(8,128)(2,1)} %get-tuple-element.268), channel_id=1, source_target_pairs={{0,2},{1,3},{2,0},{3,1},{4,6},{5,7},{6,4},{7,5},{8,10},{9,11},{10,... | collective-permute-start | bytes 1769480 | tf_op jit(solution)/shard_map/ppermute | solution.py:51
  249.6 28.3 %collective-permute-start.43 = (bf16[4,192,384]{2,1,0:T(8,128)(2,1)}, bf16[4,192,384]{2,1,0:T(8,128)(2,1)S(1)}, u32[]{:S(2)}, u32[]{:S(2)}) collective-permute-start(bf16[4,192,384]{2,1,0:T(8,128)(2,1)} %get-tuple-element.269), channel_id=1, source_target_pairs={{0,4},{1,5},{2,6},{3,7},{4,0},{5,1},{6,2},{7,3},{8,12},{9,13},{10,... | collective-permute-start | bytes 1769480 | tf_op jit(solution)/shard_map/ppermute | solution.py:51
  290.5 39.4 %all-to-all-start.5 = ((bf16[4,128,768]{2,1,0:T(8,128)(2,1)}), bf16[4,128,768]{2,1,0:T(8,128)(2,1)S(1)}, u32[]{:S(2)}, u32[]{:S(2)}) async-start(bf16[4,128,768]{2,1,0:T(8,128)(2,1)} %broadcast_select_fusion.1), calls=%async_computation.5 | async-start | bytes 1572864 | tf_op jit(solution)/shard_map/all_to_all | solution.py:60
  294.0 34.7 %collective-permute-start.45 = (bf16[4,120,768]{2,1,0:T(8,128)(2,1)}, bf16[4,120,768]{2,1,0:T(8,128)(2,1)S(1)}, u32[]{:S(2)}, u32[]{:S(2)}) collective-permute-start(bf16[4,120,768]{2,1,0:T(8,128)(2,1)} %get-tuple-element.294), channel_id=1, source_target_pairs={{0,6},{1,7},{2,4},{3,5},{4,2},{5,3},{6,0},{7,1},{8,14},{9,15},{10,... | collective-permute-start | bytes 2211848 | tf_op jit(solution)/shard_map/ppermute | solution.py:51
  295.0 33.9 %collective-permute-start.46 = (bf16[4,120,768]{2,1,0:T(8,128)(2,1)}, bf16[4,120,768]{2,1,0:T(8,128)(2,1)S(1)}, u32[]{:S(2)}, u32[]{:S(2)}) collective-permute-start(bf16[4,120,768]{2,1,0:T(8,128)(2,1)} %get-tuple-element.295), channel_id=1, source_target_pairs={{0,2},{1,3},{2,0},{3,1},{4,6},{5,7},{6,4},{7,5},{8,10},{9,11},{10,... | collective-permute-start | bytes 2211848 | tf_op jit(solution)/shard_map/ppermute | solution.py:51
  296.4 33.5 %collective-permute-start.47 = (bf16[4,120,768]{2,1,0:T(8,128)(2,1)}, bf16[4,120,768]{2,1,0:T(8,128)(2,1)}, u32[]{:S(2)}, u32[]{:S(2)}) collective-permute-start(bf16[4,120,768]{2,1,0:T(8,128)(2,1)} %get-tuple-element.296), channel_id=1, source_target_pairs={{0,4},{1,5},{2,6},{3,7},{4,0},{5,1},{6,2},{7,3},{8,12},{9,13},{10,... | collective-permute-start | bytes 2211848 | tf_op jit(solution)/shard_map/ppermute | solution.py:51
  297.5 24.1 %collective-permute-start.48 = (bf16[192,384]{1,0:T(8,128)(2,1)S(1)}, bf16[192,384]{1,0:T(8,128)(2,1)S(1)}, u32[]{:S(2)}, u32[]{:S(2)}) collective-permute-start(bf16[192,384]{1,0:T(8,128)(2,1)S(1)} %copy-done.40), channel_id=1, source_target_pairs={{0,8},{4,12},{8,0},{12,4},{16,24},{20,28},{24,16},{28,20},{1,9},{5... | collective-permute-start | bytes 442376 | tf_op jit(solution)/shard_map/ppermute | solution.py:45
  299.5 29.0 %collective-permute-start.49 = (bf16[192,384]{1,0:T(8,128)(2,1)S(1)}, bf16[192,384]{1,0:T(8,128)(2,1)S(1)}, u32[]{:S(2)}, u32[]{:S(2)}) collective-permute-start(bf16[192,384]{1,0:T(8,128)(2,1)S(1)} %copy-done.39), channel_id=1, source_target_pairs={{0,16},{4,20},{8,24},{12,28},{16,0},{20,4},{24,8},{28,12},{1,17},{... | collective-permute-start | bytes 442376 | tf_op jit(solution)/shard_map/ppermute | solution.py:45
  329.9 13.9 %collective-permute-start.51 = (bf16[2,8,48,1152]{3,2,1,0:T(8,128)(2,1)}, bf16[2,8,48,1152]{3,2,1,0:T(8,128)(2,1)S(1)}, u32[]{:S(2)}, u32[]{:S(2)}) collective-permute-start(bf16[2,8,48,1152]{3,2,1,0:T(8,128)(2,1)} %get-tuple-element.304), channel_id=1, source_target_pairs={{0,1},{1,0},{2,3},{3,2},{4,5},{5,4},{6,7},{7,6},{8,9},{9,8},{10,11... | collective-permute-start | bytes 5308424 | tf_op jit(solution)/shard_map/ppermute | solution.py:45
  349.8 26.6 %collective-permute-start.52 = (bf16[4,48,1152]{2,1,0:T(8,128)(2,1)}, bf16[4,48,1152]{2,1,0:T(8,128)(2,1)}, u32[]{:S(2)}, u32[]{:S(2)}) collective-permute-start(bf16[4,48,1152]{2,1,0:T(8,128)(2,1)} %get-tuple-element.320), channel_id=1, source_target_pairs={{0,6},{1,7},{2,4},{3,5},{4,2},{5,3},{6,0},{7,1},{8,14},{9,15},{10,... | collective-permute-start | bytes 1327112 | tf_op jit(solution)/shard_map/ppermute | solution.py:51
  351.0 25.4 %collective-permute-start.53 = (bf16[4,48,1152]{2,1,0:T(8,128)(2,1)}, bf16[4,48,1152]{2,1,0:T(8,128)(2,1)}, u32[]{:S(2)}, u32[]{:S(2)}) collective-permute-start(bf16[4,48,1152]{2,1,0:T(8,128)(2,1)} %get-tuple-element.321), channel_id=1, source_target_pairs={{0,2},{1,3},{2,0},{3,1},{4,6},{5,7},{6,4},{7,5},{8,10},{9,11},{10,... | collective-permute-start | bytes 1327112 | tf_op jit(solution)/shard_map/ppermute | solution.py:51
  352.4 24.1 %collective-permute-start.54 = (bf16[4,48,1152]{2,1,0:T(8,128)(2,1)}, bf16[4,48,1152]{2,1,0:T(8,128)(2,1)}, u32[]{:S(2)}, u32[]{:S(2)}) collective-permute-start(bf16[4,48,1152]{2,1,0:T(8,128)(2,1)} %get-tuple-element.322), channel_id=1, source_target_pairs={{0,4},{1,5},{2,6},{3,7},{4,0},{5,1},{6,2},{7,3},{8,12},{9,13},{10,... | collective-permute-start | bytes 1327112 | tf_op jit(solution)/shard_map/ppermute | solution.py:51
  353.4 9.8 %collective-permute-start.55 = (bf16[120,768]{1,0:T(8,128)(2,1)}, bf16[120,768]{1,0:T(8,128)(2,1)S(1)}, u32[]{:S(2)}, u32[]{:S(2)}) collective-permute-start(bf16[120,768]{1,0:T(8,128)(2,1)} %get-tuple-element.324), channel_id=1, source_target_pairs={{0,8},{4,12},{8,0},{12,4},{16,24},{20,28},{24,16},{28,20},{1,9},{5... | collective-permute-start | bytes 552968 | tf_op jit(solution)/shard_map/ppermute | solution.py:45
  355.0 26.1 %all-to-all-start.6 = ((bf16[4,128,768]{2,1,0:T(8,128)(2,1)}), bf16[4,128,768]{2,1,0:T(8,128)(2,1)S(1)}, u32[]{:S(2)}, u32[]{:S(2)}) async-start(bf16[4,128,768]{2,1,0:T(8,128)(2,1)} %bitcast.61), calls=%async_computation.6 | async-start | bytes 1572864 | tf_op jit(solution)/shard_map/all_to_all | solution.py:108
  360.7 15.7 %collective-permute-start.56 = (bf16[120,768]{1,0:T(8,128)(2,1)S(1)}, bf16[120,768]{1,0:T(8,128)(2,1)S(1)}, u32[]{:S(2)}, u32[]{:S(2)}) collective-permute-start(bf16[120,768]{1,0:T(8,128)(2,1)S(1)} %copy-done.37), channel_id=1, source_target_pairs={{0,16},{4,20},{8,24},{12,28},{16,0},{20,4},{24,8},{28,12},{1,17},{... | collective-permute-start | bytes 552968 | tf_op jit(solution)/shard_map/ppermute | solution.py:45
  363.2 13.3 %collective-permute-start.57 = (bf16[120,768]{1,0:T(8,128)(2,1)S(1)}, bf16[120,768]{1,0:T(8,128)(2,1)S(1)}, u32[]{:S(2)}, u32[]{:S(2)}) collective-permute-start(bf16[120,768]{1,0:T(8,128)(2,1)S(1)} %copy-done.36), channel_id=1, source_target_pairs={{0,24},{4,28},{8,16},{12,20},{16,8},{20,12},{24,0},{28,4},{1,25},{... | collective-permute-start | bytes 552968 | tf_op jit(solution)/shard_map/ppermute | solution.py:45
  382.1 14.1 %all-to-all-start.8 = ((f32[32,1,384]{2,1,0:T(1,128)}), f32[32,1,384]{2,1,0:T(1,128)S(1)}, u32[]{:S(2)}, u32[]{:S(2)}) async-start(f32[32,1,384]{2,1,0:T(1,128)} %copy.74), calls=%async_computation.8 | async-start | bytes 98304 | tf_op jit(solution)/shard_map/all_to_all | solution.py:1098
  389.2 14.8 %collective-permute-start.58 = (bf16[48,1152]{1,0:T(8,128)(2,1)}, bf16[48,1152]{1,0:T(8,128)(2,1)S(1)}, u32[]{:S(2)}, u32[]{:S(2)}) collective-permute-start(bf16[48,1152]{1,0:T(8,128)(2,1)} %get-tuple-element.340), channel_id=1, source_target_pairs={{0,8},{4,12},{8,0},{12,4},{16,24},{20,28},{24,16},{28,20},{1,9},{5... | collective-permute-start | bytes 331784 | tf_op jit(solution)/shard_map/ppermute | solution.py:45
  391.0 13.0 %collective-permute-start.59 = (bf16[48,1152]{1,0:T(8,128)(2,1)}, bf16[48,1152]{1,0:T(8,128)(2,1)S(1)}, u32[]{:S(2)}, u32[]{:S(2)}) collective-permute-start(bf16[48,1152]{1,0:T(8,128)(2,1)} %get-tuple-element.341), channel_id=1, source_target_pairs={{0,16},{4,20},{8,24},{12,28},{16,0},{20,4},{24,8},{28,12},{1,17},{... | collective-permute-start | bytes 331784 | tf_op jit(solution)/shard_map/ppermute | solution.py:45
  393.4 10.6 %collective-permute-start.60 = (bf16[48,1152]{1,0:T(8,128)(2,1)}, bf16[48,1152]{1,0:T(8,128)(2,1)S(1)}, u32[]{:S(2)}, u32[]{:S(2)}) collective-permute-start(bf16[48,1152]{1,0:T(8,128)(2,1)} %get-tuple-element.342), channel_id=1, source_target_pairs={{0,24},{4,28},{8,16},{12,20},{16,8},{20,12},{24,0},{28,4},{1,25},{... | collective-permute-start | bytes 331784 | tf_op jit(solution)/shard_map/ppermute | solution.py:45
  396.2 24.7 %all-to-all-start.7 = ((bf16[4,128,768]{2,1,0:T(8,128)(2,1)}), bf16[4,128,768]{2,1,0:T(8,128)(2,1)S(1)}, u32[]{:S(2)}, u32[]{:S(2)}) async-start(bf16[4,128,768]{2,1,0:T(8,128)(2,1)} %broadcast_select_fusion), calls=%async_computation.7 | async-start | bytes 1572864 | tf_op jit(solution)/shard_map/all_to_all | solution.py:60
  (63 other events, 693.3 us)
